TPU v7x, 256 devices: a whole 4x4x8 slice. The times are simulated.
256 devices in a mesh: visit: 8 (over x, core), patch: 32 (over y, z).
Axes of the slice: x: 4, y: 4, z: 8, core: 2. Of those that a mesh axis runs over, the one named last changes fastest.
Arguments:
- exposure: float32 [8, 512, 32768], P('visit', None, 'patch'), may hold values from -6 to 6
- variance: float32 [8, 512, 32768], P('visit', None, 'patch'), may hold values from 0.5 to 4
- col_start: int32 [8, 32768], P('visit', 'patch'), may hold values from 0 to 1018, as said below
- col_weights: float32 [8, 6, 32768], P('visit', None, 'patch')
- row_start: int32 [8, 16384], P('visit', 'patch'), may hold values from 0 to 506, as said below
- row_weights: float32 [8, 6, 16384], P('visit', None, 'patch')
- offsets: int32 [8, 32], P('visit', 'patch'), may hold values from 0 to 256
- basis_coef: float32 [8, 31], P('visit'), may hold values from -4 to 4
Outputs:
- difference: float32 [8, 512, 32768], P('visit', None, 'patch')
- coadd_image: float32 [512, 32768], P(None, 'patch')
Inputs may be any that keep to these rules, and one draw needn't show every extreme that they name: The 6 source columns from col_start lie inside the same CCD. The 6 source rows from row_start lie inside the CCD.
All inputs are finite; a program needn't handle non-finite values.
Results may differ from a plain program's by a relative error of at most 0.02.
Values may be sent and summed in bfloat16 or wider, within the bound.
No kernel may reach another device: no remote copies, remote signals or barrier semaphores. Data moves between devices by JAX's collectives and lax.ppermute only.
A program may use at most 128 MiB of HBM per device.

v0:
```python
import functools
import math

import jax
import jax.numpy as jnp
import numpy as np
from jax import lax
from jax.experimental import pallas as pl
from jax.experimental.pallas import tpu as pltpu
from jax.sharding import PartitionSpec as P

RADIUS = 10
TAPS = 6
ROWS = 512
COLS = 1024
EDGE = 256
LANES = 128
FILTERS = 12
WINDOW = 160
PAD = 16
SPREADS = (0.7, 1.5, 3.0)
DEGREES = (4, 3, 2)
F32 = jnp.float32
BF16 = jnp.bfloat16
VMEM_LIMIT = 56 * 1024 * 1024


def factor_table():
    distance = np.arange(2 * RADIUS + 1).astype(np.float32) - RADIUS
    rows = []
    for spread, degree in zip(SPREADS, DEGREES):
        gaussian = np.exp(-distance * distance / np.float32(2.0 * spread * spread)) / np.float32(
            spread * math.sqrt(2.0 * math.pi)
        )
        for exponent in range(degree + 1):
            rows.append(gaussian * (distance / np.float32(spread)) ** exponent)
    return np.stack(rows).astype(np.float32)


def kernel_terms():
    terms = [[] for _ in range(FILTERS)]
    kernel = 0
    first = 0
    for degree in DEGREES:
        for i in range(degree + 1):
            for j in range(degree + 1 - i):
                terms[first + j].append((kernel, first + i))
                kernel += 1
        first += degree + 1
    return terms


def row_band():
    factors = factor_table().astype(BF16)
    gap = np.arange(LANES)[:, None] + PAD - np.arange(WINDOW)[None, :]
    inside = np.abs(gap) <= RADIUS
    at = np.clip(gap + RADIUS, 0, 2 * RADIUS)
    band = np.where(inside[None], factors[:, at], np.zeros((), BF16))
    return band.transpose(1, 0, 2).reshape(LANES, FILTERS * WINDOW).astype(BF16)


def dot(a, b):
    return jnp.dot(a, b, preferred_element_type=F32)


def build_cols(table, low, width, cols_ref, square_ref):
    first = table[0:1, low : low + width]

    @pl.loop(0, COLS // LANES)
    def _(block):
        at = pl.multiple_of(block * LANES, LANES)
        source = lax.broadcasted_iota(jnp.int32, (LANES, width), 0).astype(F32)
        gap = source - (first - (block * LANES).astype(F32))
        value = jnp.zeros((LANES, width), F32)
        for tap in range(TAPS):
            value = jnp.where(gap == float(tap), table[tap + 1 : tap + 2, low : low + width], value)
        cols_ref[pl.ds(at, LANES), :] = value.astype(BF16)
        square_ref[pl.ds(at, LANES), :] = (value * value).astype(BF16)


def build_rows(row_start_ref, row_weights_ref, flip_ref, rows_ref, square_ref):
    flip_ref[...] = jnp.zeros_like(flip_ref)
    flip_ref[0:1, :] = row_start_ref[...].astype(F32)
    flip_ref[1 : TAPS + 1, :] = row_weights_ref[...]
    for block in range(ROWS // LANES):
        at = slice(block * LANES, (block + 1) * LANES)
        turned = jnp.transpose(flip_ref[:, at])
        gap = lax.broadcasted_iota(jnp.int32, (LANES, ROWS), 1).astype(F32) - turned[:, 0:1]
        value = jnp.zeros((LANES, ROWS), F32)
        for tap in range(TAPS):
            value = jnp.where(gap == float(tap), turned[:, tap + 1 : tap + 2], value)
        rows_ref[at, :] = value.astype(BF16)
        square_ref[at, :] = (value * value).astype(BF16)


def rolled_table(col_start_ref, col_weights_ref, table_ref, shift):
    table_ref[...] = jnp.zeros_like(table_ref)
    table_ref[0:1, :] = col_start_ref[...].astype(F32)
    table_ref[1 : TAPS + 1, :] = col_weights_ref[...]
    return pltpu.roll(table_ref[...], shift, 1)


def edge_kernel(
    offset_ref, pixels_ref, noise_ref, col_start_ref, col_weights_ref, row_start_ref, row_weights_ref,
    send_ref, head_ref, own_ref, sent_ref, last_weight_ref, last_patch_ref, rows_ref, rows2_ref,
    table_ref, flip_ref, cols_ref, cols2_ref,
):
    shift = offset_ref[0, 0]
    table = rolled_table(col_start_ref, col_weights_ref, table_ref, shift)
    build_rows(row_start_ref, row_weights_ref, flip_ref, rows_ref, rows2_ref)
    parts = jnp.concatenate([table[:, :EDGE], table[:, COLS - LANES :]], axis=1)
    build_cols(parts, 0, EDGE + LANES, cols_ref, cols2_ref)
    across = dot(pixels_ref[...].astype(BF16), cols_ref[...]).astype(BF16)
    across2 = dot(noise_ref[...].astype(BF16), cols2_ref[...]).astype(BF16)
    warped = dot(rows_ref[...], across)
    inverse = 1.0 / dot(rows2_ref[...], across2)
    scaled = warped * inverse
    mine = lax.broadcasted_iota(jnp.int32, (ROWS, EDGE), 1) >= shift
    edge_scaled = scaled[:, :EDGE]
    edge_inverse = inverse[:, :EDGE]
    own_scaled = jnp.where(mine, edge_scaled, 0.0)
    own_weight = jnp.where(mine, edge_inverse, 0.0)
    sent_scaled = jnp.where(mine, 0.0, edge_scaled)
    sent_weight = jnp.where(mine, 0.0, edge_inverse)
    own_ref[0:ROWS, :] = own_scaled
    own_ref[ROWS : 2 * ROWS, :] = own_weight
    send_ref[0:ROWS, :] = sent_scaled.astype(BF16)
    send_ref[ROWS : 2 * ROWS, :] = sent_weight.astype(BF16)
    head_ref[0:16, :] = jnp.transpose(own_scaled[:, :LANES])[0:16].astype(BF16)
    head_ref[16:32, :] = jnp.transpose(own_weight[:, :LANES])[0:16].astype(BF16)
    sent_ref[0:16, :] = jnp.transpose(sent_scaled[:, :LANES])[0:16]
    sent_ref[16:32, :] = jnp.transpose(sent_weight[:, :LANES])[0:16]
    last_inverse = inverse[:, EDGE:]
    last = scaled[:, EDGE:] / jnp.maximum(last_inverse, 0.1)
    last_weight_ref[...] = last_inverse.astype(BF16)
    last_patch_ref[...] = last.astype(BF16)
    tail = jnp.transpose(last)[LANES - 16 :].astype(BF16)
    send_ref[2 * ROWS : 2 * ROWS + 16, :] = tail[:, :256]
    send_ref[2 * ROWS + 16 :, :] = tail[:, 256:]


def middle_kernel(
    offset_ref, coef_ref, pixels_ref, noise_ref, col_start_ref, col_weights_ref, rows_ref, rows2_ref,
    last_patch_ref, last_weight_ref, factors_ref,
    patch_ref, weight_ref, taps_ref,
    table_ref, cols_ref, cols2_ref,
):
    shift = offset_ref[0, 0]
    width = COLS - EDGE - LANES
    table = rolled_table(col_start_ref, col_weights_ref, table_ref, shift)
    build_cols(table, EDGE, width, cols_ref, cols2_ref)
    across = dot(pixels_ref[...].astype(BF16), cols_ref[...]).astype(BF16)
    across2 = dot(noise_ref[...].astype(BF16), cols2_ref[...]).astype(BF16)
    warped = dot(rows_ref[...], across)
    inverse = 1.0 / dot(rows2_ref[...], across2)
    patch = (warped * inverse) / jnp.maximum(inverse, 0.1)
    weight_ref[:, :width] = inverse.astype(BF16)
    weight_ref[:, width:] = last_weight_ref[...]
    wide = jnp.concatenate([patch, last_patch_ref[...].astype(F32), jnp.zeros((ROWS, LANES), F32)], axis=1)
    patch_ref[...] = pltpu.roll(wide, RADIUS, 1).astype(BF16)
    below = lax.broadcasted_iota(jnp.int32, (LANES, LANES), 1) <= lax.broadcasted_iota(jnp.int32, (LANES, LANES), 0)
    for b, terms in enumerate(kernel_terms()):
        line = sum(coef_ref[0, k] * factors_ref[a : a + 1, :] for k, a in terms)
        line = line.astype(BF16).astype(F32)
        spread = pltpu.roll(jnp.broadcast_to(line, (LANES, LANES)), 0, 1, stride=1, stride_axis=0)
        lanes = slice(b * LANES, (b + 1) * LANES)
        taps_ref[:LANES, lanes] = jnp.where(below, spread, 0.0).astype(BF16)
        taps_ref[LANES:, lanes] = jnp.where(below, 0.0, spread).astype(BF16)


def convolve(window, taps_ref, band_ref, along_ref):
    for half in range(2):
        source = window(half)
        for piece in range(FILTERS // 2):
            lanes = slice(piece * 2 * LANES, (piece + 1) * 2 * LANES)
            along = dot(source, taps_ref[:, lanes]).astype(BF16)
            at = slice(half * LANES, (half + 1) * LANES)
            along_ref[2 * piece, PAD : PAD + ROWS, at] = along[:, :LANES]
            along_ref[2 * piece + 1, PAD : PAD + ROWS, at] = along[:, LANES:]
    for block in range(ROWS // LANES):
        source = jnp.concatenate(
            [along_ref[a, block * LANES : block * LANES + WINDOW, :] for a in range(FILTERS)], axis=0
        )
        yield block, dot(band_ref[...], source)


def clear_margins(along_ref):
    for a in range(FILTERS):
        along_ref[a, 0:PAD, :] = jnp.zeros((PAD, 2 * LANES), BF16)
        along_ref[a, PAD + ROWS :, :] = jnp.zeros((PAD, 2 * LANES), BF16)


def inner_kernel(patch_ref, weight_ref, taps_ref, band_ref, matched_ref, term_ref, along_ref):
    clear_margins(along_ref)

    @pl.loop(0, 2)
    def _(pair):
        start = pl.multiple_of(pair * 2 * LANES, 2 * LANES)

        def window(half):
            at = pl.multiple_of(start + LANES + half * LANES, LANES)
            return patch_ref[:, pl.ds(at, 2 * LANES)]

        for block, matched in convolve(window, taps_ref, band_ref, along_ref):
            rows = slice(block * LANES, (block + 1) * LANES)
            matched_ref[rows, pl.ds(start, 2 * LANES)] = matched
            weight = weight_ref[rows, pl.ds(pl.multiple_of(start + LANES, LANES), 2 * LANES)].astype(F32)
            term_ref[rows, pl.ds(start, 2 * LANES)] = (weight * matched).astype(BF16)


def outer_kernel(
    got_ref, ahead_ref, own_ref, sent_ref, patch_ref, weight_ref, taps_ref, band_ref, term_ref,
    matched_ref, terms_ref,
    along_ref, padded_ref, flip_ref, first_ref,
):
    clear_margins(along_ref)
    total_scaled = own_ref[0:ROWS, :] + got_ref[0:ROWS, :].astype(F32)
    total_weight = own_ref[ROWS : 2 * ROWS, :] + got_ref[ROWS : 2 * ROWS, :].astype(F32)
    patch = total_scaled / jnp.maximum(total_weight, 0.1)
    first_ref[...] = total_weight.astype(BF16)
    lane = lax.broadcasted_iota(jnp.int32, (ROWS, LANES), 1)
    flip_ref[...] = jnp.zeros_like(flip_ref)
    flip_ref[LANES - 16 :, :256] = got_ref[2 * ROWS : 2 * ROWS + 16, :].astype(F32)
    flip_ref[LANES - 16 :, 256:] = got_ref[2 * ROWS + 16 :, :].astype(F32)
    left = jnp.transpose(flip_ref[...])
    wide = pltpu.roll(jnp.concatenate([patch, left], axis=1), RADIUS, 1)
    padded_ref[:, :EDGE] = wide[:, :EDGE].astype(BF16)
    padded_ref[:, EDGE : EDGE + LANES] = jnp.where(
        lane < RADIUS, wide[:, EDGE:], patch_ref[:, :LANES].astype(F32)
    ).astype(BF16)
    padded_ref[:, EDGE + LANES : COLS] = patch_ref[:, LANES : COLS - EDGE]
    near_scaled = ahead_ref[0:16, :].astype(F32) + sent_ref[0:16, :]
    near_weight = ahead_ref[16:32, :].astype(F32) + sent_ref[16:32, :]
    flip_ref[0:16, :] = near_scaled / jnp.maximum(near_weight, 0.1)
    right = pltpu.roll(jnp.transpose(flip_ref[...]), RADIUS, 1)
    padded_ref[:, COLS:] = jnp.where(
        (lane >= RADIUS) & (lane < 2 * RADIUS), right,
        jnp.where(lane < RADIUS, patch_ref[:, COLS - EDGE :].astype(F32), 0.0),
    ).astype(BF16)

    for k in range(8):
        rows = slice(64 * k, 64 * k + 64)
        terms_ref[128 * k + 64 : 128 * k + 128, :EDGE] = first_ref[rows, :]
        terms_ref[128 * k + 64 : 128 * k + 128, EDGE:] = weight_ref[rows, :]
        terms_ref[128 * k : 128 * k + 64, 3 * LANES : 7 * LANES] = term_ref[rows, :]

    @pl.loop(0, 2)
    def _(pair):
        def place(half):
            return pl.multiple_of(jnp.where(pair == 0, half, 2 + 5 * half) * LANES, LANES)

        for block, matched in convolve(
            lambda half: padded_ref[:, pl.ds(place(half), 2 * LANES)], taps_ref, band_ref, along_ref
        ):
            rows = slice(block * LANES, (block + 1) * LANES)
            matched_ref[rows, pl.ds(pl.multiple_of(pair * 2 * LANES, LANES), 2 * LANES)] = matched
            for half in range(2):
                at = pl.ds(place(half), LANES)
                part = matched[:, half * LANES : (half + 1) * LANES]
                for k in (2 * block, 2 * block + 1):
                    low = 64 * (k - 2 * block)
                    weight = terms_ref[128 * k + 64 : 128 * k + 128, at].astype(F32)
                    terms_ref[128 * k : 128 * k + 64, at] = (weight * part[low : low + 64]).astype(BF16)


def final_kernel(inner_ref, outer_ref, coadd_ref, difference_ref, image_ref):
    image = coadd_ref[...].astype(F32)
    image_ref[...] = image
    difference_ref[:, : 3 * LANES] = outer_ref[:, : 3 * LANES] - image[:, : 3 * LANES]
    difference_ref[:, 3 * LANES : 7 * LANES] = inner_ref[...] - image[:, 3 * LANES : 7 * LANES]
    difference_ref[:, 7 * LANES :] = outer_ref[:, 3 * LANES :] - image[:, 7 * LANES :]


def call(body, outs, scratch, specs, flops, moved, name):
    return pl.pallas_call(
        body,
        out_shape=[jax.ShapeDtypeStruct(shape, dtype) for shape, dtype in outs],
        in_specs=specs,
        out_specs=[pl.BlockSpec(memory_space=pltpu.VMEM) for _ in outs],
        scratch_shapes=scratch,
        compiler_params=pltpu.CompilerParams(vmem_limit_bytes=VMEM_LIMIT),
        cost_estimate=pl.CostEstimate(flops=flops, bytes_accessed=moved, transcendentals=0),
        name=name,
    )


SMEM_SPEC = pl.BlockSpec(memory_space=pltpu.SMEM)
VMEM_SPEC = pl.BlockSpec(memory_space=pltpu.VMEM)


def shifted(x, axis, by):
    size = lax.axis_size(axis)
    return lax.ppermute(x, axis, [(i, (i + by) % size) for i in range(size)])


def per_device(
    exposure, variance, col_start, col_weights, row_start, row_weights, offsets, basis_coef
):
    pixels = exposure[0]
    noise = variance[0]
    col_taps = col_weights[0]
    row_taps = row_weights[0]
    factors = np.zeros((16, LANES), np.float32)
    factors[:FILTERS, : 2 * RADIUS + 1] = factor_table()
    factors = np.roll(factors, -2 * RADIUS, axis=1)
    band = jnp.asarray(row_band())
    width = EDGE + LANES
    send, head, own, sent, last_weight, last_patch, rows, rows2 = call(
        edge_kernel,
        [
            ((2 * ROWS + 32, EDGE), BF16),
            ((32, ROWS), BF16),
            ((2 * ROWS, EDGE), F32),
            ((32, ROWS), F32),
            ((ROWS, LANES), BF16),
            ((ROWS, LANES), BF16),
            ((ROWS, ROWS), BF16),
            ((ROWS, ROWS), BF16),
        ],
        [
            pltpu.VMEM((8, COLS), F32),
            pltpu.VMEM((LANES, ROWS), F32),
            pltpu.VMEM((COLS, width), BF16),
            pltpu.VMEM((COLS, width), BF16),
        ],
        [SMEM_SPEC] + [VMEM_SPEC] * 6,
        4 * ROWS * width * (COLS + ROWS),
        8 << 20,
        "edge_columns",
    )(offsets, pixels, noise, col_start, col_taps, row_start, row_taps)
    got = shifted(send, "patch", 1)
    ahead = shifted(head, "patch", -1)
    width = COLS - EDGE - LANES
    patch, weight, taps = call(
        middle_kernel,
        [
            ((ROWS, COLS - EDGE + LANES), BF16),
            ((ROWS, COLS - EDGE), BF16),
            ((2 * LANES, FILTERS * LANES), BF16),
        ],
        [
            pltpu.VMEM((8, COLS), F32),
            pltpu.VMEM((COLS, width), BF16),
            pltpu.VMEM((COLS, width), BF16),
        ],
        [SMEM_SPEC] * 2 + [VMEM_SPEC] * 9,
        4 * ROWS * width * (COLS + ROWS),
        8 << 20,
        "middle_columns",
    )(offsets, basis_coef, pixels, noise, col_start, col_taps, rows, rows2, last_patch, last_weight, jnp.asarray(factors))
    along = pltpu.VMEM((FILTERS, ROWS + 2 * PAD, 2 * LANES), BF16)
    conv_flops = 2 * ROWS * ROWS * FILTERS * (2 * LANES + WINDOW)
    inner, term = call(
        inner_kernel,
        [((ROWS, 4 * LANES), F32), ((ROWS, 4 * LANES), BF16)],
        [along],
        [VMEM_SPEC] * 4,
        conv_flops,
        8 << 20,
        "inner_match",
    )(patch, weight, taps, band)
    outer, terms = call(
        outer_kernel,
        [((ROWS, 4 * LANES), F32), ((2 * ROWS, COLS), BF16)],
        [
            along,
            pltpu.VMEM((ROWS, COLS + LANES), BF16),
            pltpu.VMEM((LANES, ROWS), F32),
            pltpu.VMEM((ROWS, EDGE), BF16),
        ],
        [VMEM_SPEC] * 9,
        conv_flops,
        8 << 20,
        "outer_match",
    )(got, ahead, own, sent, patch, weight, taps, band, term)
    summed = lax.psum_scatter(terms, "visit", scatter_dimension=0, tiled=True).astype(F32)
    piece = summed[:64] / jnp.maximum(summed[64:], 0.1)
    coadd = lax.all_gather(piece.astype(BF16), "visit", axis=0, tiled=True)
    difference, image = call(
        final_kernel,
        [((ROWS, COLS), F32), ((ROWS, COLS), F32)],
        [],
        [VMEM_SPEC] * 3,
        2 * ROWS * COLS,
        8 << 20,
        "difference",
    )(inner, outer, coadd)
    return (difference[None], image)


def solution(mesh):
    return jax.shard_map(
        per_device,
        mesh=mesh,
        in_specs=(
            P("visit", None, "patch"),
            P("visit", None, "patch"),
            P("visit", "patch"),
            P("visit", None, "patch"),
            P("visit", "patch"),
            P("visit", None, "patch"),
            P("visit", "patch"),
            P("visit", None),
        ),
        out_specs=(P("visit", None, "patch"), P(None, "patch")),
        check_vma=False,
    )
```

profile of v0, /device:TPU:1, one launch (start us, length us, event | category | flops | bytes accessed | tf_op | source)
XLA Modules:
  0.0 123.0 jit_solution(10078613567981547326)
XLA Ops:
  7.2 0.0 reduce-scatter.2.cloned.1.call-start
  7.9 1.4 %copy.16 = f32[1,6,1024]{2,1,0:T(8,128)} copy(f32[1,6,1024]{2,0,1:T(1,128)} %param.13) | data formatting | bytes 49152
  9.2 1.3 %copy.17 = f32[1,6,512]{2,1,0:T(8,128)} copy(f32[1,6,512]{2,0,1:T(1,128)} %param.15) | data formatting | bytes 24576
  10.5 7.4 %edge_columns.1 = (bf16[1056,256]{1,0:T(8,128)(2,1)}, bf16[32,512]{1,0:T(8,128)(2,1)}, f32[1024,256]{1,0:T(8,128)}, f32[32,512]{1,0:T(8,128)}, bf16[512,128]{1,0...) custom-call(s32[1,1]{1,0:T(1,128)S(6)} %copy.18.offset_ref, ...), custom_call_target="tpu_custom_call" | custom-call | flops 1207959552 | bytes 8388608 | tf_op jit(solution)/shard_map/edge_columns/pallas_call | solution.py:308
  18.0 2.5 %collective-permute-start = (bf16[1056,256]{1,0:T(8,128)(2,1)}, bf16[1056,256]{1,0:T(8,128)(2,1)S(1)}, u32[]{:S(2)}, u32[]{:S(2)}) collective-permute-start(bf16[1056,256]{1,0:T(8,128)(2,1)} %get-tuple-element.27), channel_id=1, source_target_pairs={{0,1},{1,2},{2,3},{3,4},{4,5},{5,6},{6,7},{7,8},{8,9},{9,10},{10,1... | collective-permute-start | bytes 1622024 | tf_op jit(solution)/shard_map/ppermute | solution.py:293
  20.5 6.5 %collective-permute-start.1 = (bf16[32,512]{1,0:T(8,128)(2,1)}, bf16[32,512]{1,0:T(8,128)(2,1)S(1)}, u32[]{:S(2)}, u32[]{:S(2)}) collective-permute-start(bf16[32,512]{1,0:T(8,128)(2,1)} %get-tuple-element.28), channel_id=1, source_target_pairs={{0,31},{1,0},{2,1},{3,2},{4,3},{5,4},{6,5},{7,6},{8,7},{9,8},{10,9... | collective-permute-start | bytes 98312 | tf_op jit(solution)/shard_map/ppermute | solution.py:293
  27.0 8.3 %middle_columns.1 = (bf16[512,896]{1,0:T(8,128)(2,1)}, bf16[512,768]{1,0:T(8,128)(2,1)}, bf16[256,1536]{1,0:T(8,128)(2,1)}) custom-call(s32[1,1]{1,0:T(1,128)S(6)} %copy.18.offset_ref, f32[1,31]{1,0:T(1,128)} %coef_ref.1, f32[512,1024]{1,0:T(8,128)} %bitcast.13, f32[512,1024]{1,0:T(8,128)} %bitcast.15, s32[1,1024]{1,0:T(1,128)} %col_start_ref.3, ...), custom_call_target="tpu_custom_call" | custom-call | flops 2013265920 | bytes 8388608 | tf_op jit(solution)/shard_map/middle_columns/pallas_call | solution.py:334
  35.3 6.0 %inner_match.1 = (f32[512,512]{1,0:T(8,128)}, bf16[512,512]{1,0:T(8,128)(2,1)}) custom-call(bf16[512,896]{1,0:T(8,128)(2,1)} %get-tuple-element.23.patch_ref, bf16[512,768]{1,0:T(8,128)(2,1)} %get-tuple-element.24.weight_ref, bf16[256,1536]{1,0:T(8,128)(2,1)} %get-tuple-element.25.taps_ref, bf16[128,1920]{1,0:T(8,128)(2,1)} %constant.6.clone.band_ref), custom_call_target="tpu_custom_call" | custom-call | flops 2617245696 | bytes 8388608 | tf_op jit(solution)/shard_map/inner_match/pallas_call | solution.py:353
  41.3 0.0 collective-permute-done.1.ahead_ref
  41.3 0.0 copy-start.1
  41.3 0.0 collective-permute-done.got_ref
  41.3 0.0 copy-start
  41.3 0.6 copy-done.1
  41.9 0.2 copy-done
  42.2 7.9 %outer_match.1 = (f32[512,512]{1,0:T(8,128)}, bf16[1024,1024]{1,0:T(8,128)(2,1)}) custom-call(bf16[1056,256]{1,0:T(8,128)(2,1)} %copy-done, bf16[32,512]{1,0:T(8,128)(2,1)} %copy-done.1, f32[1024,256]{1,0:T(8,128)} %get-tuple-element.29.own_ref, f32[32,512]{1,0:T(8,128)} %get-tuple-element.30.sent_ref, bf16[512,896]{1,0:T(8,128)(2,1)} %get-tuple-element.23.patch_ref, ...), custom_call_target="tpu_custom_call" | custom-call | flops 2617245696 | bytes 8388608 | tf_op jit(solution)/shard_map/outer_match/pallas_call | solution.py:362
  50.1 0.0 reduce-scatter.2.cloned.1.call-update
  50.1 0.0 all-gather.2.cloned.1.call-start
  50.1 31.7 %reduce-scatter.2.cloned.1.call-done = bf16[128,1024]{1,0:T(8,128)(2,1)} async-done(((bf16[1024,1024]{1,0:T(8,128)(2,1)}), bf16[128,1024]{1,0:T(8,128)(2,1)}) %reduce-scatter.2.cloned.1.call-update) | async-done | bytes 262160 | tf_op jit(solution)/shard_map/reduce_scatter | solution.py:376
  81.9 1.0 convert_element_type.6
  82.9 0.7 fusion.1
  83.6 0.0 all-gather.2.cloned.1.call-update
  83.6 28.5 %all-gather.2.cloned.1.call-done.coadd_ref = bf16[512,1024]{1,0:T(8,128)(2,1)} async-done(((bf16[64,1024]{1,0:T(8,128)(2,1)}), bf16[512,1024]{1,0:T(8,128)(2,1)}) %all-gather.2.cloned.1.call-update) | async-done | bytes 1048592 | tf_op jit(solution)/shard_map/all_gather | solution.py:378
  112.1 4.1 %difference.1 = (f32[512,1024]{1,0:T(8,128)}, f32[512,1024]{1,0:T(8,128)}) custom-call(f32[512,512]{1,0:T(8,128)} %get-tuple-element.26.inner_ref, f32[512,512]{1,0:T(8,128)} %get-tuple-element.32.outer_ref, bf16[512,1024]{1,0:T(8,128)(2,1)} %all-gather.2.cloned.1.call-done.coadd_ref), custom_call_target="tpu_custom_call" | custom-call | flops 1048576 | bytes 8388608 | tf_op jit(solution)/shard_map/difference/pallas_call | solution.py:379
Async XLA Ops:
  7.2 74.7 %reduce-scatter.2.cloned.1.call-start = ((), (), s32[]{:S(2)}) async-start(), calls=%async_computation.1 | async-start | bytes 2359296 | tf_op jit(solution)/shard_map/reduce_scatter | solution.py:376
  18.0 23.4 %collective-permute-start = (bf16[1056,256]{1,0:T(8,128)(2,1)}, bf16[1056,256]{1,0:T(8,128)(2,1)S(1)}, u32[]{:S(2)}, u32[]{:S(2)}) collective-permute-start(bf16[1056,256]{1,0:T(8,128)(2,1)} %get-tuple-element.27), channel_id=1, source_target_pairs={{0,1},{1,2},{2,3},{3,4},{4,5},{5,6},{6,7},{7,8},{8,9},{9,10},{10,1... | collective-permute-start | bytes 1622024 | tf_op jit(solution)/shard_map/ppermute | solution.py:293
  20.5 20.8 %collective-permute-start.1 = (bf16[32,512]{1,0:T(8,128)(2,1)}, bf16[32,512]{1,0:T(8,128)(2,1)S(1)}, u32[]{:S(2)}, u32[]{:S(2)}) collective-permute-start(bf16[32,512]{1,0:T(8,128)(2,1)} %get-tuple-element.28), channel_id=1, source_target_pairs={{0,31},{1,0},{2,1},{3,2},{4,3},{5,4},{6,5},{7,6},{8,7},{9,8},{10,9... | collective-permute-start | bytes 98312 | tf_op jit(solution)/shard_map/ppermute | solution.py:293
  41.3 0.6 copy-start.1
  41.3 0.8 copy-start
  50.1 62.0 %all-gather.2.cloned.1.call-start = ((), (), s32[]{:S(2)}) async-start(), calls=%async_computation.2 | async-start | bytes 1179648 | tf_op jit(solution)/shard_map/all_gather | solution.py:378
Sparse Core Ops, SparseCore 0:
  50.2 31.6 reduce-scatter.1
  84.3 27.7 all-gather.1
where the time goes:
time: 123 us
  waiting for transfers between devices  60.3 us (49%)
  Pallas kernels  33.7 us (27%)
  between operations  14.7 us (12%)
  starting transfers between devices  9.1 us (7%)
  local copies, waits for them, and re-layouts  3.48 us (3%)
  other arithmetic  1.69 us (1%)
    reduce_scatter x1, waiting for transfers between devices, per_device(): lax.psum_scatter(terms, 'visit', scatter_dimension=0, tiled=True)  31.7 us
    all_gather x1, waiting for transfers between devices, per_device(): coadd = lax.all_gather(piece.astype(BF16), 'visit', axis=0, tiled=True)  28.5 us
    ppermute x2, starting transfers between devices, shifted(): return lax.ppermute(x, axis, [(i, (i + by) % size) for i in range(size)])  9.02 us
    pallas_call x1, Pallas kernels, per_device(): call(middle_kernel, [((ROWS, COLS - EDGE + LANES), BF16), ((ROWS, COLS -...  8.31 us
    pallas_call x1, Pallas kernels, per_device(): call(outer_kernel, [((ROWS, 4 * LANES), F32), ((2 * ROWS, COLS), BF16)],...  7.91 us
    pallas_call x1, Pallas kernels, per_device(): call(edge_kernel, [((2 * ROWS + 32, EDGE), BF16), ((32, ROWS), BF16), ((2...  7.43 us
    pallas_call x1, Pallas kernels, per_device(): call(inner_kernel, [((ROWS, 4 * LANES), F32), ((ROWS, 4 * LANES), BF16)],...  6.03 us
    pallas_call x1, Pallas kernels, per_device(): call(final_kernel, [((ROWS, COLS), F32), ((ROWS, COLS), F32)], [], [VMEM_...  4.06 us
  transfers between devices with their start and end apart: 4, of which 2 were waited for; matrix products, arithmetic and copies ran while one was open for 0% of the time, Pallas kernels for 12%

commit v1 on v0

--- a/solution.py
+++ b/solution.py
@@ -22,7 +22,7 @@
 DEGREES = (4, 3, 2)
 F32 = jnp.float32
 BF16 = jnp.bfloat16
-VMEM_LIMIT = 56 * 1024 * 1024
+VMEM_LIMIT = 28 * 1024 * 1024
 
 
 def factor_table():
@@ -81,7 +81,8 @@
 def build_rows(row_start_ref, row_weights_ref, flip_ref, rows_ref, square_ref):
     flip_ref[...] = jnp.zeros_like(flip_ref)
     flip_ref[0:1, :] = row_start_ref[...].astype(F32)
-    flip_ref[1 : TAPS + 1, :] = row_weights_ref[...]
+    for tap in range(TAPS):
+        flip_ref[tap + 1 : tap + 2, :] = row_weights_ref[tap]
     for block in range(ROWS // LANES):
         at = slice(block * LANES, (block + 1) * LANES)
         turned = jnp.transpose(flip_ref[:, at])
@@ -96,22 +97,29 @@
 def rolled_table(col_start_ref, col_weights_ref, table_ref, shift):
     table_ref[...] = jnp.zeros_like(table_ref)
     table_ref[0:1, :] = col_start_ref[...].astype(F32)
-    table_ref[1 : TAPS + 1, :] = col_weights_ref[...]
+    for tap in range(TAPS):
+        table_ref[tap + 1 : tap + 2, :] = col_weights_ref[tap]
     return pltpu.roll(table_ref[...], shift, 1)
 
 
 def edge_kernel(
     offset_ref, pixels_ref, noise_ref, col_start_ref, col_weights_ref, row_start_ref, row_weights_ref,
     send_ref, head_ref, own_ref, sent_ref, last_weight_ref, last_patch_ref, rows_ref, rows2_ref,
-    table_ref, flip_ref, cols_ref, cols2_ref,
+    table_ref, flip_ref, cols_ref, cols2_ref, held_ref, held2_ref, sems,
 ):
+    load = pltpu.make_async_copy(pixels_ref, held_ref, sems.at[0])
+    load2 = pltpu.make_async_copy(noise_ref, held2_ref, sems.at[1])
+    load.start()
+    load2.start()
     shift = offset_ref[0, 0]
     table = rolled_table(col_start_ref, col_weights_ref, table_ref, shift)
     build_rows(row_start_ref, row_weights_ref, flip_ref, rows_ref, rows2_ref)
     parts = jnp.concatenate([table[:, :EDGE], table[:, COLS - LANES :]], axis=1)
     build_cols(parts, 0, EDGE + LANES, cols_ref, cols2_ref)
-    across = dot(pixels_ref[...].astype(BF16), cols_ref[...]).astype(BF16)
-    across2 = dot(noise_ref[...].astype(BF16), cols2_ref[...]).astype(BF16)
+    load.wait()
+    across = dot(held_ref[...].astype(BF16), cols_ref[...]).astype(BF16)
+    load2.wait()
+    across2 = dot(held2_ref[...].astype(BF16), cols2_ref[...]).astype(BF16)
     warped = dot(rows_ref[...], across)
     inverse = 1.0 / dot(rows2_ref[...], across2)
     scaled = warped * inverse
@@ -168,6 +176,11 @@
         taps_ref[LANES:, lanes] = jnp.where(below, 0.0, spread).astype(BF16)
 
 
+def row_block(step):
+    core = lax.axis_index("visit") % 2
+    return pl.multiple_of(((step + 2 * core) % 4) * LANES, LANES)
+
+
 def convolve(window, taps_ref, band_ref, along_ref):
     for half in range(2):
         source = window(half)
@@ -177,11 +190,10 @@
             at = slice(half * LANES, (half + 1) * LANES)
             along_ref[2 * piece, PAD : PAD + ROWS, at] = along[:, :LANES]
             along_ref[2 * piece + 1, PAD : PAD + ROWS, at] = along[:, LANES:]
-    for block in range(ROWS // LANES):
-        source = jnp.concatenate(
-            [along_ref[a, block * LANES : block * LANES + WINDOW, :] for a in range(FILTERS)], axis=0
-        )
-        yield block, dot(band_ref[...], source)
+    for step in range(ROWS // LANES):
+        at = row_block(step)
+        source = jnp.concatenate([along_ref[a, pl.ds(at, WINDOW), :] for a in range(FILTERS)], axis=0)
+        yield step, at, dot(band_ref[...], source)
 
 
 def clear_margins(along_ref):
@@ -201,16 +213,16 @@
             at = pl.multiple_of(start + LANES + half * LANES, LANES)
             return patch_ref[:, pl.ds(at, 2 * LANES)]
 
-        for block, matched in convolve(window, taps_ref, band_ref, along_ref):
-            rows = slice(block * LANES, (block + 1) * LANES)
+        for step, at, matched in convolve(window, taps_ref, band_ref, along_ref):
+            rows = pl.ds(at, LANES)
             matched_ref[rows, pl.ds(start, 2 * LANES)] = matched
             weight = weight_ref[rows, pl.ds(pl.multiple_of(start + LANES, LANES), 2 * LANES)].astype(F32)
-            term_ref[rows, pl.ds(start, 2 * LANES)] = (weight * matched).astype(BF16)
+            term_ref[step * LANES : (step + 1) * LANES, pl.ds(start, 2 * LANES)] = (weight * matched).astype(BF16)
 
 
 def outer_kernel(
     got_ref, ahead_ref, own_ref, sent_ref, patch_ref, weight_ref, taps_ref, band_ref, term_ref,
-    matched_ref, terms_ref,
+    matched_ref, keep_ref, give_ref,
     along_ref, padded_ref, flip_ref, first_ref,
 ):
     clear_margins(along_ref)
@@ -238,45 +250,82 @@
         jnp.where(lane < RADIUS, patch_ref[:, COLS - EDGE :].astype(F32), 0.0),
     ).astype(BF16)
 
-    for k in range(8):
-        rows = slice(64 * k, 64 * k + 64)
-        terms_ref[128 * k + 64 : 128 * k + 128, :EDGE] = first_ref[rows, :]
-        terms_ref[128 * k + 64 : 128 * k + 128, EDGE:] = weight_ref[rows, :]
-        terms_ref[128 * k : 128 * k + 64, 3 * LANES : 7 * LANES] = term_ref[rows, :]
+    halves = (keep_ref, keep_ref, give_ref, give_ref)
+    for step in range(4):
+        for part in range(2):
+            low = LANES * (2 * (step % 2) + part)
+            rows = pl.ds(pl.multiple_of(row_block(step) + 64 * part, 64), 64)
+            halves[step][low + 64 : low + 128, :EDGE] = first_ref[rows, :]
+            halves[step][low + 64 : low + 128, EDGE:] = weight_ref[rows, :]
+            from_inner = term_ref[step * LANES + 64 * part : step * LANES + 64 * part + 64, :]
+            halves[step][low : low + 64, 3 * LANES : 7 * LANES] = from_inner
 
     @pl.loop(0, 2)
     def _(pair):
         def place(half):
             return pl.multiple_of(jnp.where(pair == 0, half, 2 + 5 * half) * LANES, LANES)
 
-        for block, matched in convolve(
+        for step, start, matched in convolve(
             lambda half: padded_ref[:, pl.ds(place(half), 2 * LANES)], taps_ref, band_ref, along_ref
         ):
-            rows = slice(block * LANES, (block + 1) * LANES)
-            matched_ref[rows, pl.ds(pl.multiple_of(pair * 2 * LANES, LANES), 2 * LANES)] = matched
+            matched_ref[pl.ds(start, LANES), pl.ds(pl.multiple_of(pair * 2 * LANES, LANES), 2 * LANES)] = matched
             for half in range(2):
                 at = pl.ds(place(half), LANES)
-                part = matched[:, half * LANES : (half + 1) * LANES]
-                for k in (2 * block, 2 * block + 1):
-                    low = 64 * (k - 2 * block)
-                    weight = terms_ref[128 * k + 64 : 128 * k + 128, at].astype(F32)
-                    terms_ref[128 * k : 128 * k + 64, at] = (weight * part[low : low + 64]).astype(BF16)
-
-
-def final_kernel(inner_ref, outer_ref, coadd_ref, difference_ref, image_ref):
-    image = coadd_ref[...].astype(F32)
-    image_ref[...] = image
-    difference_ref[:, : 3 * LANES] = outer_ref[:, : 3 * LANES] - image[:, : 3 * LANES]
-    difference_ref[:, 3 * LANES : 7 * LANES] = inner_ref[...] - image[:, 3 * LANES : 7 * LANES]
-    difference_ref[:, 7 * LANES :] = outer_ref[:, 3 * LANES :] - image[:, 7 * LANES :]
-
-
-def call(body, outs, scratch, specs, flops, moved, name):
+                for part in range(2):
+                    low = LANES * (2 * (step % 2) + part)
+                    value = matched[64 * part : 64 * part + 64, half * LANES : (half + 1) * LANES]
+                    weight = halves[step][low + 64 : low + 128, at].astype(F32)
+                    halves[step][low : low + 64, at] = (weight * value).astype(BF16)
+
+
+def pair_kernel(keep_ref, got_ref, own_ref, one_ref, two_ref, three_ref):
+    chip = lax.axis_index("visit") // 2
+
+    def piece(ahead):
+        rows = pl.ds(pl.multiple_of(((chip + ahead) % 4) * LANES, LANES), LANES)
+        return keep_ref[rows, :].astype(F32) + got_ref[rows, :].astype(F32)
+
+    own_ref[...] = piece(0)
+    one_ref[...] = piece(1).astype(BF16)
+    two_ref[...] = piece(2).astype(BF16)
+    three_ref[...] = piece(3).astype(BF16)
+
+
+def coadd_kernel(own_ref, one_ref, two_ref, three_ref, coadd_ref):
+    total = own_ref[...] + one_ref[...].astype(F32) + two_ref[...].astype(F32) + three_ref[...].astype(F32)
+    coadd_ref[...] = (total[:64] / jnp.maximum(total[64:], 0.1)).astype(BF16)
+
+
+def final_kernel(*refs):
+    inner_ref, outer_ref = refs[:2]
+    pieces = refs[2:10]
+    difference_out, image_out, difference_ref, image_ref, sems = refs[10:]
+    index = lax.axis_index("visit")
+    chip, core = index // 2, index % 2
+    copies = []
+    for number, piece_ref in enumerate(pieces):
+        side, back = number // 4, number % 4
+        start = ((core + side) % 2) * (4 * 64) + ((chip + 4 - back) % 4) * 64
+        rows = pl.ds(pl.multiple_of(start, 64), 64)
+        image = piece_ref[...].astype(F32)
+        image_ref[number] = image
+        difference_ref[number, :, : 3 * LANES] = outer_ref[rows, : 3 * LANES] - image[:, : 3 * LANES]
+        difference_ref[number, :, 3 * LANES : 7 * LANES] = inner_ref[rows, :] - image[:, 3 * LANES : 7 * LANES]
+        difference_ref[number, :, 7 * LANES :] = outer_ref[rows, 3 * LANES :] - image[:, 7 * LANES :]
+        for which, (held, out) in enumerate(((image_ref, image_out), (difference_ref, difference_out))):
+            copy = pltpu.make_async_copy(held.at[number], out.at[rows, :], sems.at[which, number])
+            copy.start()
+            copies.append(copy)
+    for copy in copies:
+        copy.wait()
+
+
+def call(body, outs, scratch, specs, flops, moved, name, out_spec=None):
     return pl.pallas_call(
         body,
         out_shape=[jax.ShapeDtypeStruct(shape, dtype) for shape, dtype in outs],
         in_specs=specs,
-        out_specs=[pl.BlockSpec(memory_space=pltpu.VMEM) for _ in outs],
+        out_specs=[out_spec or VMEM_SPEC for _ in outs],
         scratch_shapes=scratch,
         compiler_params=pltpu.CompilerParams(vmem_limit_bytes=VMEM_LIMIT),
         cost_estimate=pl.CostEstimate(flops=flops, bytes_accessed=moved, transcendentals=0),
@@ -286,6 +335,7 @@
 
 SMEM_SPEC = pl.BlockSpec(memory_space=pltpu.SMEM)
 VMEM_SPEC = pl.BlockSpec(memory_space=pltpu.VMEM)
+ANY_SPEC = pl.BlockSpec(memory_space=pltpu.HBM)
 
 
 def shifted(x, axis, by):
@@ -293,13 +343,23 @@
     return lax.ppermute(x, axis, [(i, (i + by) % size) for i in range(size)])
 
 
+def in_hbm(x):
+    return pltpu.with_memory_space_constraint(x, pltpu.HBM)
+
+
+def partner(x):
+    return lax.ppermute(x, "visit", [(i, i ^ 1) for i in range(lax.axis_size("visit"))])
+
+
 def per_device(
     exposure, variance, col_start, col_weights, row_start, row_weights, offsets, basis_coef
 ):
-    pixels = exposure[0]
-    noise = variance[0]
-    col_taps = col_weights[0]
-    row_taps = row_weights[0]
+    pixels = in_hbm(exposure[0])
+    noise = in_hbm(variance[0])
+    col_taps = in_hbm(jnp.transpose(col_weights, (1, 0, 2)))
+    row_taps = in_hbm(jnp.transpose(row_weights, (1, 0, 2)))
+    col_start = in_hbm(col_start)
+    row_start = in_hbm(row_start)
     factors = np.zeros((16, LANES), np.float32)
     factors[:FILTERS, : 2 * RADIUS + 1] = factor_table()
     factors = np.roll(factors, -2 * RADIUS, axis=1)
@@ -322,8 +382,11 @@
             pltpu.VMEM((LANES, ROWS), F32),
             pltpu.VMEM((COLS, width), BF16),
             pltpu.VMEM((COLS, width), BF16),
-        ],
-        [SMEM_SPEC] + [VMEM_SPEC] * 6,
+            pltpu.VMEM((ROWS, COLS), F32),
+            pltpu.VMEM((ROWS, COLS), F32),
+            pltpu.SemaphoreType.DMA((2,)),
+        ],
+        [SMEM_SPEC] + [ANY_SPEC] * 2 + [VMEM_SPEC] * 4,
         4 * ROWS * width * (COLS + ROWS),
         8 << 20,
         "edge_columns",
@@ -359,9 +422,9 @@
         8 << 20,
         "inner_match",
     )(patch, weight, taps, band)
-    outer, terms = call(
+    outer, keep, give = call(
         outer_kernel,
-        [((ROWS, 4 * LANES), F32), ((2 * ROWS, COLS), BF16)],
+        [((ROWS, 4 * LANES), F32), ((ROWS, COLS), BF16), ((ROWS, COLS), BF16)],
         [
             along,
             pltpu.VMEM((ROWS, COLS + LANES), BF16),
@@ -373,18 +436,41 @@
         8 << 20,
         "outer_match",
     )(got, ahead, own, sent, patch, weight, taps, band, term)
-    summed = lax.psum_scatter(terms, "visit", scatter_dimension=0, tiled=True).astype(F32)
-    piece = summed[:64] / jnp.maximum(summed[64:], 0.1)
-    coadd = lax.all_gather(piece.astype(BF16), "visit", axis=0, tiled=True)
+    own_piece, *others = call(
+        pair_kernel,
+        [((LANES, COLS), F32)] + [((LANES, COLS), BF16)] * 3,
+        [],
+        [VMEM_SPEC] * 2,
+        ROWS * COLS,
+        3 << 20,
+        "pair_sum",
+    )(keep, partner(give))
+    others = [shifted(x, "visit", 2 * ahead) for ahead, x in enumerate(others, 1)]
+    (piece,) = call(
+        coadd_kernel,
+        [((64, COLS), BF16)],
+        [],
+        [VMEM_SPEC] * 4,
+        4 * LANES * COLS,
+        2 << 20,
+        "coadd",
+    )(own_piece, *others)
+    column = [piece] + [shifted(piece, "visit", 2 * ahead) for ahead in range(1, 4)]
+    pieces = column + [partner(x) for x in column]
     difference, image = call(
         final_kernel,
         [((ROWS, COLS), F32), ((ROWS, COLS), F32)],
-        [],
-        [VMEM_SPEC] * 3,
+        [
+            pltpu.VMEM((8, 64, COLS), F32),
+            pltpu.VMEM((8, 64, COLS), F32),
+            pltpu.SemaphoreType.DMA((2, 8)),
+        ],
+        [VMEM_SPEC] * 10,
         2 * ROWS * COLS,
         8 << 20,
         "difference",
-    )(inner, outer, coadd)
+        ANY_SPEC,
+    )(inner, outer, *pieces)
     return (difference[None], image)
 
 

time: 123 us -> 65.8 us (0.53)
  waiting for transfers between devices: 60.3 us -> 18.4 us
  starting transfers between devices: 9.1 us -> 24 us
  between operations: 14.7 us -> 1.53 us
  Pallas kernels: 33.7 us -> 21.7 us
  local copies, waits for them, and re-layouts: 3.48 us -> 0.01 us
  other arithmetic: 1.69 us -> 0 us
    reduce_scatter x1 -> x0, waiting for transfers between devices: 31.7 us -> none  [per_device(): lax.psum_scatter(terms, 'visit', scatter_dimension=0, tiled=True)]
    all_gather x1 -> x0, waiting for transfers between devices: 28.5 us -> none  [per_device(): coadd = lax.all_gather(piece.astype(BF16), 'visit', axis=0, tiled=True)]
    ppermute x2 -> x8, waiting for transfers between devices: 0.01 us -> 14.8 us  [shifted(): return lax.ppermute(x, axis, [(i, (i + by) % size) for i in range(size)])]
    ppermute x2 -> x8, starting transfers between devices: 9.02 us -> 18.2 us  [shifted(): return lax.ppermute(x, axis, [(i, (i + by) % size) for i in range(size)])]
    ppermute x0 -> x5, starting transfers between devices: none -> 5.85 us  [partner(): lax.ppermute(x, 'visit', [(i, i ^ 1) for i in range(lax.axis_size('visit'...]
    pallas_call x2 -> x4, Pallas kernels: 12 us -> 6.71 us  [the longest x1 4.18 us: per_device(): call(outer_kernel, [((ROWS, 4 * LANES), F32), ((ROWS, COLS), BF16), ((ROW...]
    ppermute x0 -> x5, waiting for transfers between devices: none -> 3.62 us  [partner(): lax.ppermute(x, 'visit', [(i, i ^ 1) for i in range(lax.axis_size('visit'...]
    unnamed x6, local copies, waits for them, and re-layouts: 3.48 us -> 0.01 us
  transfers between devices with their start and end apart: 4 -> 13, of which waited for: 2 -> 7; matrix products, arithmetic and copies ran while one was open for 0% -> 0% of each run, Pallas kernels for 12% -> 15%
where the time goes in v1:
time: 65.8 us; the launch traced here: 65.6 us
  starting transfers between devices  24 us (36%)
  Pallas kernels  21.7 us (33%)
  waiting for transfers between devices  18.4 us (28%)
  between operations  1.53 us (2%)
    ppermute x8, starting transfers between devices, shifted(): return lax.ppermute(x, axis, [(i, (i + by) % size) for i in range(size)])  18.2 us
    ppermute x8, waiting for transfers between devices, shifted(): return lax.ppermute(x, axis, [(i, (i + by) % size) for i in range(size)])  14.8 us
    pallas_call x1, Pallas kernels, per_device(): call(middle_kernel, [((ROWS, COLS - EDGE + LANES), BF16), ((ROWS, COLS -...  6.65 us
    ppermute x5, starting transfers between devices, partner(): lax.ppermute(x, 'visit', [(i, i ^ 1) for i in range(lax.axis_size('visit'...  5.85 us
    pallas_call x1, Pallas kernels, per_device(): call(edge_kernel, [((2 * ROWS + 32, EDGE), BF16), ((32, ROWS), BF16), ((2...  4.85 us
    pallas_call x1, Pallas kernels, per_device(): call(outer_kernel, [((ROWS, 4 * LANES), F32), ((ROWS, COLS), BF16), ((ROW...  4.18 us
    ppermute x5, waiting for transfers between devices, partner(): lax.ppermute(x, 'visit', [(i, i ^ 1) for i in range(lax.axis_size('visit'...  3.62 us
    pallas_call x1, Pallas kernels, per_device(): call(inner_kernel, [((ROWS, 4 * LANES), F32), ((ROWS, 4 * LANES), BF16)],...  3.46 us
  transfers between devices with their start and end apart: 13, of which 7 were waited for; matrix products, arithmetic and copies ran while one was open for 0% of the time, Pallas kernels for 15%

profile of v1, /device:TPU:1, one launch (start us, length us, event | category | flops | bytes accessed | tf_op | source)
XLA Modules:
  0.0 65.6 jit_solution(2100488117658005235)
XLA Ops:
  1.3 0.0 copy-start
  1.3 0.0 copy-start.2
  1.3 4.8 %edge_columns.1 = (bf16[1056,256]{1,0:T(8,128)(2,1)S(1)}, bf16[32,512]{1,0:T(8,128)(2,1)S(1)}, f32[1024,256]{1,0:T(8,128)S(1)}, f32[32,512]{1,0:T(8,128)S(1)}, b...) custom-call(s32[1,1]{1,0:T(1,128)S(6)} %copy.12.offset_ref, ...), custom_call_target="tpu_custom_call" | custom-call | flops 1207959552 | bytes 8388608 | tf_op jit(solution)/shard_map/edge_columns/pallas_call | solution.py:368
  6.2 2.5 %collective-permute-start = (bf16[1056,256]{1,0:T(8,128)(2,1)S(1)}, bf16[1056,256]{1,0:T(8,128)(2,1)S(1)}, u32[]{:S(2)}, u32[]{:S(2)}) collective-permute-start(bf16[1056,256]{1,0:T(8,128)(2,1)S(1)} %get-tuple-element.32), channel_id=1, source_target_pairs={{0,1},{1,2},{2,3},{3,4},{4,5},{5,6},{6,7},{7,8},{8,9},{9,10},{10,1... | collective-permute-start | bytes 1622024 | tf_op jit(solution)/shard_map/ppermute | solution.py:343
  8.7 6.5 %collective-permute-start.1 = (bf16[32,512]{1,0:T(8,128)(2,1)S(1)}, bf16[32,512]{1,0:T(8,128)(2,1)S(1)}, u32[]{:S(2)}, u32[]{:S(2)}) collective-permute-start(bf16[32,512]{1,0:T(8,128)(2,1)S(1)} %get-tuple-element.33), channel_id=1, source_target_pairs={{0,31},{1,0},{2,1},{3,2},{4,3},{5,4},{6,5},{7,6},{8,7},{9,8},{10,9... | collective-permute-start | bytes 98312 | tf_op jit(solution)/shard_map/ppermute | solution.py:343
  15.2 0.0 copy-done
  15.2 0.0 copy-done.2
  15.2 0.0 copy-start.1
  15.2 6.7 %middle_columns.1 = (bf16[512,896]{1,0:T(8,128)(2,1)S(1)}, bf16[512,768]{1,0:T(8,128)(2,1)S(1)}, bf16[256,1536]{1,0:T(8,128)(2,1)S(1)}) custom-call(s32[1,1]{1,0:T(1,128)S(6)} %copy.12.offset_ref, f32[1,31]{1,0:T(1,128)S(1)} %copy-done, f32[512,1024]{1,0:T(8,128)} %bitcast.6, f32[512,1024]{1,0:T(8,128)} %bitcast.8, s32[1,1024]{1,0:T(1,128)} %col_start_ref.3, ...), custom_call_target="tpu_custom_call" | custom-call | flops 2013265920 | bytes 8388608 | tf_op jit(solution)/shard_map/middle_columns/pallas_call | solution.py:397
  21.8 0.0 copy-done.1
  21.9 3.5 %inner_match.1 = (f32[512,512]{1,0:T(8,128)S(1)}, bf16[512,512]{1,0:T(8,128)(2,1)S(1)}) custom-call(bf16[512,896]{1,0:T(8,128)(2,1)S(1)} %get-tuple-element.28.patch_ref, bf16[512,768]{1,0:T(8,128)(2,1)S(1)} %get-tuple-element.29.weight_ref, bf16[256,1536]{1,0:T(8,128)(2,1)S(1)} %get-tuple-element.30.taps_ref, bf16[128,1920]{1,0:T(8,128)(2,1)S(1)} %copy-done.1), custom_call_target="tpu_custom_call" | custom-call | flops 2617245696 | bytes 8388608 | tf_op jit(solution)/shard_map/inner_match/pallas_call | solution.py:416
  25.3 0.0 collective-permute-done.1.ahead_ref
  25.3 1.8 %collective-permute-done.got_ref = bf16[1056,256]{1,0:T(8,128)(2,1)S(1)} collective-permute-done((bf16[1056,256]{1,0:T(8,128)(2,1)S(1)}, bf16[1056,256]{1,0:T(8,128)(2,1)S(1)}, u32[]{:S(2)}, u32[]{:S(2)}) %collective-permute-start) | collective-permute-done | bytes 540704 | tf_op jit(solution)/shard_map/ppermute | solution.py:343
  27.1 4.2 %outer_match.1 = (f32[512,512]{1,0:T(8,128)S(1)}, bf16[512,1024]{1,0:T(8,128)(2,1)S(1)}, bf16[512,1024]{1,0:T(8,128)(2,1)S(1)}) custom-call(bf16[1056,256]{1,0:T(8,128)(2,1)S(1)} %collective-permute-done.got_ref, bf16[32,512]{1,0:T(8,128)(2,1)S(1)} %collective-permute-done.1.ahead_ref, f32[1024,256]{1,0:T(8,128)S(1)} %get-tuple-element.34.own_ref, ...), custom_call_target="tpu_custom_call" | custom-call | flops 2617245696 | bytes 8388608 | tf_op jit(solution)/shard_map/outer_match/pallas_call | solution.py:425
  31.3 1.3 %collective-permute-start.2 = (bf16[512,1024]{1,0:T(8,128)(2,1)S(1)}, bf16[512,1024]{1,0:T(8,128)(2,1)S(1)}, u32[]{:S(2)}, u32[]{:S(2)}) collective-permute-start(bf16[512,1024]{1,0:T(8,128)(2,1)S(1)} %get-tuple-element.39), channel_id=1, source_target_pairs={{0,32},{32,0},{64,96},{96,64},{128,160},{160,128},{192,224},{224,1... | collective-permute-start | bytes 3145736 | tf_op jit(solution)/shard_map/ppermute | solution.py:351
  32.6 2.3 %collective-permute-done.2.got_ref = bf16[512,1024]{1,0:T(8,128)(2,1)S(1)} collective-permute-done((bf16[512,1024]{1,0:T(8,128)(2,1)S(1)}, bf16[512,1024]{1,0:T(8,128)(2,1)S(1)}, u32[]{:S(2)}, u32[]{:S(2)}) %collective-permute-start.2) | collective-permute-done | bytes 1048608 | tf_op jit(solution)/shard_map/ppermute | solution.py:351
  34.9 0.2 pair_sum.1
  35.1 1.3 %collective-permute-start.3 = (bf16[128,1024]{1,0:T(8,128)(2,1)S(1)}, bf16[128,1024]{1,0:T(8,128)(2,1)S(1)}, u32[]{:S(2)}, u32[]{:S(2)}) collective-permute-start(bf16[128,1024]{1,0:T(8,128)(2,1)S(1)} %get-tuple-element.41), channel_id=1, source_target_pairs={{0,64},{32,96},{64,128},{96,160},{128,192},{160,224},{192,0},{224,... | collective-permute-start | bytes 786440 | tf_op jit(solution)/shard_map/ppermute | solution.py:343
  36.4 2.5 %collective-permute-start.4 = (bf16[128,1024]{1,0:T(8,128)(2,1)S(1)}, bf16[128,1024]{1,0:T(8,128)(2,1)S(1)}, u32[]{:S(2)}, u32[]{:S(2)}) collective-permute-start(bf16[128,1024]{1,0:T(8,128)(2,1)S(1)} %get-tuple-element.42), channel_id=1, source_target_pairs={{0,128},{32,160},{64,192},{96,224},{128,0},{160,32},{192,64},{224,... | collective-permute-start | bytes 786440 | tf_op jit(solution)/shard_map/ppermute | solution.py:343
  38.9 1.2 %collective-permute-start.5 = (bf16[128,1024]{1,0:T(8,128)(2,1)S(1)}, bf16[128,1024]{1,0:T(8,128)(2,1)S(1)}, u32[]{:S(2)}, u32[]{:S(2)}) collective-permute-start(bf16[128,1024]{1,0:T(8,128)(2,1)S(1)} %get-tuple-element.43), channel_id=1, source_target_pairs={{0,192},{32,224},{64,0},{96,32},{128,64},{160,96},{192,128},{224,1... | collective-permute-start | bytes 786440 | tf_op jit(solution)/shard_map/ppermute | solution.py:343
  40.0 3.9 %collective-permute-done.3.one_ref = bf16[128,1024]{1,0:T(8,128)(2,1)S(1)} collective-permute-done((bf16[128,1024]{1,0:T(8,128)(2,1)S(1)}, bf16[128,1024]{1,0:T(8,128)(2,1)S(1)}, u32[]{:S(2)}, u32[]{:S(2)}) %collective-permute-start.3) | collective-permute-done | bytes 262176 | tf_op jit(solution)/shard_map/ppermute | solution.py:343
  43.9 6.6 %collective-permute-done.4.two_ref = bf16[128,1024]{1,0:T(8,128)(2,1)S(1)} collective-permute-done((bf16[128,1024]{1,0:T(8,128)(2,1)S(1)}, bf16[128,1024]{1,0:T(8,128)(2,1)S(1)}, u32[]{:S(2)}, u32[]{:S(2)}) %collective-permute-start.4) | collective-permute-done | bytes 262176 | tf_op jit(solution)/shard_map/ppermute | solution.py:343
  50.5 0.0 collective-permute-done.5.three_ref
  50.5 0.1 coadd.1.refs_2_
  50.7 1.3 %collective-permute-start.6 = (bf16[64,1024]{1,0:T(8,128)(2,1)S(1)}, bf16[64,1024]{1,0:T(8,128)(2,1)S(1)}, u32[]{:S(2)}, u32[]{:S(2)}) collective-permute-start(bf16[64,1024]{1,0:T(8,128)(2,1)S(1)} %coadd.1.refs_2_), channel_id=1, source_target_pairs={{0,64},{32,96},{64,128},{96,160},{128,192},{160,224},{192,0},{224,... | collective-permute-start | bytes 393224 | tf_op jit(solution)/shard_map/ppermute | solution.py:343
  52.0 2.8 %collective-permute-start.7 = (bf16[64,1024]{1,0:T(8,128)(2,1)S(1)}, bf16[64,1024]{1,0:T(8,128)(2,1)S(1)}, u32[]{:S(2)}, u32[]{:S(2)}) collective-permute-start(bf16[64,1024]{1,0:T(8,128)(2,1)S(1)} %coadd.1.refs_2_), channel_id=1, source_target_pairs={{0,128},{32,160},{64,192},{96,224},{128,0},{160,32},{192,64},{224,... | collective-permute-start | bytes 393224 | tf_op jit(solution)/shard_map/ppermute | solution.py:343
  54.7 0.2 collective-permute-start.8
  54.9 2.3 %collective-permute-start.9 = (bf16[64,1024]{1,0:T(8,128)(2,1)S(1)}, bf16[64,1024]{1,0:T(8,128)(2,1)S(1)}, u32[]{:S(2)}, u32[]{:S(2)}) collective-permute-start(bf16[64,1024]{1,0:T(8,128)(2,1)S(1)} %coadd.1.refs_2_), channel_id=1, source_target_pairs={{0,32},{32,0},{64,96},{96,64},{128,160},{160,128},{192,224},{224,1... | collective-permute-start | bytes 393224 | tf_op jit(solution)/shard_map/ppermute | solution.py:351
  57.2 0.0 collective-permute-done.6.refs_3_
  57.2 0.9 %collective-permute-start.10 = (bf16[64,1024]{1,0:T(8,128)(2,1)S(1)}, bf16[64,1024]{1,0:T(8,128)(2,1)S(1)}, u32[]{:S(2)}, u32[]{:S(2)}) collective-permute-start(bf16[64,1024]{1,0:T(8,128)(2,1)S(1)} %collective-permute-done.6.refs_3_), channel_id=1, source_target_pairs={{0,32},{32,0},{64,96},{96,64},{128,160},{160,128},{192,224},{224,1... | collective-permute-start | bytes 393224 | tf_op jit(solution)/shard_map/ppermute | solution.py:351
  58.1 2.5 %collective-permute-done.7.refs_4_ = bf16[64,1024]{1,0:T(8,128)(2,1)S(1)} collective-permute-done((bf16[64,1024]{1,0:T(8,128)(2,1)S(1)}, bf16[64,1024]{1,0:T(8,128)(2,1)S(1)}, u32[]{:S(2)}, u32[]{:S(2)}) %collective-permute-start.7) | collective-permute-done | bytes 131104 | tf_op jit(solution)/shard_map/ppermute | solution.py:343
  60.6 1.3 %collective-permute-start.11 = (bf16[64,1024]{1,0:T(8,128)(2,1)S(1)}, bf16[64,1024]{1,0:T(8,128)(2,1)S(1)}, u32[]{:S(2)}, u32[]{:S(2)}) collective-permute-start(bf16[64,1024]{1,0:T(8,128)(2,1)S(1)} %collective-permute-done.7.refs_4_), channel_id=1, source_target_pairs={{0,32},{32,0},{64,96},{96,64},{128,160},{160,128},{192,224},{224,1... | collective-permute-start | bytes 393224 | tf_op jit(solution)/shard_map/ppermute | solution.py:351
  62.0 0.0 collective-permute-done.8.refs_5_
  62.0 0.0 collective-permute-start.12
  62.0 0.0 collective-permute-done.9.refs_6_
  62.0 0.0 collective-permute-done.10.refs_7_
  62.0 1.0 %collective-permute-done.11.refs_8_ = bf16[64,1024]{1,0:T(8,128)(2,1)S(1)} collective-permute-done((bf16[64,1024]{1,0:T(8,128)(2,1)S(1)}, bf16[64,1024]{1,0:T(8,128)(2,1)S(1)}, u32[]{:S(2)}, u32[]{:S(2)}) %collective-permute-start.11) | collective-permute-done | bytes 131104 | tf_op jit(solution)/shard_map/ppermute | solution.py:351
  62.9 0.4 collective-permute-done.12.refs_9_
  63.3 2.2 %difference.1 = (f32[512,1024]{1,0:T(8,128)}, f32[512,1024]{1,0:T(8,128)}) custom-call(f32[512,512]{1,0:T(8,128)S(1)} %get-tuple-element.31.refs_0_, f32[512,512]{1,0:T(8,128)S(1)} %get-tuple-element.37.refs_1_, bf16[64,1024]{1,0:T(8,128)(2,1)S(1)} %coadd.1.refs_2_, bf16[64,1024]{1,0:T(8,128)(2,1)S(1)} %collective-permute-done.6.refs_3_, ...), custom_call_target="tpu_custom_call" | custom-call | flops 1048576 | bytes 8388608 | tf_op jit(solution)/shard_map/difference/pallas_call | solution.py:460
Async XLA Ops:
  1.3 13.9 %copy-start = (f32[1,31]{1,0:T(1,128)S(1)}, f32[1,31]{1,0:T(1,128)}, u32[]{:S(2)}) copy-start(f32[1,31]{1,0:T(1,128)} %coef_ref.1) | copy-start | bytes 376
  1.3 13.9 %copy-start.2 = (f32[16,128]{1,0:T(8,128)S(1)}, f32[16,128]{1,0:T(8,128)}, u32[]{:S(2)}) copy-start(f32[16,128]{1,0:T(8,128)} %constant.5.clone.factors_ref) | copy-start | bytes 24580
  6.2 20.9 %collective-permute-start = (bf16[1056,256]{1,0:T(8,128)(2,1)S(1)}, bf16[1056,256]{1,0:T(8,128)(2,1)S(1)}, u32[]{:S(2)}, u32[]{:S(2)}) collective-permute-start(bf16[1056,256]{1,0:T(8,128)(2,1)S(1)} %get-tuple-element.32), channel_id=1, source_target_pairs={{0,1},{1,2},{2,3},{3,4},{4,5},{5,6},{6,7},{7,8},{8,9},{9,10},{10,1... | collective-permute-start | bytes 1622024 | tf_op jit(solution)/shard_map/ppermute | solution.py:343
  8.7 16.6 %collective-permute-start.1 = (bf16[32,512]{1,0:T(8,128)(2,1)S(1)}, bf16[32,512]{1,0:T(8,128)(2,1)S(1)}, u32[]{:S(2)}, u32[]{:S(2)}) collective-permute-start(bf16[32,512]{1,0:T(8,128)(2,1)S(1)} %get-tuple-element.33), channel_id=1, source_target_pairs={{0,31},{1,0},{2,1},{3,2},{4,3},{5,4},{6,5},{7,6},{8,7},{9,8},{10,9... | collective-permute-start | bytes 98312 | tf_op jit(solution)/shard_map/ppermute | solution.py:343
  15.2 6.7 %copy-start.1 = (bf16[128,1920]{1,0:T(8,128)(2,1)S(1)}, bf16[128,1920]{1,0:T(8,128)(2,1)}, u32[]{:S(2)}) copy-start(bf16[128,1920]{1,0:T(8,128)(2,1)} %constant.4.clone.band_ref) | copy-start | bytes 1474564
  31.3 3.6 %collective-permute-start.2 = (bf16[512,1024]{1,0:T(8,128)(2,1)S(1)}, bf16[512,1024]{1,0:T(8,128)(2,1)S(1)}, u32[]{:S(2)}, u32[]{:S(2)}) collective-permute-start(bf16[512,1024]{1,0:T(8,128)(2,1)S(1)} %get-tuple-element.39), channel_id=1, source_target_pairs={{0,32},{32,0},{64,96},{96,64},{128,160},{160,128},{192,224},{224,1... | collective-permute-start | bytes 3145736 | tf_op jit(solution)/shard_map/ppermute | solution.py:351
  35.1 8.8 %collective-permute-start.3 = (bf16[128,1024]{1,0:T(8,128)(2,1)S(1)}, bf16[128,1024]{1,0:T(8,128)(2,1)S(1)}, u32[]{:S(2)}, u32[]{:S(2)}) collective-permute-start(bf16[128,1024]{1,0:T(8,128)(2,1)S(1)} %get-tuple-element.41), channel_id=1, source_target_pairs={{0,64},{32,96},{64,128},{96,160},{128,192},{160,224},{192,0},{224,... | collective-permute-start | bytes 786440 | tf_op jit(solution)/shard_map/ppermute | solution.py:343
  36.4 14.1 %collective-permute-start.4 = (bf16[128,1024]{1,0:T(8,128)(2,1)S(1)}, bf16[128,1024]{1,0:T(8,128)(2,1)S(1)}, u32[]{:S(2)}, u32[]{:S(2)}) collective-permute-start(bf16[128,1024]{1,0:T(8,128)(2,1)S(1)} %get-tuple-element.42), channel_id=1, source_target_pairs={{0,128},{32,160},{64,192},{96,224},{128,0},{160,32},{192,64},{224,... | collective-permute-start | bytes 786440 | tf_op jit(solution)/shard_map/ppermute | solution.py:343
  38.9 11.7 %collective-permute-start.5 = (bf16[128,1024]{1,0:T(8,128)(2,1)S(1)}, bf16[128,1024]{1,0:T(8,128)(2,1)S(1)}, u32[]{:S(2)}, u32[]{:S(2)}) collective-permute-start(bf16[128,1024]{1,0:T(8,128)(2,1)S(1)} %get-tuple-element.43), channel_id=1, source_target_pairs={{0,192},{32,224},{64,0},{96,32},{128,64},{160,96},{192,128},{224,1... | collective-permute-start | bytes 786440 | tf_op jit(solution)/shard_map/ppermute | solution.py:343
  50.7 6.6 %collective-permute-start.6 = (bf16[64,1024]{1,0:T(8,128)(2,1)S(1)}, bf16[64,1024]{1,0:T(8,128)(2,1)S(1)}, u32[]{:S(2)}, u32[]{:S(2)}) collective-permute-start(bf16[64,1024]{1,0:T(8,128)(2,1)S(1)} %coadd.1.refs_2_), channel_id=1, source_target_pairs={{0,64},{32,96},{64,128},{96,160},{128,192},{160,224},{192,0},{224,... | collective-permute-start | bytes 393224 | tf_op jit(solution)/shard_map/ppermute | solution.py:343
  52.0 8.7 %collective-permute-start.7 = (bf16[64,1024]{1,0:T(8,128)(2,1)S(1)}, bf16[64,1024]{1,0:T(8,128)(2,1)S(1)}, u32[]{:S(2)}, u32[]{:S(2)}) collective-permute-start(bf16[64,1024]{1,0:T(8,128)(2,1)S(1)} %coadd.1.refs_2_), channel_id=1, source_target_pairs={{0,128},{32,160},{64,192},{96,224},{128,0},{160,32},{192,64},{224,... | collective-permute-start | bytes 393224 | tf_op jit(solution)/shard_map/ppermute | solution.py:343
  54.7 7.3 %collective-permute-start.8 = (bf16[64,1024]{1,0:T(8,128)(2,1)S(1)}, bf16[64,1024]{1,0:T(8,128)(2,1)S(1)}, u32[]{:S(2)}, u32[]{:S(2)}) collective-permute-start(bf16[64,1024]{1,0:T(8,128)(2,1)S(1)} %coadd.1.refs_2_), channel_id=1, source_target_pairs={{0,192},{32,224},{64,0},{96,32},{128,64},{160,96},{192,128},{224,1... | collective-permute-start | bytes 393224 | tf_op jit(solution)/shard_map/ppermute | solution.py:343
  54.9 7.0 %collective-permute-start.9 = (bf16[64,1024]{1,0:T(8,128)(2,1)S(1)}, bf16[64,1024]{1,0:T(8,128)(2,1)S(1)}, u32[]{:S(2)}, u32[]{:S(2)}) collective-permute-start(bf16[64,1024]{1,0:T(8,128)(2,1)S(1)} %coadd.1.refs_2_), channel_id=1, source_target_pairs={{0,32},{32,0},{64,96},{96,64},{128,160},{160,128},{192,224},{224,1... | collective-permute-start | bytes 393224 | tf_op jit(solution)/shard_map/ppermute | solution.py:351
  57.2 4.7 %collective-permute-start.10 = (bf16[64,1024]{1,0:T(8,128)(2,1)S(1)}, bf16[64,1024]{1,0:T(8,128)(2,1)S(1)}, u32[]{:S(2)}, u32[]{:S(2)}) collective-permute-start(bf16[64,1024]{1,0:T(8,128)(2,1)S(1)} %collective-permute-done.6.refs_3_), channel_id=1, source_target_pairs={{0,32},{32,0},{64,96},{96,64},{128,160},{160,128},{192,224},{224,1... | collective-permute-start | bytes 393224 | tf_op jit(solution)/shard_map/ppermute | solution.py:351
  60.6 2.3 %collective-permute-start.11 = (bf16[64,1024]{1,0:T(8,128)(2,1)S(1)}, bf16[64,1024]{1,0:T(8,128)(2,1)S(1)}, u32[]{:S(2)}, u32[]{:S(2)}) collective-permute-start(bf16[64,1024]{1,0:T(8,128)(2,1)S(1)} %collective-permute-done.7.refs_4_), channel_id=1, source_target_pairs={{0,32},{32,0},{64,96},{96,64},{128,160},{160,128},{192,224},{224,1... | collective-permute-start | bytes 393224 | tf_op jit(solution)/shard_map/ppermute | solution.py:351
  62.0 1.3 %collective-permute-start.12 = (bf16[64,1024]{1,0:T(8,128)(2,1)S(1)}, bf16[64,1024]{1,0:T(8,128)(2,1)S(1)}, u32[]{:S(2)}, u32[]{:S(2)}) collective-permute-start(bf16[64,1024]{1,0:T(8,128)(2,1)S(1)} %collective-permute-done.8.refs_5_), channel_id=1, source_target_pairs={{0,32},{32,0},{64,96},{96,64},{128,160},{160,128},{192,224},{224,1... | collective-permute-start | bytes 393224 | tf_op jit(solution)/shard_map/ppermute | solution.py:351

commit v2 on v1

v2 whole, which is shorter than its diff:
```python
import functools
import math

import jax
import jax.numpy as jnp
import numpy as np
from jax import lax
from jax.experimental import pallas as pl
from jax.experimental.pallas import tpu as pltpu
from jax.sharding import PartitionSpec as P

RADIUS = 10
TAPS = 6
ROWS = 512
COLS = 1024
EDGE = 256
LANES = 128
FILTERS = 12
WINDOW = 160
PAD = 16
REACH = 272
PIECE = 64
SPREADS = (0.7, 1.5, 3.0)
DEGREES = (4, 3, 2)
F32 = jnp.float32
BF16 = jnp.bfloat16
VMEM_LIMIT = 28 * 1024 * 1024


def factor_table():
    distance = np.arange(2 * RADIUS + 1).astype(np.float32) - RADIUS
    rows = []
    for spread, degree in zip(SPREADS, DEGREES):
        gaussian = np.exp(-distance * distance / np.float32(2.0 * spread * spread)) / np.float32(
            spread * math.sqrt(2.0 * math.pi)
        )
        for exponent in range(degree + 1):
            rows.append(gaussian * (distance / np.float32(spread)) ** exponent)
    return np.stack(rows).astype(np.float32)


def kernel_terms():
    terms = [[] for _ in range(FILTERS)]
    kernel = 0
    first = 0
    for degree in DEGREES:
        for i in range(degree + 1):
            for j in range(degree + 1 - i):
                terms[first + j].append((kernel, first + i))
                kernel += 1
        first += degree + 1
    return terms


def row_band():
    factors = factor_table().astype(BF16)
    gap = np.arange(LANES)[:, None] + PAD - np.arange(WINDOW)[None, :]
    inside = np.abs(gap) <= RADIUS
    at = np.clip(gap + RADIUS, 0, 2 * RADIUS)
    band = np.where(inside[None], factors[:, at], np.zeros((), BF16))
    return band.transpose(1, 0, 2).reshape(LANES, FILTERS * WINDOW).astype(BF16)


def dot(a, b):
    return jnp.dot(a, b, preferred_element_type=F32)


def build_cols(table, low, width, cols_ref, square_ref):
    first = table[0:1, low : low + width]

    @pl.loop(0, COLS // LANES)
    def _(block):
        at = pl.multiple_of(block * LANES, LANES)
        source = lax.broadcasted_iota(jnp.int32, (LANES, width), 0).astype(F32)
        gap = source - (first - (block * LANES).astype(F32))
        value = jnp.zeros((LANES, width), F32)
        for tap in range(TAPS):
            value = jnp.where(gap == float(tap), table[tap + 1 : tap + 2, low : low + width], value)
        cols_ref[pl.ds(at, LANES), :] = value.astype(BF16)
        square_ref[pl.ds(at, LANES), :] = (value * value).astype(BF16)


def build_rows(row_start_ref, row_weights_ref, flip_ref, rows_ref, square_ref):
    flip_ref[...] = jnp.zeros_like(flip_ref)
    flip_ref[0:1, :] = row_start_ref[...].astype(F32)
    for tap in range(TAPS):
        flip_ref[tap + 1 : tap + 2, :] = row_weights_ref[tap]
    for block in range(ROWS // LANES):
        at = slice(block * LANES, (block + 1) * LANES)
        turned = jnp.transpose(flip_ref[:, at])
        gap = lax.broadcasted_iota(jnp.int32, (LANES, ROWS), 1).astype(F32) - turned[:, 0:1]
        value = jnp.zeros((LANES, ROWS), F32)
        for tap in range(TAPS):
            value = jnp.where(gap == float(tap), turned[:, tap + 1 : tap + 2], value)
        rows_ref[at, :] = value.astype(BF16)
        square_ref[at, :] = (value * value).astype(BF16)


def half_start(side):
    core = lax.axis_index("visit") % 2
    half = (core + 1 - side) % 2
    return half, pl.multiple_of(half * (ROWS - REACH), PAD)


def edge_kernel(
    offset_ref, pixels_ref, noise_ref, col_start_ref, col_weights_ref, row_start_ref, row_weights_ref,
    send_ref, rest_ref, edge_ref, last_weight_ref, last_patch_ref, rows_ref, rows2_ref, low_ref, low2_ref, rolled_ref,
    table_ref, flip_ref, cols_ref, cols2_ref, held_ref, held2_ref, whole_ref,
    col_first_ref, col_taps_ref, row_first_ref, row_taps_ref, sems,
):
    loads = [
        pltpu.make_async_copy(source, target, sems.at[number])
        for number, (source, target) in enumerate(
            (
                (row_start_ref, row_first_ref),
                (row_weights_ref, row_taps_ref),
                (col_start_ref, col_first_ref),
                (col_weights_ref, col_taps_ref),
                (pixels_ref, held_ref),
                (noise_ref, held2_ref),
            )
        )
    ]
    for load in loads:
        load.start()
    shift = offset_ref[0, 0]
    for load in loads[:2]:
        load.wait()
    build_rows(row_first_ref, row_taps_ref, flip_ref, rows_ref, rows2_ref)
    for load in loads[2:4]:
        load.wait()
    table_ref[...] = jnp.zeros_like(table_ref)
    table_ref[0:1, :] = col_first_ref[...].astype(F32)
    for tap in range(TAPS):
        table_ref[tap + 1 : tap + 2, :] = col_taps_ref[tap]
    table = pltpu.roll(table_ref[...], shift, 1)
    rolled_ref[...] = table
    parts = jnp.concatenate([table[:, :EDGE], table[:, COLS - LANES :]], axis=1)
    build_cols(parts, 0, EDGE + LANES, cols_ref, cols2_ref)
    loads[4].wait()
    low_ref[...] = held_ref[...].astype(BF16)
    across = dot(low_ref[...], cols_ref[...]).astype(BF16)
    loads[5].wait()
    low2_ref[...] = held2_ref[...].astype(BF16)
    across2 = dot(low2_ref[...], cols2_ref[...]).astype(BF16)
    warped = dot(rows_ref[...], across)
    inverse = 1.0 / dot(rows2_ref[...], across2)
    scaled = warped * inverse
    mine = lax.broadcasted_iota(jnp.int32, (ROWS, EDGE), 1) >= shift
    edge_scaled = scaled[:, :EDGE]
    edge_inverse = inverse[:, :EDGE]
    edge_ref[0:ROWS, :] = edge_scaled
    edge_ref[ROWS:, :] = edge_inverse
    whole_ref[0:ROWS, :] = jnp.where(mine, 0.0, edge_scaled).astype(BF16)
    whole_ref[ROWS:, :] = jnp.where(mine, 0.0, edge_inverse).astype(BF16)
    half, start = half_start(0)
    rest = pl.multiple_of((1 - half) * REACH, PAD)
    send_ref[0:REACH, :] = whole_ref[pl.ds(start, REACH), :]
    send_ref[REACH : 2 * REACH, :] = whole_ref[pl.ds(start + ROWS, REACH), :]
    rest_ref[0 : ROWS - REACH, :] = whole_ref[pl.ds(rest, ROWS - REACH), :]
    rest_ref[ROWS - REACH :, :] = whole_ref[pl.ds(rest + ROWS, ROWS - REACH), :]
    last_inverse = inverse[:, EDGE:]
    last = scaled[:, EDGE:] / jnp.maximum(last_inverse, 0.1)
    last_weight_ref[...] = last_inverse.astype(BF16)
    last_patch_ref[...] = last.astype(BF16)
    tail = jnp.transpose(last)[LANES - 16 :].astype(BF16)
    send_ref[2 * REACH : 2 * REACH + 16, :] = tail[:, :256]
    send_ref[2 * REACH + 16 :, :] = tail[:, 256:]


def middle_kernel(
    offset_ref, coef_ref, low_ref, low2_ref, rolled_ref, rows_ref, rows2_ref,
    last_patch_ref, last_weight_ref, factors_ref, edge_ref,
    patch_ref, weight_ref, taps_ref, head_ref, sent_ref,
    cols_ref, cols2_ref,
):
    turned = jnp.concatenate(
        [jnp.transpose(edge_ref[0:ROWS, :LANES])[0:16], jnp.transpose(edge_ref[ROWS:, :LANES])[0:16]], axis=0
    )
    column = lax.broadcasted_iota(jnp.int32, (32, ROWS), 0) % 16
    head_ref[...] = jnp.where(column >= offset_ref[0, 0], turned, 0.0).astype(BF16)
    sent_ref[...] = jnp.where(column >= offset_ref[0, 0], 0.0, turned)
    width = COLS - EDGE - LANES
    build_cols(rolled_ref[...], EDGE, width, cols_ref, cols2_ref)
    across = dot(low_ref[...], cols_ref[...]).astype(BF16)
    across2 = dot(low2_ref[...], cols2_ref[...]).astype(BF16)
    warped = dot(rows_ref[...], across)
    inverse = 1.0 / dot(rows2_ref[...], across2)
    patch = (warped * inverse) / jnp.maximum(inverse, 0.1)
    weight_ref[:, :width] = inverse.astype(BF16)
    weight_ref[:, width:] = last_weight_ref[...]
    wide = jnp.concatenate([patch, last_patch_ref[...].astype(F32), jnp.zeros((ROWS, LANES), F32)], axis=1)
    patch_ref[...] = pltpu.roll(wide, RADIUS, 1).astype(BF16)
    below = lax.broadcasted_iota(jnp.int32, (LANES, LANES), 1) <= lax.broadcasted_iota(jnp.int32, (LANES, LANES), 0)
    for b, terms in enumerate(kernel_terms()):
        line = sum(coef_ref[0, k] * factors_ref[a : a + 1, :] for k, a in terms)
        line = line.astype(BF16).astype(F32)
        spread = pltpu.roll(jnp.broadcast_to(line, (LANES, LANES)), 0, 1, stride=1, stride_axis=0)
        lanes = slice(b * LANES, (b + 1) * LANES)
        taps_ref[:LANES, lanes] = jnp.where(below, spread, 0.0).astype(BF16)
        taps_ref[LANES:, lanes] = jnp.where(below, 0.0, spread).astype(BF16)


def row_block(step):
    core = lax.axis_index("visit") % 2
    return pl.multiple_of(((step + 2 * core) % 4) * LANES, LANES)


def convolve(window, taps_ref, band_ref, along_ref):
    for half in range(2):
        source = window(half)
        for piece in range(FILTERS // 2):
            lanes = slice(piece * 2 * LANES, (piece + 1) * 2 * LANES)
            along = dot(source, taps_ref[:, lanes]).astype(BF16)
            at = slice(half * LANES, (half + 1) * LANES)
            along_ref[2 * piece, PAD : PAD + ROWS, at] = along[:, :LANES]
            along_ref[2 * piece + 1, PAD : PAD + ROWS, at] = along[:, LANES:]
    for step in range(ROWS // LANES):
        at = row_block(step)
        source = jnp.concatenate([along_ref[a, pl.ds(at, WINDOW), :] for a in range(FILTERS)], axis=0)
        yield step, at, dot(band_ref[...], source)


def clear_margins(along_ref):
    for a in range(FILTERS):
        along_ref[a, 0:PAD, :] = jnp.zeros((PAD, 2 * LANES), BF16)
        along_ref[a, PAD + ROWS :, :] = jnp.zeros((PAD, 2 * LANES), BF16)


def inner_kernel(patch_ref, weight_ref, taps_ref, band_ref, matched_ref, keep_ref, give_ref, along_ref):
    clear_margins(along_ref)
    halves = (keep_ref, keep_ref, give_ref, give_ref)
    for step in range(4):
        low = LANES * (step % 2)
        halves[step][low : low + LANES, 4 * LANES :] = weight_ref[pl.ds(row_block(step), LANES), :]

    @pl.loop(0, 2)
    def _(pair):
        start = pl.multiple_of(pair * 2 * LANES, 2 * LANES)

        def window(half):
            at = pl.multiple_of(start + LANES + half * LANES, LANES)
            return patch_ref[:, pl.ds(at, 2 * LANES)]

        for step, at, matched in convolve(window, taps_ref, band_ref, along_ref):
            rows = pl.ds(at, LANES)
            matched_ref[rows, pl.ds(start, 2 * LANES)] = matched
            weight = weight_ref[rows, pl.ds(pl.multiple_of(start + LANES, LANES), 2 * LANES)].astype(F32)
            low = LANES * (step % 2)
            halves[step][low : low + LANES, pl.ds(start, 2 * LANES)] = (weight * matched).astype(BF16)


def match_half(
    side, offset_ref, scaled, weights, edge_ref, patch_ref, weight_ref, left, right, taps_ref, band_ref,
    matched_ref, term_ref, along_ref, padded_ref, held_ref,
):
    half, start = half_start(side)
    window = pl.ds(start, REACH)
    inside = pl.multiple_of(half * PAD, PAD)
    for a in range(FILTERS):
        along_ref[a, 0:PAD, :] = jnp.zeros((PAD, 2 * LANES), BF16)
        along_ref[a, REACH:, :] = jnp.zeros((PAD, 2 * LANES), BF16)
    mine = lax.broadcasted_iota(jnp.int32, (REACH, EDGE), 1) >= offset_ref[0, 0]
    total_scaled = jnp.where(mine, edge_ref[window, :], 0.0) + scaled.astype(F32)
    total_weight = jnp.where(mine, edge_ref[pl.ds(start + ROWS, REACH), :], 0.0) + weights.astype(F32)
    patch = total_scaled / jnp.maximum(total_weight, 0.1)
    held_ref[:, :EDGE] = total_weight.astype(BF16)
    held_ref[:, EDGE:] = weight_ref[window, :]
    lane = lax.broadcasted_iota(jnp.int32, (REACH, LANES), 1)
    wide = pltpu.roll(jnp.concatenate([patch, left[window, :]], axis=1), RADIUS, 1)
    padded_ref[:, :EDGE] = wide[:, :EDGE].astype(BF16)
    padded_ref[:, EDGE : EDGE + LANES] = jnp.where(
        lane < RADIUS, wide[:, EDGE:], patch_ref[window, :LANES].astype(F32)
    ).astype(BF16)
    padded_ref[:, EDGE + LANES : COLS] = patch_ref[window, LANES : COLS - EDGE]
    padded_ref[:, COLS:] = jnp.where(
        (lane >= RADIUS) & (lane < 2 * RADIUS), right[window, :],
        jnp.where(lane < RADIUS, patch_ref[window, COLS - EDGE :].astype(F32), 0.0),
    ).astype(BF16)
    own = pl.ds(inside, ROWS // 2)
    term_ref[:, 4 * LANES :] = held_ref[own, :EDGE]

    @pl.loop(0, 2)
    def _(pair):
        def place(half):
            return pl.multiple_of(jnp.where(pair == 0, half, 2 + 5 * half) * LANES, LANES)

        for number in range(2):
            source = padded_ref[:, pl.ds(place(number), 2 * LANES)]
            at = slice(number * LANES, (number + 1) * LANES)
            rows = pl.ds(pl.multiple_of(PAD - inside, PAD), REACH)
            for piece in range(FILTERS // 2):
                along = dot(source, taps_ref[:, piece * 2 * LANES : (piece + 1) * 2 * LANES]).astype(BF16)
                along_ref[2 * piece, rows, at] = along[:, :LANES]
                along_ref[2 * piece + 1, rows, at] = along[:, LANES:]
        lanes = pl.ds(pl.multiple_of(pair * 2 * LANES, LANES), 2 * LANES)
        for step in range(2):
            at = slice(step * LANES, (step + 1) * LANES)
            source = jnp.concatenate(
                [along_ref[a, step * LANES : step * LANES + WINDOW, :] for a in range(FILTERS)], axis=0
            )
            matched = dot(band_ref[...], source)
            matched_ref[at, lanes] = matched
            rows = pl.ds(pl.multiple_of(inside + step * LANES, PAD), LANES)
            weight = jnp.concatenate([held_ref[rows, pl.ds(place(number), LANES)] for number in range(2)], axis=1)
            term_ref[at, lanes] = (weight.astype(F32) * matched).astype(BF16)


def given_kernel(
    offset_ref, got_ref, ahead_ref, edge_ref, sent_ref, patch_ref, weight_ref, taps_ref, band_ref,
    matched_ref, term_ref, left_ref, right_ref,
    along_ref, padded_ref, held_ref, flip_ref,
):
    flip_ref[...] = jnp.zeros_like(flip_ref)
    flip_ref[LANES - 16 :, :256] = got_ref[2 * REACH : 2 * REACH + 16, :].astype(F32)
    flip_ref[LANES - 16 :, 256:] = got_ref[2 * REACH + 16 :, :].astype(F32)
    left_ref[...] = jnp.transpose(flip_ref[...])
    near_scaled = ahead_ref[0:16, :].astype(F32) + sent_ref[0:16, :]
    near_weight = ahead_ref[16:32, :].astype(F32) + sent_ref[16:32, :]
    flip_ref[0:16, :] = near_scaled / jnp.maximum(near_weight, 0.1)
    right_ref[...] = pltpu.roll(jnp.transpose(flip_ref[...]), RADIUS, 1)
    match_half(
        0, offset_ref, got_ref[0:REACH, :], got_ref[REACH : 2 * REACH, :], edge_ref, patch_ref, weight_ref,
        left_ref, right_ref, taps_ref, band_ref, matched_ref, term_ref, along_ref, padded_ref, held_ref,
    )


def kept_kernel(
    offset_ref, got_ref, rest_ref, edge_ref, patch_ref, weight_ref, left_ref, right_ref, taps_ref, band_ref,
    matched_ref, term_ref,
    along_ref, padded_ref, held_ref, joined_ref,
):
    half, _ = half_start(1)
    count = ROWS - REACH
    both = REACH - count
    for part in range(2):
        there = pl.multiple_of(part * REACH + half * count, PAD)
        here = pl.multiple_of(part * REACH + (1 - half) * count, PAD)
        joined_ref[pl.ds(here, both), :] = got_ref[pl.ds(there, both), :]
        here = pl.multiple_of(part * REACH + half * both, PAD)
        joined_ref[pl.ds(here, count), :] = rest_ref[part * count : (part + 1) * count, :]
    match_half(
        1, offset_ref, joined_ref[0:REACH, :], joined_ref[REACH:, :], edge_ref, patch_ref, weight_ref,
        left_ref, right_ref, taps_ref, band_ref, matched_ref, term_ref, along_ref, padded_ref, held_ref,
    )


def pair_kernel(keep_ref, got_ref, keep2_ref, got2_ref, own_ref, one_ref, two_ref, three_ref):
    chip = lax.axis_index("visit") // 2
    width = keep_ref.shape[1]
    for ahead, out_ref in enumerate((own_ref, one_ref, two_ref, three_ref)):
        rows = pl.ds(pl.multiple_of(((chip + ahead) % 4) * PIECE, PIECE), PIECE)
        first = keep_ref[rows, :].astype(F32) + got_ref[rows, :].astype(F32)
        second = keep2_ref[rows, :].astype(F32) + got2_ref[rows, :].astype(F32)
        out_ref[:, :width] = first.astype(out_ref.dtype)
        out_ref[:, width:] = second.astype(out_ref.dtype)


def coadd_kernel(own_ref, one_ref, two_ref, three_ref, coadd_ref):
    total = own_ref[...] + one_ref[...].astype(F32) + two_ref[...].astype(F32) + three_ref[...].astype(F32)
    inner, outer = total[:, : COLS + 2 * LANES], total[:, COLS + 2 * LANES :]
    weight = jnp.maximum(jnp.concatenate([outer[:, 4 * LANES :], inner[:, 4 * LANES :]], axis=1), 0.1)
    terms = jnp.concatenate([outer[:, : 3 * LANES], inner[:, : 4 * LANES], outer[:, 3 * LANES : 4 * LANES]], axis=1)
    coadd_ref[...] = (terms / weight).astype(BF16)


def final_kernel(side, *refs):
    inner_ref, outer_ref = refs[:2]
    pieces = refs[2:6]
    difference_out, image_out, difference_ref, image_ref, sems = refs[-5:]
    index = lax.axis_index("visit")
    chip, core = index // 2, index % 2
    copies = []
    for back, piece_ref in enumerate(pieces):
        within = pl.multiple_of(((chip + 4 - back) % 4) * PIECE, PIECE)
        rows = pl.ds(pl.multiple_of(((core + side) % 2) * (4 * PIECE) + within, PIECE), PIECE)
        near = pl.ds(within, PIECE)
        image = piece_ref[...].astype(F32)
        image_ref[back] = image
        difference_ref[back, :, : 3 * LANES] = outer_ref[near, : 3 * LANES] - image[:, : 3 * LANES]
        difference_ref[back, :, 3 * LANES : 7 * LANES] = inner_ref[rows, :] - image[:, 3 * LANES : 7 * LANES]
        difference_ref[back, :, 7 * LANES :] = outer_ref[near, 3 * LANES :] - image[:, 7 * LANES :]
        for which, (held, out) in enumerate(((image_ref, image_out), (difference_ref, difference_out))):
            copy = pltpu.make_async_copy(held.at[back], out.at[rows, :], sems.at[which, back])
            copy.start()
            copies.append(copy)
    for copy in copies:
        copy.wait()


def call(body, outs, scratch, specs, flops, moved, name, out_spec=None, aliases=None):
    return pl.pallas_call(
        body,
        out_shape=[jax.ShapeDtypeStruct(shape, dtype) for shape, dtype in outs],
        in_specs=specs,
        out_specs=[out_spec or VMEM_SPEC for _ in outs],
        scratch_shapes=scratch,
        input_output_aliases=aliases or {},
        compiler_params=pltpu.CompilerParams(vmem_limit_bytes=VMEM_LIMIT),
        cost_estimate=pl.CostEstimate(flops=flops, bytes_accessed=moved, transcendentals=0),
        name=name,
    )


SMEM_SPEC = pl.BlockSpec(memory_space=pltpu.SMEM)
VMEM_SPEC = pl.BlockSpec(memory_space=pltpu.VMEM)
HBM_SPEC = pl.BlockSpec(memory_space=pltpu.HBM)


def shifted(x, axis, by):
    size = lax.axis_size(axis)
    return lax.ppermute(x, axis, [(i, (i + by) % size) for i in range(size)])


def in_hbm(x):
    return pltpu.with_memory_space_constraint(x, pltpu.HBM)


def partner(x):
    return lax.ppermute(x, "visit", [(i, i ^ 1) for i in range(lax.axis_size("visit"))])


def per_device(
    exposure, variance, col_start, col_weights, row_start, row_weights, offsets, basis_coef
):
    pixels = in_hbm(exposure[0])
    noise = in_hbm(variance[0])
    col_taps = in_hbm(jnp.transpose(col_weights, (1, 0, 2)))
    row_taps = in_hbm(jnp.transpose(row_weights, (1, 0, 2)))
    col_start = in_hbm(col_start)
    row_start = in_hbm(row_start)
    factors = np.zeros((16, LANES), np.float32)
    factors[:FILTERS, : 2 * RADIUS + 1] = factor_table()
    factors = np.roll(factors, -2 * RADIUS, axis=1)
    band = jnp.asarray(row_band())
    width = EDGE + LANES
    send, rest, edge, last_weight, last_patch, rows, rows2, low, low2, rolled = call(
        edge_kernel,
        [
            ((2 * REACH + 32, EDGE), BF16),
            ((2 * (ROWS - REACH), EDGE), BF16),
            ((2 * ROWS, EDGE), F32),
            ((ROWS, LANES), BF16),
            ((ROWS, LANES), BF16),
            ((ROWS, ROWS), BF16),
            ((ROWS, ROWS), BF16),
            ((ROWS, COLS), BF16),
            ((ROWS, COLS), BF16),
            ((8, COLS), F32),
        ],
        [
            pltpu.VMEM((8, COLS), F32),
            pltpu.VMEM((LANES, ROWS), F32),
            pltpu.VMEM((COLS, width), BF16),
            pltpu.VMEM((COLS, width), BF16),
            pltpu.VMEM((ROWS, COLS), F32),
            pltpu.VMEM((ROWS, COLS), F32),
            pltpu.VMEM((2 * ROWS, EDGE), BF16),
            pltpu.VMEM((1, COLS), jnp.int32),
            pltpu.VMEM((TAPS, 1, COLS), F32),
            pltpu.VMEM((1, ROWS), jnp.int32),
            pltpu.VMEM((TAPS, 1, ROWS), F32),
            pltpu.SemaphoreType.DMA((6,)),
        ],
        [SMEM_SPEC] + [HBM_SPEC] * 6,
        4 * ROWS * width * (COLS + ROWS),
        8 << 20,
        "edge_columns",
    )(offsets, pixels, noise, col_start, col_taps, row_start, row_taps)
    got = shifted(send, "patch", 1)
    got_rest = shifted(rest, "patch", 1)
    width = COLS - EDGE - LANES
    patch, weight, taps, head, sent = call(
        middle_kernel,
        [
            ((ROWS, COLS - EDGE + LANES), BF16),
            ((ROWS, COLS - EDGE), BF16),
            ((2 * LANES, FILTERS * LANES), BF16),
            ((32, ROWS), BF16),
            ((32, ROWS), F32),
        ],
        [pltpu.VMEM((COLS, width), BF16), pltpu.VMEM((COLS, width), BF16)],
        [SMEM_SPEC] * 2 + [VMEM_SPEC] * 9,
        1 << 20,
        1 << 10,
        "middle_columns",
    )(offsets, basis_coef, low, low2, rolled, rows, rows2, last_patch, last_weight, jnp.asarray(factors), edge)
    ahead = shifted(head, "patch", -1)
    conv_flops = 2 * ROWS * ROWS * FILTERS * (2 * LANES + WINDOW)
    inner_width = COLS + 2 * LANES
    inner, keep, give = call(
        inner_kernel,
        [((ROWS, 4 * LANES), F32), ((ROWS // 2, inner_width), BF16), ((ROWS // 2, inner_width), BF16)],
        [pltpu.VMEM((FILTERS, ROWS + 2 * PAD, 2 * LANES), BF16)],
        [VMEM_SPEC] * 4,
        1 << 20,
        1 << 10,
        "inner_match",
    )(patch, weight, taps, band)
    inner_sum = keep, partner(give)
    outer_width = 4 * LANES + EDGE
    half_outs = [((ROWS // 2, 4 * LANES), F32), ((ROWS // 2, outer_width), BF16)]
    half_scratch = [
        pltpu.VMEM((FILTERS, REACH + PAD, 2 * LANES), BF16),
        pltpu.VMEM((REACH, COLS + LANES), BF16),
        pltpu.VMEM((REACH, COLS), BF16),
    ]
    given, give, left, right = call(
        given_kernel,
        half_outs + [((ROWS, LANES), F32)] * 2,
        half_scratch + [pltpu.VMEM((LANES, ROWS), F32)],
        [SMEM_SPEC] + [VMEM_SPEC] * 8,
        1 << 20,
        1 << 10,
        "given_match",
    )(offsets, got, ahead, edge, sent, patch, weight, taps, band)
    kept, keep = call(
        kept_kernel,
        half_outs,
        half_scratch + [pltpu.VMEM((2 * REACH, EDGE), BF16)],
        [SMEM_SPEC] + [VMEM_SPEC] * 9,
        8 * conv_flops,
        64 << 20,
        "kept_match",
    )(offsets, got, got_rest, edge, patch, weight, left, right, taps, band)
    own_piece, *others = call(
        pair_kernel,
        [((PIECE, inner_width + outer_width), F32)] + [((PIECE, inner_width + outer_width), BF16)] * 3,
        [],
        [VMEM_SPEC] * 4,
        ROWS * COLS,
        3 << 20,
        "pair_sum",
    )(*inner_sum, keep, partner(give))
    others = [shifted(x, "visit", 2 * ahead) for ahead, x in enumerate(others, 1)]
    (piece,) = call(
        coadd_kernel, [((PIECE, COLS), BF16)], [], [VMEM_SPEC] * 4, 8 * PIECE * COLS, 2 << 20, "coadd"
    )(own_piece, *others)
    column = [piece] + [shifted(piece, "visit", 2 * ahead) for ahead in range(1, 4)]
    swapped = [partner(x) for x in column]
    outs = [((ROWS, COLS), F32), ((ROWS, COLS), F32)]
    scratch = [pltpu.VMEM((4, PIECE, COLS), F32), pltpu.VMEM((4, PIECE, COLS), F32), pltpu.SemaphoreType.DMA((2, 4))]
    half_done = call(
        functools.partial(final_kernel, 0), outs, scratch, [VMEM_SPEC] * 6, ROWS * COLS, 4 << 20, "difference_own", HBM_SPEC
    )(inner, kept, *column)
    difference, image = call(
        functools.partial(final_kernel, 1), outs, scratch, [VMEM_SPEC] * 6 + [HBM_SPEC] * 2, ROWS * COLS, 4 << 20,
        "difference_other", HBM_SPEC, {6: 0, 7: 1},
    )(inner, given, *swapped, *half_done)
    return (difference[None], image)


def solution(mesh):
    return jax.shard_map(
        per_device,
        mesh=mesh,
        in_specs=(
            P("visit", None, "patch"),
            P("visit", None, "patch"),
            P("visit", "patch"),
            P("visit", None, "patch"),
            P("visit", "patch"),
            P("visit", None, "patch"),
            P("visit", "patch"),
            P("visit", None),
        ),
        out_specs=(P("visit", None, "patch"), P(None, "patch")),
        check_vma=False,
    )
```

time: 65.8 us -> 62.4 us (0.948)
  waiting for transfers between devices: 18.4 us -> 13.6 us
  starting transfers between devices: 24 us -> 25.1 us
    ppermute x5 -> x6, waiting for transfers between devices: 3.62 us -> 0.02 us  [partner(): lax.ppermute(x, 'visit', [(i, i ^ 1) for i in range(lax.axis_size('visit'...]
    pallas_call x6 -> x8, Pallas kernels: 15 us -> 17 us  [the longest x1 4.91 us: per_device(): call(edge_kernel, [((2 * REACH + 32, EDGE), BF16), ((2 * (ROWS - REACH),...]
    pallas_call x1, Pallas kernels: 6.65 us -> 4.95 us  [per_device(): call(middle_kernel, [((ROWS, COLS - EDGE + LANES), BF16), ((ROWS, COLS -...]
    ppermute x5 -> x6, starting transfers between devices: 5.85 us -> 7.54 us  [partner(): lax.ppermute(x, 'visit', [(i, i ^ 1) for i in range(lax.axis_size('visit'...]
    ppermute x8 -> x9, waiting for transfers between devices: 14.8 us -> 13.6 us  [shifted(): return lax.ppermute(x, axis, [(i, (i + by) % size) for i in range(size)])]
    ppermute x8 -> x9, starting transfers between devices: 18.2 us -> 17.6 us  [shifted(): return lax.ppermute(x, axis, [(i, (i + by) % size) for i in range(size)])]
  transfers between devices with their start and end apart: 13 -> 15, of which waited for: 7 -> 4; matrix products, arithmetic and copies ran while one was open for 0% -> 0% of each run, Pallas kernels for 15% -> 24%
where the time goes in v2:
time: 62.4 us; the launch traced here: 62.3 us
  starting transfers between devices  25.1 us (40%)
  Pallas kernels  21.9 us (35%)
  waiting for transfers between devices  13.6 us (22%)
  between operations  1.57 us (3%)
    ppermute x9, starting transfers between devices, shifted(): return lax.ppermute(x, axis, [(i, (i + by) % size) for i in range(size)])  17.6 us
    ppermute x9, waiting for transfers between devices, shifted(): return lax.ppermute(x, axis, [(i, (i + by) % size) for i in range(size)])  13.6 us
    ppermute x6, starting transfers between devices, partner(): lax.ppermute(x, 'visit', [(i, i ^ 1) for i in range(lax.axis_size('visit'...  7.54 us
    pallas_call x1, Pallas kernels, per_device(): call(middle_kernel, [((ROWS, COLS - EDGE + LANES), BF16), ((ROWS, COLS -...  4.95 us
    pallas_call x1, Pallas kernels, per_device(): call(edge_kernel, [((2 * REACH + 32, EDGE), BF16), ((2 * (ROWS - REACH),...  4.91 us
    pallas_call x1, Pallas kernels, per_device(): call(inner_kernel, [((ROWS, 4 * LANES), F32), ((ROWS // 2, inner_width),...  3.55 us
    pallas_call x1, Pallas kernels, per_device(): call(given_kernel, half_outs + [((ROWS, LANES), F32)] * 2, half_scratch +...  2.74 us
    pallas_call x1, Pallas kernels, per_device(): call(kept_kernel, half_outs, half_scratch + [pltpu.VMEM((2 * REACH, EDGE)...  2.6 us
  transfers between devices with their start and end apart: 15, of which 4 were waited for; matrix products, arithmetic and copies ran while one was open for 0% of the time, Pallas kernels for 24%

profile of v2, /device:TPU:1, one launch (start us, length us, event | category | flops | bytes accessed | tf_op | source)
XLA Modules:
  0.0 62.3 jit_solution(12145288556740967008)
XLA Ops:
  1.3 0.0 copy-start.1
  1.3 0.0 copy-start.2
  1.3 4.9 %edge_columns.1 = (bf16[576,256]{1,0:T(8,128)(2,1)S(1)}, bf16[480,256]{1,0:T(8,128)(2,1)S(1)}, f32[1024,256]{1,0:T(8,128)S(1)}, bf16[512,128]{1,0:T(8,128)(2,1)S...) custom-call(s32[1,1]{1,0:T(1,128)S(6)} %copy.16.offset_ref, ...), custom_call_target="tpu_custom_call" | custom-call | flops 1207959552 | bytes 8388608 | tf_op jit(solution)/shard_map/edge_columns/pallas_call | solution.py:437
  6.2 2.5 %collective-permute-start = (bf16[576,256]{1,0:T(8,128)(2,1)S(1)}, bf16[576,256]{1,0:T(8,128)(2,1)S(1)}, u32[]{:S(2)}, u32[]{:S(2)}) collective-permute-start(bf16[576,256]{1,0:T(8,128)(2,1)S(1)} %get-tuple-element.46), channel_id=1, source_target_pairs={{0,1},{1,2},{2,3},{3,4},{4,5},{5,6},{6,7},{7,8},{8,9},{9,10},{10,1... | collective-permute-start | bytes 884744 | tf_op jit(solution)/shard_map/ppermute | solution.py:412
  8.8 1.6 %collective-permute-start.3 = (bf16[480,256]{1,0:T(8,128)(2,1)S(1)}, bf16[480,256]{1,0:T(8,128)(2,1)S(1)}, u32[]{:S(2)}, u32[]{:S(2)}) collective-permute-start(bf16[480,256]{1,0:T(8,128)(2,1)S(1)} %get-tuple-element.52), channel_id=1, source_target_pairs={{0,1},{1,2},{2,3},{3,4},{4,5},{5,6},{6,7},{7,8},{8,9},{9,10},{10,1... | collective-permute-start | bytes 737288 | tf_op jit(solution)/shard_map/ppermute | solution.py:412
  10.4 0.0 copy-done.1
  10.4 0.0 copy-done.2
  10.4 0.0 copy-start
  10.4 5.0 %middle_columns.1 = (bf16[512,896]{1,0:T(8,128)(2,1)S(1)}, bf16[512,768]{1,0:T(8,128)(2,1)S(1)}, bf16[256,1536]{1,0:T(8,128)(2,1)S(1)}, bf16[32,512]{1,0:T(8,128)(2,1)S(1)}, f32[32,512]{1,0:T(8,128)S(1)}) custom-call(s32[1,1]{1,0:T(1,128)S(6)} %copy.16.offset_ref, f32[1,31]{1,0:T(1,128)S(1)} %copy-done.2, bf16[512,1024]{1,0:T(8,128)(2,1)S(1)} %get-tuple-element.34.low_ref, ...), custom_call_target="tpu_custom_call" | custom-call | flops 1048576 | bytes 1024 | tf_op jit(solution)/shard_map/middle_columns/pallas_call | solution.py:473
  15.4 5.0 %collective-permute-start.1 = (bf16[32,512]{1,0:T(8,128)(2,1)S(1)}, bf16[32,512]{1,0:T(8,128)(2,1)S(1)}, u32[]{:S(2)}, u32[]{:S(2)}) collective-permute-start(bf16[32,512]{1,0:T(8,128)(2,1)S(1)} %get-tuple-element.47), channel_id=1, source_target_pairs={{0,31},{1,0},{2,1},{3,2},{4,3},{5,4},{6,5},{7,6},{8,7},{9,8},{10,9... | collective-permute-start | bytes 98312 | tf_op jit(solution)/shard_map/ppermute | solution.py:412
  20.3 0.0 copy-done
  20.3 3.5 %inner_match.1 = (f32[512,512]{1,0:T(8,128)S(1)}, bf16[256,1280]{1,0:T(8,128)(2,1)S(1)}, bf16[256,1280]{1,0:T(8,128)(2,1)S(1)}) custom-call(bf16[512,896]{1,0:T(8,128)(2,1)S(1)} %get-tuple-element.42.patch_ref, bf16[512,768]{1,0:T(8,128)(2,1)S(1)} %get-tuple-element.43.weight_ref, bf16[256,1536]{1,0:T(8,128)(2,1)S(1)} %get-tuple-element.44.taps_ref, ...), custom_call_target="tpu_custom_call" | custom-call | flops 1048576 | bytes 1024 | tf_op jit(solution)/shard_map/inner_match/pallas_call | solution.py:491
  23.9 1.0 %collective-permute-start.2 = (bf16[256,1280]{1,0:T(8,128)(2,1)S(1)}, bf16[256,1280]{1,0:T(8,128)(2,1)S(1)}, u32[]{:S(2)}, u32[]{:S(2)}) collective-permute-start(bf16[256,1280]{1,0:T(8,128)(2,1)S(1)} %get-tuple-element.51), channel_id=1, source_target_pairs={{0,32},{32,0},{64,96},{96,64},{128,160},{160,128},{192,224},{224,1... | collective-permute-start | bytes 1966088 | tf_op jit(solution)/shard_map/ppermute | solution.py:420
  24.9 0.0 collective-permute-done.1.ahead_ref
  24.9 0.0 collective-permute-done.got_ref
  24.9 2.7 %given_match.1 = (f32[256,512]{1,0:T(8,128)S(1)}, bf16[256,768]{1,0:T(8,128)(2,1)S(1)}, f32[512,128]{1,0:T(8,128)S(1)}, f32[512,128]{1,0:T(8,128)S(1)}) custom-call(s32[1,1]{1,0:T(1,128)S(6)} %copy.16.offset_ref, bf16[576,256]{1,0:T(8,128)(2,1)S(1)} %collective-permute-done.got_ref, bf16[32,512]{1,0:T(8,128)(2,1)S(1)} %collective-permute-done.1.ahead_ref, ...), custom_call_target="tpu_custom_call" | custom-call | flops 1048576 | bytes 1024 | tf_op jit(solution)/shard_map/given_match/pallas_call | solution.py:508
  27.7 0.3 collective-permute-start.4
  28.0 0.0 collective-permute-done.3.rest_ref
  28.0 2.6 %kept_match.1 = (f32[256,512]{1,0:T(8,128)S(1)}, bf16[256,768]{1,0:T(8,128)(2,1)S(1)}) custom-call(s32[1,1]{1,0:T(1,128)S(6)} %copy.16.offset_ref, bf16[576,256]{1,0:T(8,128)(2,1)S(1)} %collective-permute-done.got_ref, bf16[480,256]{1,0:T(8,128)(2,1)S(1)} %collective-permute-done.3.rest_ref, f32[1024,256]{1,0:T(8,128)S(1)} %get-tuple-element.41.edge_ref, ...), custom_call_target="tpu_custom_call" | custom-call | flops 20937965568 | bytes 67108864 | tf_op jit(solution)/shard_map/kept_match/pallas_call | solution.py:517
  30.6 0.0 collective-permute-done.2.got_ref
  30.6 0.0 collective-permute-done.4.got2_ref
  30.6 0.3 pair_sum.1
  30.9 1.3 %collective-permute-start.5 = (bf16[64,2048]{1,0:T(8,128)(2,1)S(1)}, bf16[64,2048]{1,0:T(8,128)(2,1)S(1)}, u32[]{:S(2)}, u32[]{:S(2)}) collective-permute-start(bf16[64,2048]{1,0:T(8,128)(2,1)S(1)} %get-tuple-element.58), channel_id=1, source_target_pairs={{0,64},{32,96},{64,128},{96,160},{128,192},{160,224},{192,0},{224,... | collective-permute-start | bytes 786440 | tf_op jit(solution)/shard_map/ppermute | solution.py:412
  32.2 2.5 %collective-permute-start.6 = (bf16[64,2048]{1,0:T(8,128)(2,1)S(1)}, bf16[64,2048]{1,0:T(8,128)(2,1)S(1)}, u32[]{:S(2)}, u32[]{:S(2)}) collective-permute-start(bf16[64,2048]{1,0:T(8,128)(2,1)S(1)} %get-tuple-element.59), channel_id=1, source_target_pairs={{0,128},{32,160},{64,192},{96,224},{128,0},{160,32},{192,64},{224,... | collective-permute-start | bytes 786440 | tf_op jit(solution)/shard_map/ppermute | solution.py:412
  34.6 1.1 %collective-permute-start.7 = (bf16[64,2048]{1,0:T(8,128)(2,1)S(1)}, bf16[64,2048]{1,0:T(8,128)(2,1)S(1)}, u32[]{:S(2)}, u32[]{:S(2)}) collective-permute-start(bf16[64,2048]{1,0:T(8,128)(2,1)S(1)} %get-tuple-element.60), channel_id=1, source_target_pairs={{0,192},{32,224},{64,0},{96,32},{128,64},{160,96},{192,128},{224,1... | collective-permute-start | bytes 786440 | tf_op jit(solution)/shard_map/ppermute | solution.py:412
  35.8 3.8 %collective-permute-done.5.one_ref = bf16[64,2048]{1,0:T(8,128)(2,1)S(1)} collective-permute-done((bf16[64,2048]{1,0:T(8,128)(2,1)S(1)}, bf16[64,2048]{1,0:T(8,128)(2,1)S(1)}, u32[]{:S(2)}, u32[]{:S(2)}) %collective-permute-start.5) | collective-permute-done | bytes 262176 | tf_op jit(solution)/shard_map/ppermute | solution.py:412
  39.6 6.6 %collective-permute-done.6.two_ref = bf16[64,2048]{1,0:T(8,128)(2,1)S(1)} collective-permute-done((bf16[64,2048]{1,0:T(8,128)(2,1)S(1)}, bf16[64,2048]{1,0:T(8,128)(2,1)S(1)}, u32[]{:S(2)}, u32[]{:S(2)}) %collective-permute-start.6) | collective-permute-done | bytes 262176 | tf_op jit(solution)/shard_map/ppermute | solution.py:412
  46.2 0.0 collective-permute-done.7.three_ref
  46.2 0.1 coadd.1.refs_2_
  46.3 2.9 %collective-permute-start.13 = (bf16[64,1024]{1,0:T(8,128)(2,1)S(1)}, bf16[64,1024]{1,0:T(8,128)(2,1)S(1)}, u32[]{:S(2)}, u32[]{:S(2)}) collective-permute-start(bf16[64,1024]{1,0:T(8,128)(2,1)S(1)} %coadd.1.refs_2_), channel_id=1, source_target_pairs={{0,192},{32,224},{64,0},{96,32},{128,64},{160,96},{192,128},{224,1... | collective-permute-start | bytes 393224 | tf_op jit(solution)/shard_map/ppermute | solution.py:412
  49.2 0.1 collective-permute-start.11
  49.3 0.6 collective-permute-start.9
  49.9 1.9 %collective-permute-start.8 = (bf16[64,1024]{1,0:T(8,128)(2,1)S(1)}, bf16[64,1024]{1,0:T(8,128)(2,1)S(1)}, u32[]{:S(2)}, u32[]{:S(2)}) collective-permute-start(bf16[64,1024]{1,0:T(8,128)(2,1)S(1)} %coadd.1.refs_2_), channel_id=1, source_target_pairs={{0,32},{32,0},{64,96},{96,64},{128,160},{160,128},{192,224},{224,1... | collective-permute-start | bytes 393224 | tf_op jit(solution)/shard_map/ppermute | solution.py:420
  51.8 2.7 %collective-permute-done.13.refs_5_ = bf16[64,1024]{1,0:T(8,128)(2,1)S(1)} collective-permute-done((bf16[64,1024]{1,0:T(8,128)(2,1)S(1)}, bf16[64,1024]{1,0:T(8,128)(2,1)S(1)}, u32[]{:S(2)}, u32[]{:S(2)}) %collective-permute-start.13) | collective-permute-done | bytes 131104 | tf_op jit(solution)/shard_map/ppermute | solution.py:412
  54.5 1.2 %collective-permute-start.14 = (bf16[64,1024]{1,0:T(8,128)(2,1)S(1)}, bf16[64,1024]{1,0:T(8,128)(2,1)S(1)}, u32[]{:S(2)}, u32[]{:S(2)}) collective-permute-start(bf16[64,1024]{1,0:T(8,128)(2,1)S(1)} %collective-permute-done.13.refs_5_), channel_id=1, source_target_pairs={{0,32},{32,0},{64,96},{96,64},{128,160},{160,128},{192,224},{224,1... | collective-permute-start | bytes 393224 | tf_op jit(solution)/shard_map/ppermute | solution.py:420
  55.7 0.0 collective-permute-done.11.refs_4_
  55.8 2.1 %collective-permute-start.12 = (bf16[64,1024]{1,0:T(8,128)(2,1)S(1)}, bf16[64,1024]{1,0:T(8,128)(2,1)S(1)}, u32[]{:S(2)}, u32[]{:S(2)}) collective-permute-start(bf16[64,1024]{1,0:T(8,128)(2,1)S(1)} %collective-permute-done.11.refs_4_), channel_id=1, source_target_pairs={{0,32},{32,0},{64,96},{96,64},{128,160},{160,128},{192,224},{224,1... | collective-permute-start | bytes 393224 | tf_op jit(solution)/shard_map/ppermute | solution.py:420
  57.9 0.5 collective-permute-done.9.refs_3_
  58.3 0.9 %collective-permute-start.10 = (bf16[64,1024]{1,0:T(8,128)(2,1)S(1)}, bf16[64,1024]{1,0:T(8,128)(2,1)S(1)}, u32[]{:S(2)}, u32[]{:S(2)}) collective-permute-start(bf16[64,1024]{1,0:T(8,128)(2,1)S(1)} %collective-permute-done.9.refs_3_), channel_id=1, source_target_pairs={{0,32},{32,0},{64,96},{96,64},{128,160},{160,128},{192,224},{224,1... | collective-permute-start | bytes 393224 | tf_op jit(solution)/shard_map/ppermute | solution.py:420
  59.2 1.4 %difference_own.1 = (f32[512,1024]{1,0:T(8,128)}, f32[512,1024]{1,0:T(8,128)}) custom-call(f32[512,512]{1,0:T(8,128)S(1)} %get-tuple-element.45.refs_0_, f32[256,512]{1,0:T(8,128)S(1)} %get-tuple-element.61.refs_1_, bf16[64,1024]{1,0:T(8,128)(2,1)S(1)} %coadd.1.refs_2_, bf16[64,1024]{1,0:T(8,128)(2,1)S(1)} %collective-permute-done.9.refs_3_, ...), custom_call_target="tpu_custom_call" | custom-call | flops 524288 | bytes 4194304 | tf_op jit(solution)/shard_map/difference_own/pallas_call | solution.py:543
  60.7 0.0 collective-permute-done.8.refs_2_
  60.7 0.0 collective-permute-done.14.refs_5_
  60.7 0.0 collective-permute-done.12.refs_4_
  60.7 0.0 collective-permute-done.10.refs_3_
  60.7 1.4 %difference_other.1 = (f32[512,1024]{1,0:T(8,128)}, f32[512,1024]{1,0:T(8,128)}) custom-call(f32[512,512]{1,0:T(8,128)S(1)} %get-tuple-element.45.refs_0_, f32[256,512]{1,0:T(8,128)S(1)} %get-tuple-element.49.refs_1_, bf16[64,1024]{1,0:T(8,128)(2,1)S(1)} %collective-permute-done.8.refs_2_, ...), custom_call_target="tpu_custom_call", output_to_operand_aliasing={{0}: (6, {}), {1}: (7, {})} | custom-call | flops 524288 | bytes 4194304 | tf_op jit(solution)/shard_map/difference_other/pallas_call | solution.py:546
Async XLA Ops:
  1.3 9.1 %copy-start.1 = (f32[16,128]{1,0:T(8,128)S(1)}, f32[16,128]{1,0:T(8,128)}, u32[]{:S(2)}) copy-start(f32[16,128]{1,0:T(8,128)} %constant.5.clone.factors_ref) | copy-start | bytes 24580
  1.3 9.1 %copy-start.2 = (f32[1,31]{1,0:T(1,128)S(1)}, f32[1,31]{1,0:T(1,128)}, u32[]{:S(2)}) copy-start(f32[1,31]{1,0:T(1,128)} %coef_ref.1) | copy-start | bytes 376
  6.2 18.7 %collective-permute-start = (bf16[576,256]{1,0:T(8,128)(2,1)S(1)}, bf16[576,256]{1,0:T(8,128)(2,1)S(1)}, u32[]{:S(2)}, u32[]{:S(2)}) collective-permute-start(bf16[576,256]{1,0:T(8,128)(2,1)S(1)} %get-tuple-element.46), channel_id=1, source_target_pairs={{0,1},{1,2},{2,3},{3,4},{4,5},{5,6},{6,7},{7,8},{8,9},{9,10},{10,1... | collective-permute-start | bytes 884744 | tf_op jit(solution)/shard_map/ppermute | solution.py:412
  8.8 19.2 %collective-permute-start.3 = (bf16[480,256]{1,0:T(8,128)(2,1)S(1)}, bf16[480,256]{1,0:T(8,128)(2,1)S(1)}, u32[]{:S(2)}, u32[]{:S(2)}) collective-permute-start(bf16[480,256]{1,0:T(8,128)(2,1)S(1)} %get-tuple-element.52), channel_id=1, source_target_pairs={{0,1},{1,2},{2,3},{3,4},{4,5},{5,6},{6,7},{7,8},{8,9},{9,10},{10,1... | collective-permute-start | bytes 737288 | tf_op jit(solution)/shard_map/ppermute | solution.py:412
  10.4 9.9 %copy-start = (bf16[128,1920]{1,0:T(8,128)(2,1)S(1)}, bf16[128,1920]{1,0:T(8,128)(2,1)}, u32[]{:S(2)}) copy-start(bf16[128,1920]{1,0:T(8,128)(2,1)} %constant.4.clone.band_ref) | copy-start | bytes 1474564
  15.4 9.6 %collective-permute-start.1 = (bf16[32,512]{1,0:T(8,128)(2,1)S(1)}, bf16[32,512]{1,0:T(8,128)(2,1)S(1)}, u32[]{:S(2)}, u32[]{:S(2)}) collective-permute-start(bf16[32,512]{1,0:T(8,128)(2,1)S(1)} %get-tuple-element.47), channel_id=1, source_target_pairs={{0,31},{1,0},{2,1},{3,2},{4,3},{5,4},{6,5},{7,6},{8,7},{9,8},{10,9... | collective-permute-start | bytes 98312 | tf_op jit(solution)/shard_map/ppermute | solution.py:412
  23.9 6.7 %collective-permute-start.2 = (bf16[256,1280]{1,0:T(8,128)(2,1)S(1)}, bf16[256,1280]{1,0:T(8,128)(2,1)S(1)}, u32[]{:S(2)}, u32[]{:S(2)}) collective-permute-start(bf16[256,1280]{1,0:T(8,128)(2,1)S(1)} %get-tuple-element.51), channel_id=1, source_target_pairs={{0,32},{32,0},{64,96},{96,64},{128,160},{160,128},{192,224},{224,1... | collective-permute-start | bytes 1966088 | tf_op jit(solution)/shard_map/ppermute | solution.py:420
  27.7 2.9 %collective-permute-start.4 = (bf16[256,768]{1,0:T(8,128)(2,1)S(1)}, bf16[256,768]{1,0:T(8,128)(2,1)S(1)}, u32[]{:S(2)}, u32[]{:S(2)}) collective-permute-start(bf16[256,768]{1,0:T(8,128)(2,1)S(1)} %get-tuple-element.56), channel_id=1, source_target_pairs={{0,32},{32,0},{64,96},{96,64},{128,160},{160,128},{192,224},{224,1... | collective-permute-start | bytes 1179656 | tf_op jit(solution)/shard_map/ppermute | solution.py:420
  30.9 8.7 %collective-permute-start.5 = (bf16[64,2048]{1,0:T(8,128)(2,1)S(1)}, bf16[64,2048]{1,0:T(8,128)(2,1)S(1)}, u32[]{:S(2)}, u32[]{:S(2)}) collective-permute-start(bf16[64,2048]{1,0:T(8,128)(2,1)S(1)} %get-tuple-element.58), channel_id=1, source_target_pairs={{0,64},{32,96},{64,128},{96,160},{128,192},{160,224},{192,0},{224,... | collective-permute-start | bytes 786440 | tf_op jit(solution)/shard_map/ppermute | solution.py:412
  32.2 14.0 %collective-permute-start.6 = (bf16[64,2048]{1,0:T(8,128)(2,1)S(1)}, bf16[64,2048]{1,0:T(8,128)(2,1)S(1)}, u32[]{:S(2)}, u32[]{:S(2)}) collective-permute-start(bf16[64,2048]{1,0:T(8,128)(2,1)S(1)} %get-tuple-element.59), channel_id=1, source_target_pairs={{0,128},{32,160},{64,192},{96,224},{128,0},{160,32},{192,64},{224,... | collective-permute-start | bytes 786440 | tf_op jit(solution)/shard_map/ppermute | solution.py:412
  34.6 11.6 %collective-permute-start.7 = (bf16[64,2048]{1,0:T(8,128)(2,1)S(1)}, bf16[64,2048]{1,0:T(8,128)(2,1)S(1)}, u32[]{:S(2)}, u32[]{:S(2)}) collective-permute-start(bf16[64,2048]{1,0:T(8,128)(2,1)S(1)} %get-tuple-element.60), channel_id=1, source_target_pairs={{0,192},{32,224},{64,0},{96,32},{128,64},{160,96},{192,128},{224,1... | collective-permute-start | bytes 786440 | tf_op jit(solution)/shard_map/ppermute | solution.py:412
  46.3 8.2 %collective-permute-start.13 = (bf16[64,1024]{1,0:T(8,128)(2,1)S(1)}, bf16[64,1024]{1,0:T(8,128)(2,1)S(1)}, u32[]{:S(2)}, u32[]{:S(2)}) collective-permute-start(bf16[64,1024]{1,0:T(8,128)(2,1)S(1)} %coadd.1.refs_2_), channel_id=1, source_target_pairs={{0,192},{32,224},{64,0},{96,32},{128,64},{160,96},{192,128},{224,1... | collective-permute-start | bytes 393224 | tf_op jit(solution)/shard_map/ppermute | solution.py:412
  49.2 6.6 %collective-permute-start.11 = (bf16[64,1024]{1,0:T(8,128)(2,1)S(1)}, bf16[64,1024]{1,0:T(8,128)(2,1)S(1)}, u32[]{:S(2)}, u32[]{:S(2)}) collective-permute-start(bf16[64,1024]{1,0:T(8,128)(2,1)S(1)} %coadd.1.refs_2_), channel_id=1, source_target_pairs={{0,128},{32,160},{64,192},{96,224},{128,0},{160,32},{192,64},{224,... | collective-permute-start | bytes 393224 | tf_op jit(solution)/shard_map/ppermute | solution.py:412
  49.3 9.0 %collective-permute-start.9 = (bf16[64,1024]{1,0:T(8,128)(2,1)S(1)}, bf16[64,1024]{1,0:T(8,128)(2,1)S(1)}, u32[]{:S(2)}, u32[]{:S(2)}) collective-permute-start(bf16[64,1024]{1,0:T(8,128)(2,1)S(1)} %coadd.1.refs_2_), channel_id=1, source_target_pairs={{0,64},{32,96},{64,128},{96,160},{128,192},{160,224},{192,0},{224,... | collective-permute-start | bytes 393224 | tf_op jit(solution)/shard_map/ppermute | solution.py:412
  49.9 10.8 %collective-permute-start.8 = (bf16[64,1024]{1,0:T(8,128)(2,1)S(1)}, bf16[64,1024]{1,0:T(8,128)(2,1)S(1)}, u32[]{:S(2)}, u32[]{:S(2)}) collective-permute-start(bf16[64,1024]{1,0:T(8,128)(2,1)S(1)} %coadd.1.refs_2_), channel_id=1, source_target_pairs={{0,32},{32,0},{64,96},{96,64},{128,160},{160,128},{192,224},{224,1... | collective-permute-start | bytes 393224 | tf_op jit(solution)/shard_map/ppermute | solution.py:420
  54.5 6.2 %collective-permute-start.14 = (bf16[64,1024]{1,0:T(8,128)(2,1)S(1)}, bf16[64,1024]{1,0:T(8,128)(2,1)S(1)}, u32[]{:S(2)}, u32[]{:S(2)}) collective-permute-start(bf16[64,1024]{1,0:T(8,128)(2,1)S(1)} %collective-permute-done.13.refs_5_), channel_id=1, source_target_pairs={{0,32},{32,0},{64,96},{96,64},{128,160},{160,128},{192,224},{224,1... | collective-permute-start | bytes 393224 | tf_op jit(solution)/shard_map/ppermute | solution.py:420
  55.8 4.9 %collective-permute-start.12 = (bf16[64,1024]{1,0:T(8,128)(2,1)S(1)}, bf16[64,1024]{1,0:T(8,128)(2,1)S(1)}, u32[]{:S(2)}, u32[]{:S(2)}) collective-permute-start(bf16[64,1024]{1,0:T(8,128)(2,1)S(1)} %collective-permute-done.11.refs_4_), channel_id=1, source_target_pairs={{0,32},{32,0},{64,96},{96,64},{128,160},{160,128},{192,224},{224,1... | collective-permute-start | bytes 393224 | tf_op jit(solution)/shard_map/ppermute | solution.py:420
  58.3 2.4 %collective-permute-start.10 = (bf16[64,1024]{1,0:T(8,128)(2,1)S(1)}, bf16[64,1024]{1,0:T(8,128)(2,1)S(1)}, u32[]{:S(2)}, u32[]{:S(2)}) collective-permute-start(bf16[64,1024]{1,0:T(8,128)(2,1)S(1)} %collective-permute-done.9.refs_3_), channel_id=1, source_target_pairs={{0,32},{32,0},{64,96},{96,64},{128,160},{160,128},{192,224},{224,1... | collective-permute-start | bytes 393224 | tf_op jit(solution)/shard_map/ppermute | solution.py:420

commit v3 on v2

--- a/solution.py
+++ b/solution.py
@@ -65,35 +65,43 @@
     return jnp.dot(a, b, preferred_element_type=F32)
 
 
+def nth_tap(gap):
+    return jnp.where((gap & -8) == 0, gap, 7)
+
+
 def build_cols(table, low, width, cols_ref, square_ref):
-    first = table[0:1, low : low + width]
+    taps = table[:, low : low + width]
+    first = taps[TAPS : TAPS + 1].astype(jnp.int32)
+    taps = jnp.where(lax.broadcasted_iota(jnp.int32, (8, width), 0) < TAPS, taps, 0.0)
+    base = lax.broadcasted_iota(jnp.int32, (8, width), 0) - first
 
     @pl.loop(0, COLS // LANES)
     def _(block):
-        at = pl.multiple_of(block * LANES, LANES)
-        source = lax.broadcasted_iota(jnp.int32, (LANES, width), 0).astype(F32)
-        gap = source - (first - (block * LANES).astype(F32))
-        value = jnp.zeros((LANES, width), F32)
-        for tap in range(TAPS):
-            value = jnp.where(gap == float(tap), table[tap + 1 : tap + 2, low : low + width], value)
-        cols_ref[pl.ds(at, LANES), :] = value.astype(BF16)
-        square_ref[pl.ds(at, LANES), :] = (value * value).astype(BF16)
+        for group in range(LANES // PAD):
+            at = block * LANES + group * PAD
+            value = jnp.concatenate(
+                [jnp.take_along_axis(taps, nth_tap(base + (at + step)), axis=0) for step in (0, 8)], axis=0
+            )
+            rows = pl.ds(pl.multiple_of(at, PAD), PAD)
+            cols_ref[rows, :] = value.astype(BF16)
+            square_ref[rows, :] = (value * value).astype(BF16)
 
 
 def build_rows(row_start_ref, row_weights_ref, flip_ref, rows_ref, square_ref):
     flip_ref[...] = jnp.zeros_like(flip_ref)
-    flip_ref[0:1, :] = row_start_ref[...].astype(F32)
     for tap in range(TAPS):
-        flip_ref[tap + 1 : tap + 2, :] = row_weights_ref[tap]
+        flip_ref[tap : tap + 1, :] = row_weights_ref[tap]
+    flip_ref[8:9, :] = row_start_ref[...].astype(F32)
     for block in range(ROWS // LANES):
         at = slice(block * LANES, (block + 1) * LANES)
         turned = jnp.transpose(flip_ref[:, at])
-        gap = lax.broadcasted_iota(jnp.int32, (LANES, ROWS), 1).astype(F32) - turned[:, 0:1]
-        value = jnp.zeros((LANES, ROWS), F32)
-        for tap in range(TAPS):
-            value = jnp.where(gap == float(tap), turned[:, tap + 1 : tap + 2], value)
-        rows_ref[at, :] = value.astype(BF16)
-        square_ref[at, :] = (value * value).astype(BF16)
+        lane = lax.broadcasted_iota(jnp.int32, (LANES, LANES), 1)
+        base = lane - turned[:, 8:9].astype(jnp.int32)
+        for part in range(ROWS // LANES):
+            value = jnp.take_along_axis(turned, nth_tap(base + part * LANES), axis=1)
+            lanes = slice(part * LANES, (part + 1) * LANES)
+            rows_ref[at, lanes] = value.astype(BF16)
+            square_ref[at, lanes] = (value * value).astype(BF16)
 
 
 def half_start(side):
@@ -130,9 +138,9 @@
     for load in loads[2:4]:
         load.wait()
     table_ref[...] = jnp.zeros_like(table_ref)
-    table_ref[0:1, :] = col_first_ref[...].astype(F32)
     for tap in range(TAPS):
-        table_ref[tap + 1 : tap + 2, :] = col_taps_ref[tap]
+        table_ref[tap : tap + 1, :] = col_taps_ref[tap]
+    table_ref[TAPS : TAPS + 1, :] = col_first_ref[...].astype(F32)
     table = pltpu.roll(table_ref[...], shift, 1)
     rolled_ref[...] = table
     parts = jnp.concatenate([table[:, :EDGE], table[:, COLS - LANES :]], axis=1)
@@ -345,10 +353,10 @@
     )
 
 
-def pair_kernel(keep_ref, got_ref, keep2_ref, got2_ref, own_ref, one_ref, two_ref, three_ref):
+def pair_kernel(keep_ref, got_ref, keep2_ref, got2_ref, own_ref, two_ref, one_ref, three_ref):
     chip = lax.axis_index("visit") // 2
     width = keep_ref.shape[1]
-    for ahead, out_ref in enumerate((own_ref, one_ref, two_ref, three_ref)):
+    for ahead, out_ref in ((0, own_ref), (2, two_ref), (1, one_ref), (3, three_ref)):
         rows = pl.ds(pl.multiple_of(((chip + ahead) % 4) * PIECE, PIECE), PIECE)
         first = keep_ref[rows, :].astype(F32) + got_ref[rows, :].astype(F32)
         second = keep2_ref[rows, :].astype(F32) + got2_ref[rows, :].astype(F32)
@@ -364,28 +372,43 @@
     coadd_ref[...] = (terms / weight).astype(BF16)
 
 
-def final_kernel(side, *refs):
-    inner_ref, outer_ref = refs[:2]
-    pieces = refs[2:6]
+def final_kernel(places, *refs):
+    inner_ref, *outer_refs = refs[:3]
     difference_out, image_out, difference_ref, image_ref, sems = refs[-5:]
     index = lax.axis_index("visit")
     chip, core = index // 2, index % 2
     copies = []
-    for back, piece_ref in enumerate(pieces):
+    for number, (side, back) in enumerate(places):
+        outer_ref = outer_refs[side]
         within = pl.multiple_of(((chip + 4 - back) % 4) * PIECE, PIECE)
         rows = pl.ds(pl.multiple_of(((core + side) % 2) * (4 * PIECE) + within, PIECE), PIECE)
         near = pl.ds(within, PIECE)
-        image = piece_ref[...].astype(F32)
-        image_ref[back] = image
-        difference_ref[back, :, : 3 * LANES] = outer_ref[near, : 3 * LANES] - image[:, : 3 * LANES]
-        difference_ref[back, :, 3 * LANES : 7 * LANES] = inner_ref[rows, :] - image[:, 3 * LANES : 7 * LANES]
-        difference_ref[back, :, 7 * LANES :] = outer_ref[near, 3 * LANES :] - image[:, 7 * LANES :]
+        image = refs[3 + number][...].astype(F32)
+        image_ref[number] = image
+        difference_ref[number, :, : 3 * LANES] = outer_ref[near, : 3 * LANES] - image[:, : 3 * LANES]
+        difference_ref[number, :, 3 * LANES : 7 * LANES] = inner_ref[rows, :] - image[:, 3 * LANES : 7 * LANES]
+        difference_ref[number, :, 7 * LANES :] = outer_ref[near, 3 * LANES :] - image[:, 7 * LANES :]
         for which, (held, out) in enumerate(((image_ref, image_out), (difference_ref, difference_out))):
-            copy = pltpu.make_async_copy(held.at[back], out.at[rows, :], sems.at[which, back])
+            copy = pltpu.make_async_copy(held.at[number], out.at[rows, :], sems.at[which, number])
             copy.start()
             copies.append(copy)
     for copy in copies:
         copy.wait()
+
+
+def finish(places, matched, pieces, done, name, moved):
+    count = len(places)
+    return call(
+        functools.partial(final_kernel, places),
+        [((ROWS, COLS), F32), ((ROWS, COLS), F32)],
+        [pltpu.VMEM((count, PIECE, COLS), F32)] * 2 + [pltpu.SemaphoreType.DMA((2, count))],
+        [VMEM_SPEC] * (3 + count) + [HBM_SPEC] * len(done),
+        count * PIECE * COLS,
+        moved,
+        name,
+        HBM_SPEC,
+        {3 + count + i: i for i in range(len(done))},
+    )(*matched, *pieces, *done)
 
 
 def call(body, outs, scratch, specs, flops, moved, name, out_spec=None, aliases=None):
@@ -532,21 +555,19 @@
         3 << 20,
         "pair_sum",
     )(*inner_sum, keep, partner(give))
-    others = [shifted(x, "visit", 2 * ahead) for ahead, x in enumerate(others, 1)]
+    others = [shifted(x, "visit", 2 * ahead) for ahead, x in zip((2, 1, 3), others)]
     (piece,) = call(
         coadd_kernel, [((PIECE, COLS), BF16)], [], [VMEM_SPEC] * 4, 8 * PIECE * COLS, 2 << 20, "coadd"
     )(own_piece, *others)
-    column = [piece] + [shifted(piece, "visit", 2 * ahead) for ahead in range(1, 4)]
+    backs = (1, 3, 2)
+    column = [shifted(piece, "visit", 2 * ahead) for ahead in backs]
+    matched = inner, kept, given
+    across = partner(piece)
+    done = finish(((0, 0), (1, 0)), matched, [piece, across], [], "difference_near", 1 << 20)
+    *done, column[2] = lax.optimization_barrier((*done, column[2]))
     swapped = [partner(x) for x in column]
-    outs = [((ROWS, COLS), F32), ((ROWS, COLS), F32)]
-    scratch = [pltpu.VMEM((4, PIECE, COLS), F32), pltpu.VMEM((4, PIECE, COLS), F32), pltpu.SemaphoreType.DMA((2, 4))]
-    half_done = call(
-        functools.partial(final_kernel, 0), outs, scratch, [VMEM_SPEC] * 6, ROWS * COLS, 4 << 20, "difference_own", HBM_SPEC
-    )(inner, kept, *column)
-    difference, image = call(
-        functools.partial(final_kernel, 1), outs, scratch, [VMEM_SPEC] * 6 + [HBM_SPEC] * 2, ROWS * COLS, 4 << 20,
-        "difference_other", HBM_SPEC, {6: 0, 7: 1},
-    )(inner, given, *swapped, *half_done)
+    done = finish(tuple((0, back) for back in backs), matched, column, done, "difference_own", 64 << 20)
+    difference, image = finish(tuple((1, back) for back in backs), matched, swapped, done, "difference_other", 3 << 20)
     return (difference[None], image)
 
 

time: 62.4 us -> 59.9 us (0.960)
  starting transfers between devices: 25.1 us -> 23 us
    ppermute x6, starting transfers between devices: 7.54 us -> 4.73 us  [partner(): lax.ppermute(x, 'visit', [(i, i ^ 1) for i in range(lax.axis_size('visit'...]
    ppermute x9, starting transfers between devices: 17.6 us -> 18.2 us  [shifted(): return lax.ppermute(x, axis, [(i, (i + by) % size) for i in range(size)])]
    pallas_call x2 -> x3, Pallas kernels: 2.81 us -> 3.46 us  [finish(): call(functools.partial(final_kernel, places), [((ROWS, COLS), F32), ((ROW...]
  transfers between devices with their start and end apart: 15 -> 15, of which waited for: 4 -> 4; matrix products, arithmetic and copies ran while one was open for 0% -> 0% of each run, Pallas kernels for 24% -> 26%
where the time goes in v3:
time: 59.9 us
  starting transfers between devices  23 us (38%)
  Pallas kernels  22 us (37%)
  waiting for transfers between devices  13.3 us (22%)
  between operations  1.57 us (3%)
    ppermute x9, starting transfers between devices, shifted(): return lax.ppermute(x, axis, [(i, (i + by) % size) for i in range(size)])  18.2 us
    ppermute x9, waiting for transfers between devices, shifted(): return lax.ppermute(x, axis, [(i, (i + by) % size) for i in range(size)])  13.3 us
    ppermute x6, starting transfers between devices, partner(): lax.ppermute(x, 'visit', [(i, i ^ 1) for i in range(lax.axis_size('visit'...  4.73 us
    pallas_call x1, Pallas kernels, per_device(): call(edge_kernel, [((2 * REACH + 32, EDGE), BF16), ((2 * (ROWS - REACH),...  4.73 us
    pallas_call x1, Pallas kernels, per_device(): call(middle_kernel, [((ROWS, COLS - EDGE + LANES), BF16), ((ROWS, COLS -...  4.57 us
    pallas_call x1, Pallas kernels, per_device(): call(inner_kernel, [((ROWS, 4 * LANES), F32), ((ROWS // 2, inner_width),...  3.51 us
    pallas_call x3, Pallas kernels, finish(): call(functools.partial(final_kernel, places), [((ROWS, COLS), F32), ((ROW...  3.46 us
    pallas_call x1, Pallas kernels, per_device(): call(given_kernel, half_outs + [((ROWS, LANES), F32)] * 2, half_scratch +...  2.72 us
  transfers between devices with their start and end apart: 15, of which 4 were waited for; matrix products, arithmetic and copies ran while one was open for 0% of the time, Pallas kernels for 26%

profile of v3, /device:TPU:1, one launch (start us, length us, event | category | flops | bytes accessed | tf_op | source)
XLA Modules:
  0.0 59.9 jit_solution(7095278712558937678)
XLA Ops:
  1.3 0.0 copy-start.1
  1.3 0.0 copy-start.2
  1.3 4.7 %edge_columns.1 = (bf16[576,256]{1,0:T(8,128)(2,1)S(1)}, bf16[480,256]{1,0:T(8,128)(2,1)S(1)}, f32[1024,256]{1,0:T(8,128)S(1)}, bf16[512,128]{1,0:T(8,128)(2,1)S...) custom-call(s32[1,1]{1,0:T(1,128)S(6)} %copy.20.offset_ref, ...), custom_call_target="tpu_custom_call" | custom-call | flops 1207959552 | bytes 8388608 | tf_op jit(solution)/shard_map/edge_columns/pallas_call | solution.py:460
  6.0 2.6 %collective-permute-start = (bf16[576,256]{1,0:T(8,128)(2,1)S(1)}, bf16[576,256]{1,0:T(8,128)(2,1)S(1)}, u32[]{:S(2)}, u32[]{:S(2)}) collective-permute-start(bf16[576,256]{1,0:T(8,128)(2,1)S(1)} %get-tuple-element.51), channel_id=1, source_target_pairs={{0,1},{1,2},{2,3},{3,4},{4,5},{5,6},{6,7},{7,8},{8,9},{9,10},{10,1... | collective-permute-start | bytes 884744 | tf_op jit(solution)/shard_map/ppermute | solution.py:435
  8.6 1.6 %collective-permute-start.1 = (bf16[480,256]{1,0:T(8,128)(2,1)S(1)}, bf16[480,256]{1,0:T(8,128)(2,1)S(1)}, u32[]{:S(2)}, u32[]{:S(2)}) collective-permute-start(bf16[480,256]{1,0:T(8,128)(2,1)S(1)} %get-tuple-element.52), channel_id=1, source_target_pairs={{0,1},{1,2},{2,3},{3,4},{4,5},{5,6},{6,7},{7,8},{8,9},{9,10},{10,1... | collective-permute-start | bytes 737288 | tf_op jit(solution)/shard_map/ppermute | solution.py:435
  10.2 0.0 copy-done.1
  10.2 0.0 copy-done.2
  10.2 0.0 copy-start
  10.2 4.6 %middle_columns.1 = (bf16[512,896]{1,0:T(8,128)(2,1)S(1)}, bf16[512,768]{1,0:T(8,128)(2,1)S(1)}, bf16[256,1536]{1,0:T(8,128)(2,1)S(1)}, bf16[32,512]{1,0:T(8,128)(2,1)S(1)}, f32[32,512]{1,0:T(8,128)S(1)}) custom-call(s32[1,1]{1,0:T(1,128)S(6)} %copy.20.offset_ref, f32[1,31]{1,0:T(1,128)S(1)} %copy-done.2, bf16[512,1024]{1,0:T(8,128)(2,1)S(1)} %get-tuple-element.39.low_ref, ...), custom_call_target="tpu_custom_call" | custom-call | flops 1048576 | bytes 1024 | tf_op jit(solution)/shard_map/middle_columns/pallas_call | solution.py:496
  14.8 5.0 %collective-permute-start.2 = (bf16[32,512]{1,0:T(8,128)(2,1)S(1)}, bf16[32,512]{1,0:T(8,128)(2,1)S(1)}, u32[]{:S(2)}, u32[]{:S(2)}) collective-permute-start(bf16[32,512]{1,0:T(8,128)(2,1)S(1)} %get-tuple-element.53), channel_id=1, source_target_pairs={{0,31},{1,0},{2,1},{3,2},{4,3},{5,4},{6,5},{7,6},{8,7},{9,8},{10,9... | collective-permute-start | bytes 98312 | tf_op jit(solution)/shard_map/ppermute | solution.py:435
  19.8 0.0 copy-done
  19.8 3.5 %inner_match.1 = (f32[512,512]{1,0:T(8,128)S(1)}, bf16[256,1280]{1,0:T(8,128)(2,1)S(1)}, bf16[256,1280]{1,0:T(8,128)(2,1)S(1)}) custom-call(bf16[512,896]{1,0:T(8,128)(2,1)S(1)} %get-tuple-element.47.patch_ref, bf16[512,768]{1,0:T(8,128)(2,1)S(1)} %get-tuple-element.48.weight_ref, bf16[256,1536]{1,0:T(8,128)(2,1)S(1)} %get-tuple-element.49.taps_ref, ...), custom_call_target="tpu_custom_call" | custom-call | flops 1048576 | bytes 1024 | tf_op jit(solution)/shard_map/inner_match/pallas_call | solution.py:514
  23.3 1.1 %collective-permute-start.3 = (bf16[256,1280]{1,0:T(8,128)(2,1)S(1)}, bf16[256,1280]{1,0:T(8,128)(2,1)S(1)}, u32[]{:S(2)}, u32[]{:S(2)}) collective-permute-start(bf16[256,1280]{1,0:T(8,128)(2,1)S(1)} %get-tuple-element.60), channel_id=1, source_target_pairs={{0,32},{32,0},{64,96},{96,64},{128,160},{160,128},{192,224},{224,1... | collective-permute-start | bytes 1966088 | tf_op jit(solution)/shard_map/ppermute | solution.py:443
  24.3 0.0 collective-permute-done.2.ahead_ref
  24.3 0.0 collective-permute-done.got_ref
  24.3 2.7 %given_match.1 = (f32[256,512]{1,0:T(8,128)S(1)}, bf16[256,768]{1,0:T(8,128)(2,1)S(1)}, f32[512,128]{1,0:T(8,128)S(1)}, f32[512,128]{1,0:T(8,128)S(1)}) custom-call(s32[1,1]{1,0:T(1,128)S(6)} %copy.20.offset_ref, bf16[576,256]{1,0:T(8,128)(2,1)S(1)} %collective-permute-done.got_ref, bf16[32,512]{1,0:T(8,128)(2,1)S(1)} %collective-permute-done.2.ahead_ref, ...), custom_call_target="tpu_custom_call" | custom-call | flops 1048576 | bytes 1024 | tf_op jit(solution)/shard_map/given_match/pallas_call | solution.py:531
  27.1 0.3 collective-permute-start.4
  27.4 0.0 collective-permute-done.1.rest_ref
  27.4 2.6 %kept_match.1 = (f32[256,512]{1,0:T(8,128)S(1)}, bf16[256,768]{1,0:T(8,128)(2,1)S(1)}) custom-call(s32[1,1]{1,0:T(1,128)S(6)} %copy.20.offset_ref, bf16[576,256]{1,0:T(8,128)(2,1)S(1)} %collective-permute-done.got_ref, bf16[480,256]{1,0:T(8,128)(2,1)S(1)} %collective-permute-done.1.rest_ref, f32[1024,256]{1,0:T(8,128)S(1)} %get-tuple-element.46.edge_ref, ...), custom_call_target="tpu_custom_call" | custom-call | flops 20937965568 | bytes 67108864 | tf_op jit(solution)/shard_map/kept_match/pallas_call | solution.py:540
  30.0 0.0 collective-permute-done.3.got_ref
  30.0 0.0 collective-permute-done.4.got2_ref
  30.0 0.3 pair_sum.1
  30.2 2.8 %collective-permute-start.5 = (bf16[64,2048]{1,0:T(8,128)(2,1)S(1)}, bf16[64,2048]{1,0:T(8,128)(2,1)S(1)}, u32[]{:S(2)}, u32[]{:S(2)}) collective-permute-start(bf16[64,2048]{1,0:T(8,128)(2,1)S(1)} %get-tuple-element.64), channel_id=1, source_target_pairs={{0,128},{32,160},{64,192},{96,224},{128,0},{160,32},{192,64},{224,... | collective-permute-start | bytes 786440 | tf_op jit(solution)/shard_map/ppermute | solution.py:435
  33.1 0.3 collective-permute-start.6
  33.4 2.4 %collective-permute-start.7 = (bf16[64,2048]{1,0:T(8,128)(2,1)S(1)}, bf16[64,2048]{1,0:T(8,128)(2,1)S(1)}, u32[]{:S(2)}, u32[]{:S(2)}) collective-permute-start(bf16[64,2048]{1,0:T(8,128)(2,1)S(1)} %get-tuple-element.66), channel_id=1, source_target_pairs={{0,192},{32,224},{64,0},{96,32},{128,64},{160,96},{192,128},{224,1... | collective-permute-start | bytes 786440 | tf_op jit(solution)/shard_map/ppermute | solution.py:435
  35.7 3.1 %collective-permute-done.5.one_ref = bf16[64,2048]{1,0:T(8,128)(2,1)S(1)} collective-permute-done((bf16[64,2048]{1,0:T(8,128)(2,1)S(1)}, bf16[64,2048]{1,0:T(8,128)(2,1)S(1)}, u32[]{:S(2)}, u32[]{:S(2)}) %collective-permute-start.5) | collective-permute-done | bytes 262176 | tf_op jit(solution)/shard_map/ppermute | solution.py:435
  38.9 6.8 %collective-permute-done.6.two_ref = bf16[64,2048]{1,0:T(8,128)(2,1)S(1)} collective-permute-done((bf16[64,2048]{1,0:T(8,128)(2,1)S(1)}, bf16[64,2048]{1,0:T(8,128)(2,1)S(1)}, u32[]{:S(2)}, u32[]{:S(2)}) %collective-permute-start.6) | collective-permute-done | bytes 262176 | tf_op jit(solution)/shard_map/ppermute | solution.py:435
  45.7 0.0 collective-permute-done.7.three_ref
  45.7 0.1 coadd.1.refs_3_
  45.8 0.7 %collective-permute-start.12 = (bf16[64,1024]{1,0:T(8,128)(2,1)S(1)}, bf16[64,1024]{1,0:T(8,128)(2,1)S(1)}, u32[]{:S(2)}, u32[]{:S(2)}) collective-permute-start(bf16[64,1024]{1,0:T(8,128)(2,1)S(1)} %coadd.1.refs_3_), channel_id=1, source_target_pairs={{0,32},{32,0},{64,96},{96,64},{128,160},{160,128},{192,224},{224,1... | collective-permute-start | bytes 393224 | tf_op jit(solution)/shard_map/ppermute | solution.py:443
  46.5 1.8 %collective-permute-start.13 = (bf16[64,1024]{1,0:T(8,128)(2,1)S(1)}, bf16[64,1024]{1,0:T(8,128)(2,1)S(1)}, u32[]{:S(2)}, u32[]{:S(2)}) collective-permute-start(bf16[64,1024]{1,0:T(8,128)(2,1)S(1)} %coadd.1.refs_3_), channel_id=1, source_target_pairs={{0,128},{32,160},{64,192},{96,224},{128,0},{160,32},{192,64},{224,... | collective-permute-start | bytes 393224 | tf_op jit(solution)/shard_map/ppermute | solution.py:435
  48.3 1.8 %collective-permute-start.10 = (bf16[64,1024]{1,0:T(8,128)(2,1)S(1)}, bf16[64,1024]{1,0:T(8,128)(2,1)S(1)}, u32[]{:S(2)}, u32[]{:S(2)}) collective-permute-start(bf16[64,1024]{1,0:T(8,128)(2,1)S(1)} %coadd.1.refs_3_), channel_id=1, source_target_pairs={{0,192},{32,224},{64,0},{96,32},{128,64},{160,96},{192,128},{224,1... | collective-permute-start | bytes 393224 | tf_op jit(solution)/shard_map/ppermute | solution.py:435
  50.1 0.0 collective-permute-start.8
  50.1 0.0 collective-permute-done.12.refs_4_
  50.1 1.0 %difference_near.1 = (f32[512,1024]{1,0:T(8,128)}, f32[512,1024]{1,0:T(8,128)}) custom-call(f32[512,512]{1,0:T(8,128)S(1)} %get-tuple-element.50.refs_0_, f32[256,512]{1,0:T(8,128)S(1)} %get-tuple-element.57.refs_1_, f32[256,512]{1,0:T(8,128)S(1)} %get-tuple-element.58.refs_2_, bf16[64,1024]{1,0:T(8,128)(2,1)S(1)} %coadd.1.refs_3_, ...), custom_call_target="tpu_custom_call" | custom-call | flops 131072 | bytes 1048576 | tf_op jit(solution)/shard_map/difference_near/pallas_call | solution.py:401
  51.1 1.9 %collective-permute-done.13.refs_5_ = bf16[64,1024]{1,0:T(8,128)(2,1)S(1)} collective-permute-done((bf16[64,1024]{1,0:T(8,128)(2,1)S(1)}, bf16[64,1024]{1,0:T(8,128)(2,1)S(1)}, u32[]{:S(2)}, u32[]{:S(2)}) %collective-permute-start.13) | collective-permute-done | bytes 131104 | tf_op jit(solution)/shard_map/ppermute | solution.py:435
  53.1 1.3 %collective-permute-start.14 = (bf16[64,1024]{1,0:T(8,128)(2,1)S(1)}, bf16[64,1024]{1,0:T(8,128)(2,1)S(1)}, u32[]{:S(2)}, u32[]{:S(2)}) collective-permute-start(bf16[64,1024]{1,0:T(8,128)(2,1)S(1)} %collective-permute-done.13.refs_5_), channel_id=1, source_target_pairs={{0,32},{32,0},{64,96},{96,64},{128,160},{160,128},{192,224},{224,1... | collective-permute-start | bytes 393224 | tf_op jit(solution)/shard_map/ppermute | solution.py:443
  54.4 1.4 %collective-permute-done.10.refs_4_ = bf16[64,1024]{1,0:T(8,128)(2,1)S(1)} collective-permute-done((bf16[64,1024]{1,0:T(8,128)(2,1)S(1)}, bf16[64,1024]{1,0:T(8,128)(2,1)S(1)}, u32[]{:S(2)}, u32[]{:S(2)}) %collective-permute-start.10) | collective-permute-done | bytes 131104 | tf_op jit(solution)/shard_map/ppermute | solution.py:435
  55.8 0.9 %collective-permute-start.11 = (bf16[64,1024]{1,0:T(8,128)(2,1)S(1)}, bf16[64,1024]{1,0:T(8,128)(2,1)S(1)}, u32[]{:S(2)}, u32[]{:S(2)}) collective-permute-start(bf16[64,1024]{1,0:T(8,128)(2,1)S(1)} %collective-permute-done.10.refs_4_), channel_id=1, source_target_pairs={{0,32},{32,0},{64,96},{96,64},{128,160},{160,128},{192,224},{224,1... | collective-permute-start | bytes 393224 | tf_op jit(solution)/shard_map/ppermute | solution.py:443
  56.7 0.0 collective-permute-done.8.refs_3_
  56.7 0.5 collective-permute-start.9
  57.2 1.2 %difference_own.1 = (f32[512,1024]{1,0:T(8,128)}, f32[512,1024]{1,0:T(8,128)}) custom-call(f32[512,512]{1,0:T(8,128)S(1)} %get-tuple-element.50.refs_0_, f32[256,512]{1,0:T(8,128)S(1)} %get-tuple-element.57.refs_1_, f32[256,512]{1,0:T(8,128)S(1)} %get-tuple-element.58.refs_2_, ...), custom_call_target="tpu_custom_call", output_to_operand_aliasing={{0}: (6, {}), {1}: (7, {})} | custom-call | flops 196608 | bytes 67108864 | tf_op jit(solution)/shard_map/difference_own/pallas_call | solution.py:401
  58.4 0.0 collective-permute-done.14.refs_5_
  58.4 0.0 collective-permute-done.11.refs_4_
  58.5 0.0 collective-permute-done.9.refs_3_
  58.5 1.2 %difference_other.1 = (f32[512,1024]{1,0:T(8,128)}, f32[512,1024]{1,0:T(8,128)}) custom-call(f32[512,512]{1,0:T(8,128)S(1)} %get-tuple-element.50.refs_0_, f32[256,512]{1,0:T(8,128)S(1)} %get-tuple-element.57.refs_1_, f32[256,512]{1,0:T(8,128)S(1)} %get-tuple-element.58.refs_2_, ...), custom_call_target="tpu_custom_call", output_to_operand_aliasing={{0}: (6, {}), {1}: (7, {})} | custom-call | flops 196608 | bytes 3145728 | tf_op jit(solution)/shard_map/difference_other/pallas_call | solution.py:401
Async XLA Ops:
  1.3 8.9 %copy-start.1 = (f32[16,128]{1,0:T(8,128)S(1)}, f32[16,128]{1,0:T(8,128)}, u32[]{:S(2)}) copy-start(f32[16,128]{1,0:T(8,128)} %constant.5.clone.factors_ref) | copy-start | bytes 24580
  1.3 8.9 %copy-start.2 = (f32[1,31]{1,0:T(1,128)S(1)}, f32[1,31]{1,0:T(1,128)}, u32[]{:S(2)}) copy-start(f32[1,31]{1,0:T(1,128)} %coef_ref.1) | copy-start | bytes 376
  6.0 18.3 %collective-permute-start = (bf16[576,256]{1,0:T(8,128)(2,1)S(1)}, bf16[576,256]{1,0:T(8,128)(2,1)S(1)}, u32[]{:S(2)}, u32[]{:S(2)}) collective-permute-start(bf16[576,256]{1,0:T(8,128)(2,1)S(1)} %get-tuple-element.51), channel_id=1, source_target_pairs={{0,1},{1,2},{2,3},{3,4},{4,5},{5,6},{6,7},{7,8},{8,9},{9,10},{10,1... | collective-permute-start | bytes 884744 | tf_op jit(solution)/shard_map/ppermute | solution.py:435
  8.6 18.8 %collective-permute-start.1 = (bf16[480,256]{1,0:T(8,128)(2,1)S(1)}, bf16[480,256]{1,0:T(8,128)(2,1)S(1)}, u32[]{:S(2)}, u32[]{:S(2)}) collective-permute-start(bf16[480,256]{1,0:T(8,128)(2,1)S(1)} %get-tuple-element.52), channel_id=1, source_target_pairs={{0,1},{1,2},{2,3},{3,4},{4,5},{5,6},{6,7},{7,8},{8,9},{9,10},{10,1... | collective-permute-start | bytes 737288 | tf_op jit(solution)/shard_map/ppermute | solution.py:435
  10.2 9.5 %copy-start = (bf16[128,1920]{1,0:T(8,128)(2,1)S(1)}, bf16[128,1920]{1,0:T(8,128)(2,1)}, u32[]{:S(2)}) copy-start(bf16[128,1920]{1,0:T(8,128)(2,1)} %constant.4.clone.band_ref) | copy-start | bytes 1474564
  14.8 9.5 %collective-permute-start.2 = (bf16[32,512]{1,0:T(8,128)(2,1)S(1)}, bf16[32,512]{1,0:T(8,128)(2,1)S(1)}, u32[]{:S(2)}, u32[]{:S(2)}) collective-permute-start(bf16[32,512]{1,0:T(8,128)(2,1)S(1)} %get-tuple-element.53), channel_id=1, source_target_pairs={{0,31},{1,0},{2,1},{3,2},{4,3},{5,4},{6,5},{7,6},{8,7},{9,8},{10,9... | collective-permute-start | bytes 98312 | tf_op jit(solution)/shard_map/ppermute | solution.py:435
  23.3 6.7 %collective-permute-start.3 = (bf16[256,1280]{1,0:T(8,128)(2,1)S(1)}, bf16[256,1280]{1,0:T(8,128)(2,1)S(1)}, u32[]{:S(2)}, u32[]{:S(2)}) collective-permute-start(bf16[256,1280]{1,0:T(8,128)(2,1)S(1)} %get-tuple-element.60), channel_id=1, source_target_pairs={{0,32},{32,0},{64,96},{96,64},{128,160},{160,128},{192,224},{224,1... | collective-permute-start | bytes 1966088 | tf_op jit(solution)/shard_map/ppermute | solution.py:443
  27.1 2.9 %collective-permute-start.4 = (bf16[256,768]{1,0:T(8,128)(2,1)S(1)}, bf16[256,768]{1,0:T(8,128)(2,1)S(1)}, u32[]{:S(2)}, u32[]{:S(2)}) collective-permute-start(bf16[256,768]{1,0:T(8,128)(2,1)S(1)} %get-tuple-element.62), channel_id=1, source_target_pairs={{0,32},{32,0},{64,96},{96,64},{128,160},{160,128},{192,224},{224,1... | collective-permute-start | bytes 1179656 | tf_op jit(solution)/shard_map/ppermute | solution.py:443
  30.2 8.6 %collective-permute-start.5 = (bf16[64,2048]{1,0:T(8,128)(2,1)S(1)}, bf16[64,2048]{1,0:T(8,128)(2,1)S(1)}, u32[]{:S(2)}, u32[]{:S(2)}) collective-permute-start(bf16[64,2048]{1,0:T(8,128)(2,1)S(1)} %get-tuple-element.64), channel_id=1, source_target_pairs={{0,128},{32,160},{64,192},{96,224},{128,0},{160,32},{192,64},{224,... | collective-permute-start | bytes 786440 | tf_op jit(solution)/shard_map/ppermute | solution.py:435
  33.1 12.6 %collective-permute-start.6 = (bf16[64,2048]{1,0:T(8,128)(2,1)S(1)}, bf16[64,2048]{1,0:T(8,128)(2,1)S(1)}, u32[]{:S(2)}, u32[]{:S(2)}) collective-permute-start(bf16[64,2048]{1,0:T(8,128)(2,1)S(1)} %get-tuple-element.65), channel_id=1, source_target_pairs={{0,64},{32,96},{64,128},{96,160},{128,192},{160,224},{192,0},{224,... | collective-permute-start | bytes 786440 | tf_op jit(solution)/shard_map/ppermute | solution.py:435
  33.4 12.3 %collective-permute-start.7 = (bf16[64,2048]{1,0:T(8,128)(2,1)S(1)}, bf16[64,2048]{1,0:T(8,128)(2,1)S(1)}, u32[]{:S(2)}, u32[]{:S(2)}) collective-permute-start(bf16[64,2048]{1,0:T(8,128)(2,1)S(1)} %get-tuple-element.66), channel_id=1, source_target_pairs={{0,192},{32,224},{64,0},{96,32},{128,64},{160,96},{192,128},{224,1... | collective-permute-start | bytes 786440 | tf_op jit(solution)/shard_map/ppermute | solution.py:435
  45.8 4.3 %collective-permute-start.12 = (bf16[64,1024]{1,0:T(8,128)(2,1)S(1)}, bf16[64,1024]{1,0:T(8,128)(2,1)S(1)}, u32[]{:S(2)}, u32[]{:S(2)}) collective-permute-start(bf16[64,1024]{1,0:T(8,128)(2,1)S(1)} %coadd.1.refs_3_), channel_id=1, source_target_pairs={{0,32},{32,0},{64,96},{96,64},{128,160},{160,128},{192,224},{224,1... | collective-permute-start | bytes 393224 | tf_op jit(solution)/shard_map/ppermute | solution.py:443
  46.5 6.6 %collective-permute-start.13 = (bf16[64,1024]{1,0:T(8,128)(2,1)S(1)}, bf16[64,1024]{1,0:T(8,128)(2,1)S(1)}, u32[]{:S(2)}, u32[]{:S(2)}) collective-permute-start(bf16[64,1024]{1,0:T(8,128)(2,1)S(1)} %coadd.1.refs_3_), channel_id=1, source_target_pairs={{0,128},{32,160},{64,192},{96,224},{128,0},{160,32},{192,64},{224,... | collective-permute-start | bytes 393224 | tf_op jit(solution)/shard_map/ppermute | solution.py:435
  48.3 7.6 %collective-permute-start.10 = (bf16[64,1024]{1,0:T(8,128)(2,1)S(1)}, bf16[64,1024]{1,0:T(8,128)(2,1)S(1)}, u32[]{:S(2)}, u32[]{:S(2)}) collective-permute-start(bf16[64,1024]{1,0:T(8,128)(2,1)S(1)} %coadd.1.refs_3_), channel_id=1, source_target_pairs={{0,192},{32,224},{64,0},{96,32},{128,64},{160,96},{192,128},{224,1... | collective-permute-start | bytes 393224 | tf_op jit(solution)/shard_map/ppermute | solution.py:435
  50.1 6.6 %collective-permute-start.8 = (bf16[64,1024]{1,0:T(8,128)(2,1)S(1)}, bf16[64,1024]{1,0:T(8,128)(2,1)S(1)}, u32[]{:S(2)}, u32[]{:S(2)}) collective-permute-start(bf16[64,1024]{1,0:T(8,128)(2,1)S(1)} %coadd.1.refs_3_), channel_id=1, source_target_pairs={{0,64},{32,96},{64,128},{96,160},{128,192},{160,224},{192,0},{224,... | collective-permute-start | bytes 393224 | tf_op jit(solution)/shard_map/ppermute | solution.py:435
  53.1 5.4 %collective-permute-start.14 = (bf16[64,1024]{1,0:T(8,128)(2,1)S(1)}, bf16[64,1024]{1,0:T(8,128)(2,1)S(1)}, u32[]{:S(2)}, u32[]{:S(2)}) collective-permute-start(bf16[64,1024]{1,0:T(8,128)(2,1)S(1)} %collective-permute-done.13.refs_5_), channel_id=1, source_target_pairs={{0,32},{32,0},{64,96},{96,64},{128,160},{160,128},{192,224},{224,1... | collective-permute-start | bytes 393224 | tf_op jit(solution)/shard_map/ppermute | solution.py:443
  55.8 2.6 %collective-permute-start.11 = (bf16[64,1024]{1,0:T(8,128)(2,1)S(1)}, bf16[64,1024]{1,0:T(8,128)(2,1)S(1)}, u32[]{:S(2)}, u32[]{:S(2)}) collective-permute-start(bf16[64,1024]{1,0:T(8,128)(2,1)S(1)} %collective-permute-done.10.refs_4_), channel_id=1, source_target_pairs={{0,32},{32,0},{64,96},{96,64},{128,160},{160,128},{192,224},{224,1... | collective-permute-start | bytes 393224 | tf_op jit(solution)/shard_map/ppermute | solution.py:443
  56.7 1.7 %collective-permute-start.9 = (bf16[64,1024]{1,0:T(8,128)(2,1)S(1)}, bf16[64,1024]{1,0:T(8,128)(2,1)S(1)}, u32[]{:S(2)}, u32[]{:S(2)}) collective-permute-start(bf16[64,1024]{1,0:T(8,128)(2,1)S(1)} %collective-permute-done.8.refs_3_), channel_id=1, source_target_pairs={{0,32},{32,0},{64,96},{96,64},{128,160},{160,128},{192,224},{224,1... | collective-permute-start | bytes 393224 | tf_op jit(solution)/shard_map/ppermute | solution.py:443

commit v4 on v3

--- a/solution.py
+++ b/solution.py
@@ -562,12 +562,11 @@
     backs = (1, 3, 2)
     column = [shifted(piece, "visit", 2 * ahead) for ahead in backs]
     matched = inner, kept, given
-    across = partner(piece)
-    done = finish(((0, 0), (1, 0)), matched, [piece, across], [], "difference_near", 1 << 20)
+    done = finish(((0, 0),), matched, [piece], [], "difference_near", 1 << 20)
     *done, column[2] = lax.optimization_barrier((*done, column[2]))
-    swapped = [partner(x) for x in column]
+    swapped = [partner(x) for x in [piece, *column]]
     done = finish(tuple((0, back) for back in backs), matched, column, done, "difference_own", 64 << 20)
-    difference, image = finish(tuple((1, back) for back in backs), matched, swapped, done, "difference_other", 3 << 20)
+    difference, image = finish(tuple((1, back) for back in (0, *backs)), matched, swapped, done, "difference_other", 3 << 20)
     return (difference[None], image)
 
 

time: 59.9 us -> 59.1 us (0.987)
  waiting for transfers between devices: 13.3 us -> 10.8 us
  starting transfers between devices: 23 us -> 24.7 us
    ppermute x9, waiting for transfers between devices: 13.3 us -> 10.7 us  [shifted(): return lax.ppermute(x, axis, [(i, (i + by) % size) for i in range(size)])]
    ppermute x6, starting transfers between devices: 4.73 us -> 6.37 us  [partner(): lax.ppermute(x, 'visit', [(i, i ^ 1) for i in range(lax.axis_size('visit'...]
  transfers between devices with their start and end apart: 15 -> 15, of which waited for: 4 -> 3; matrix products, arithmetic and copies ran while one was open for 0% -> 0% of each run, Pallas kernels for 26% -> 26%
where the time goes in v4:
time: 59.1 us
  starting transfers between devices  24.7 us (42%)
  Pallas kernels  21.9 us (37%)
  waiting for transfers between devices  10.8 us (18%)
  between operations  1.58 us (3%)
    ppermute x9, starting transfers between devices, shifted(): return lax.ppermute(x, axis, [(i, (i + by) % size) for i in range(size)])  18.4 us
    ppermute x9, waiting for transfers between devices, shifted(): return lax.ppermute(x, axis, [(i, (i + by) % size) for i in range(size)])  10.7 us
    ppermute x6, starting transfers between devices, partner(): lax.ppermute(x, 'visit', [(i, i ^ 1) for i in range(lax.axis_size('visit'...  6.37 us
    pallas_call x1, Pallas kernels, per_device(): call(edge_kernel, [((2 * REACH + 32, EDGE), BF16), ((2 * (ROWS - REACH),...  4.73 us
    pallas_call x1, Pallas kernels, per_device(): call(middle_kernel, [((ROWS, COLS - EDGE + LANES), BF16), ((ROWS, COLS -...  4.57 us
    pallas_call x1, Pallas kernels, per_device(): call(inner_kernel, [((ROWS, 4 * LANES), F32), ((ROWS // 2, inner_width),...  3.51 us
    pallas_call x3, Pallas kernels, finish(): call(functools.partial(final_kernel, places), [((ROWS, COLS), F32), ((ROW...  3.45 us
    pallas_call x1, Pallas kernels, per_device(): call(given_kernel, half_outs + [((ROWS, LANES), F32)] * 2, half_scratch +...  2.72 us
  transfers between devices with their start and end apart: 15, of which 3 were waited for; matrix products, arithmetic and copies ran while one was open for 0% of the time, Pallas kernels for 26%

profile of v4, /device:TPU:1, one launch (start us, length us, event | category | flops | bytes accessed | tf_op | source)
XLA Modules:
  0.0 59.1 jit_solution(5139663067832799338)
XLA Ops:
  1.3 0.0 copy-start.1
  1.3 0.0 copy-start.2
  1.3 4.7 %edge_columns.1 = (bf16[576,256]{1,0:T(8,128)(2,1)S(1)}, bf16[480,256]{1,0:T(8,128)(2,1)S(1)}, f32[1024,256]{1,0:T(8,128)S(1)}, bf16[512,128]{1,0:T(8,128)(2,1)S...) custom-call(s32[1,1]{1,0:T(1,128)S(6)} %copy.20.offset_ref, ...), custom_call_target="tpu_custom_call" | custom-call | flops 1207959552 | bytes 8388608 | tf_op jit(solution)/shard_map/edge_columns/pallas_call | solution.py:460
  6.0 2.6 %collective-permute-start = (bf16[576,256]{1,0:T(8,128)(2,1)S(1)}, bf16[576,256]{1,0:T(8,128)(2,1)S(1)}, u32[]{:S(2)}, u32[]{:S(2)}) collective-permute-start(bf16[576,256]{1,0:T(8,128)(2,1)S(1)} %get-tuple-element.51), channel_id=1, source_target_pairs={{0,1},{1,2},{2,3},{3,4},{4,5},{5,6},{6,7},{7,8},{8,9},{9,10},{10,1... | collective-permute-start | bytes 884744 | tf_op jit(solution)/shard_map/ppermute | solution.py:435
  8.6 1.6 %collective-permute-start.1 = (bf16[480,256]{1,0:T(8,128)(2,1)S(1)}, bf16[480,256]{1,0:T(8,128)(2,1)S(1)}, u32[]{:S(2)}, u32[]{:S(2)}) collective-permute-start(bf16[480,256]{1,0:T(8,128)(2,1)S(1)} %get-tuple-element.52), channel_id=1, source_target_pairs={{0,1},{1,2},{2,3},{3,4},{4,5},{5,6},{6,7},{7,8},{8,9},{9,10},{10,1... | collective-permute-start | bytes 737288 | tf_op jit(solution)/shard_map/ppermute | solution.py:435
  10.2 0.0 copy-done.1
  10.2 0.0 copy-done.2
  10.2 0.0 copy-start
  10.2 4.6 %middle_columns.1 = (bf16[512,896]{1,0:T(8,128)(2,1)S(1)}, bf16[512,768]{1,0:T(8,128)(2,1)S(1)}, bf16[256,1536]{1,0:T(8,128)(2,1)S(1)}, bf16[32,512]{1,0:T(8,128)(2,1)S(1)}, f32[32,512]{1,0:T(8,128)S(1)}) custom-call(s32[1,1]{1,0:T(1,128)S(6)} %copy.20.offset_ref, f32[1,31]{1,0:T(1,128)S(1)} %copy-done.2, bf16[512,1024]{1,0:T(8,128)(2,1)S(1)} %get-tuple-element.39.low_ref, ...), custom_call_target="tpu_custom_call" | custom-call | flops 1048576 | bytes 1024 | tf_op jit(solution)/shard_map/middle_columns/pallas_call | solution.py:496
  14.8 5.0 %collective-permute-start.2 = (bf16[32,512]{1,0:T(8,128)(2,1)S(1)}, bf16[32,512]{1,0:T(8,128)(2,1)S(1)}, u32[]{:S(2)}, u32[]{:S(2)}) collective-permute-start(bf16[32,512]{1,0:T(8,128)(2,1)S(1)} %get-tuple-element.53), channel_id=1, source_target_pairs={{0,31},{1,0},{2,1},{3,2},{4,3},{5,4},{6,5},{7,6},{8,7},{9,8},{10,9... | collective-permute-start | bytes 98312 | tf_op jit(solution)/shard_map/ppermute | solution.py:435
  19.8 0.0 copy-done
  19.8 3.5 %inner_match.1 = (f32[512,512]{1,0:T(8,128)S(1)}, bf16[256,1280]{1,0:T(8,128)(2,1)S(1)}, bf16[256,1280]{1,0:T(8,128)(2,1)S(1)}) custom-call(bf16[512,896]{1,0:T(8,128)(2,1)S(1)} %get-tuple-element.47.patch_ref, bf16[512,768]{1,0:T(8,128)(2,1)S(1)} %get-tuple-element.48.weight_ref, bf16[256,1536]{1,0:T(8,128)(2,1)S(1)} %get-tuple-element.49.taps_ref, ...), custom_call_target="tpu_custom_call" | custom-call | flops 1048576 | bytes 1024 | tf_op jit(solution)/shard_map/inner_match/pallas_call | solution.py:514
  23.3 1.1 %collective-permute-start.3 = (bf16[256,1280]{1,0:T(8,128)(2,1)S(1)}, bf16[256,1280]{1,0:T(8,128)(2,1)S(1)}, u32[]{:S(2)}, u32[]{:S(2)}) collective-permute-start(bf16[256,1280]{1,0:T(8,128)(2,1)S(1)} %get-tuple-element.60), channel_id=1, source_target_pairs={{0,32},{32,0},{64,96},{96,64},{128,160},{160,128},{192,224},{224,1... | collective-permute-start | bytes 1966088 | tf_op jit(solution)/shard_map/ppermute | solution.py:443
  24.3 0.0 collective-permute-done.2.ahead_ref
  24.3 0.0 collective-permute-done.got_ref
  24.3 2.7 %given_match.1 = (f32[256,512]{1,0:T(8,128)S(1)}, bf16[256,768]{1,0:T(8,128)(2,1)S(1)}, f32[512,128]{1,0:T(8,128)S(1)}, f32[512,128]{1,0:T(8,128)S(1)}) custom-call(s32[1,1]{1,0:T(1,128)S(6)} %copy.20.offset_ref, bf16[576,256]{1,0:T(8,128)(2,1)S(1)} %collective-permute-done.got_ref, bf16[32,512]{1,0:T(8,128)(2,1)S(1)} %collective-permute-done.2.ahead_ref, ...), custom_call_target="tpu_custom_call" | custom-call | flops 1048576 | bytes 1024 | tf_op jit(solution)/shard_map/given_match/pallas_call | solution.py:531
  27.1 0.3 collective-permute-start.4
  27.4 0.0 collective-permute-done.1.rest_ref
  27.4 2.6 %kept_match.1 = (f32[256,512]{1,0:T(8,128)S(1)}, bf16[256,768]{1,0:T(8,128)(2,1)S(1)}) custom-call(s32[1,1]{1,0:T(1,128)S(6)} %copy.20.offset_ref, bf16[576,256]{1,0:T(8,128)(2,1)S(1)} %collective-permute-done.got_ref, bf16[480,256]{1,0:T(8,128)(2,1)S(1)} %collective-permute-done.1.rest_ref, f32[1024,256]{1,0:T(8,128)S(1)} %get-tuple-element.46.edge_ref, ...), custom_call_target="tpu_custom_call" | custom-call | flops 20937965568 | bytes 67108864 | tf_op jit(solution)/shard_map/kept_match/pallas_call | solution.py:540
  30.0 0.0 collective-permute-done.3.got_ref
  30.0 0.0 collective-permute-done.4.got2_ref
  30.0 0.3 pair_sum.1
  30.2 2.8 %collective-permute-start.5 = (bf16[64,2048]{1,0:T(8,128)(2,1)S(1)}, bf16[64,2048]{1,0:T(8,128)(2,1)S(1)}, u32[]{:S(2)}, u32[]{:S(2)}) collective-permute-start(bf16[64,2048]{1,0:T(8,128)(2,1)S(1)} %get-tuple-element.64), channel_id=1, source_target_pairs={{0,128},{32,160},{64,192},{96,224},{128,0},{160,32},{192,64},{224,... | collective-permute-start | bytes 786440 | tf_op jit(solution)/shard_map/ppermute | solution.py:435
  33.1 0.3 collective-permute-start.6
  33.4 2.4 %collective-permute-start.7 = (bf16[64,2048]{1,0:T(8,128)(2,1)S(1)}, bf16[64,2048]{1,0:T(8,128)(2,1)S(1)}, u32[]{:S(2)}, u32[]{:S(2)}) collective-permute-start(bf16[64,2048]{1,0:T(8,128)(2,1)S(1)} %get-tuple-element.66), channel_id=1, source_target_pairs={{0,192},{32,224},{64,0},{96,32},{128,64},{160,96},{192,128},{224,1... | collective-permute-start | bytes 786440 | tf_op jit(solution)/shard_map/ppermute | solution.py:435
  35.7 3.1 %collective-permute-done.5.one_ref = bf16[64,2048]{1,0:T(8,128)(2,1)S(1)} collective-permute-done((bf16[64,2048]{1,0:T(8,128)(2,1)S(1)}, bf16[64,2048]{1,0:T(8,128)(2,1)S(1)}, u32[]{:S(2)}, u32[]{:S(2)}) %collective-permute-start.5) | collective-permute-done | bytes 262176 | tf_op jit(solution)/shard_map/ppermute | solution.py:435
  38.9 6.8 %collective-permute-done.6.two_ref = bf16[64,2048]{1,0:T(8,128)(2,1)S(1)} collective-permute-done((bf16[64,2048]{1,0:T(8,128)(2,1)S(1)}, bf16[64,2048]{1,0:T(8,128)(2,1)S(1)}, u32[]{:S(2)}, u32[]{:S(2)}) %collective-permute-start.6) | collective-permute-done | bytes 262176 | tf_op jit(solution)/shard_map/ppermute | solution.py:435
  45.7 0.0 collective-permute-done.7.three_ref
  45.7 0.1 coadd.1.refs_3_
  45.8 1.0 %collective-permute-start.13 = (bf16[64,1024]{1,0:T(8,128)(2,1)S(1)}, bf16[64,1024]{1,0:T(8,128)(2,1)S(1)}, u32[]{:S(2)}, u32[]{:S(2)}) collective-permute-start(bf16[64,1024]{1,0:T(8,128)(2,1)S(1)} %coadd.1.refs_3_), channel_id=1, source_target_pairs={{0,128},{32,160},{64,192},{96,224},{128,0},{160,32},{192,64},{224,... | collective-permute-start | bytes 393224 | tf_op jit(solution)/shard_map/ppermute | solution.py:435
  46.9 2.1 %collective-permute-start.9 = (bf16[64,1024]{1,0:T(8,128)(2,1)S(1)}, bf16[64,1024]{1,0:T(8,128)(2,1)S(1)}, u32[]{:S(2)}, u32[]{:S(2)}) collective-permute-start(bf16[64,1024]{1,0:T(8,128)(2,1)S(1)} %coadd.1.refs_3_), channel_id=1, source_target_pairs={{0,64},{32,96},{64,128},{96,160},{128,192},{160,224},{192,0},{224,... | collective-permute-start | bytes 393224 | tf_op jit(solution)/shard_map/ppermute | solution.py:435
  48.9 0.6 %collective-permute-start.11 = (bf16[64,1024]{1,0:T(8,128)(2,1)S(1)}, bf16[64,1024]{1,0:T(8,128)(2,1)S(1)}, u32[]{:S(2)}, u32[]{:S(2)}) collective-permute-start(bf16[64,1024]{1,0:T(8,128)(2,1)S(1)} %coadd.1.refs_3_), channel_id=1, source_target_pairs={{0,192},{32,224},{64,0},{96,32},{128,64},{160,96},{192,128},{224,1... | collective-permute-start | bytes 393224 | tf_op jit(solution)/shard_map/ppermute | solution.py:435
  49.5 2.2 %collective-permute-start.8 = (bf16[64,1024]{1,0:T(8,128)(2,1)S(1)}, bf16[64,1024]{1,0:T(8,128)(2,1)S(1)}, u32[]{:S(2)}, u32[]{:S(2)}) collective-permute-start(bf16[64,1024]{1,0:T(8,128)(2,1)S(1)} %coadd.1.refs_3_), channel_id=1, source_target_pairs={{0,32},{32,0},{64,96},{96,64},{128,160},{160,128},{192,224},{224,1... | collective-permute-start | bytes 393224 | tf_op jit(solution)/shard_map/ppermute | solution.py:443
  51.8 0.8 %difference_near.1 = (f32[512,1024]{1,0:T(8,128)}, f32[512,1024]{1,0:T(8,128)}) custom-call(f32[512,512]{1,0:T(8,128)S(1)} %get-tuple-element.50.refs_0_, f32[256,512]{1,0:T(8,128)S(1)} %get-tuple-element.57.refs_1_, f32[256,512]{1,0:T(8,128)S(1)} %get-tuple-element.58.refs_2_, bf16[64,1024]{1,0:T(8,128)(2,1)S(1)} %coadd.1.refs_3_), custom_call_target="tpu_custom_call" | custom-call | flops 65536 | bytes 1048576 | tf_op jit(solution)/shard_map/difference_near/pallas_call | solution.py:401
  52.6 0.0 collective-permute-done.13.refs_5_
  52.6 1.7 %collective-permute-start.14 = (bf16[64,1024]{1,0:T(8,128)(2,1)S(1)}, bf16[64,1024]{1,0:T(8,128)(2,1)S(1)}, u32[]{:S(2)}, u32[]{:S(2)}) collective-permute-start(bf16[64,1024]{1,0:T(8,128)(2,1)S(1)} %collective-permute-done.13.refs_5_), channel_id=1, source_target_pairs={{0,32},{32,0},{64,96},{96,64},{128,160},{160,128},{192,224},{224,1... | collective-permute-start | bytes 393224 | tf_op jit(solution)/shard_map/ppermute | solution.py:443
  54.4 0.8 %collective-permute-done.9.refs_3_ = bf16[64,1024]{1,0:T(8,128)(2,1)S(1)} collective-permute-done((bf16[64,1024]{1,0:T(8,128)(2,1)S(1)}, bf16[64,1024]{1,0:T(8,128)(2,1)S(1)}, u32[]{:S(2)}, u32[]{:S(2)}) %collective-permute-start.9) | collective-permute-done | bytes 131104 | tf_op jit(solution)/shard_map/ppermute | solution.py:435
  55.2 1.0 %collective-permute-start.10 = (bf16[64,1024]{1,0:T(8,128)(2,1)S(1)}, bf16[64,1024]{1,0:T(8,128)(2,1)S(1)}, u32[]{:S(2)}, u32[]{:S(2)}) collective-permute-start(bf16[64,1024]{1,0:T(8,128)(2,1)S(1)} %collective-permute-done.9.refs_3_), channel_id=1, source_target_pairs={{0,32},{32,0},{64,96},{96,64},{128,160},{160,128},{192,224},{224,1... | collective-permute-start | bytes 393224 | tf_op jit(solution)/shard_map/ppermute | solution.py:443
  56.1 0.0 collective-permute-done.11.refs_4_
  56.1 0.1 collective-permute-start.12
  56.2 1.2 %difference_own.1 = (f32[512,1024]{1,0:T(8,128)}, f32[512,1024]{1,0:T(8,128)}) custom-call(f32[512,512]{1,0:T(8,128)S(1)} %get-tuple-element.50.refs_0_, f32[256,512]{1,0:T(8,128)S(1)} %get-tuple-element.57.refs_1_, f32[256,512]{1,0:T(8,128)S(1)} %get-tuple-element.58.refs_2_, ...), custom_call_target="tpu_custom_call", output_to_operand_aliasing={{0}: (6, {}), {1}: (7, {})} | custom-call | flops 196608 | bytes 67108864 | tf_op jit(solution)/shard_map/difference_own/pallas_call | solution.py:401
  57.4 0.0 collective-permute-done.8.refs_3_
  57.4 0.0 collective-permute-done.14.refs_6_
  57.4 0.0 collective-permute-done.10.refs_4_
  57.4 0.0 collective-permute-done.12.refs_5_
  57.5 1.4 %difference_other.1 = (f32[512,1024]{1,0:T(8,128)}, f32[512,1024]{1,0:T(8,128)}) custom-call(f32[512,512]{1,0:T(8,128)S(1)} %get-tuple-element.50.refs_0_, f32[256,512]{1,0:T(8,128)S(1)} %get-tuple-element.57.refs_1_, f32[256,512]{1,0:T(8,128)S(1)} %get-tuple-element.58.refs_2_, ...), custom_call_target="tpu_custom_call", output_to_operand_aliasing={{0}: (7, {}), {1}: (8, {})} | custom-call | flops 262144 | bytes 3145728 | tf_op jit(solution)/shard_map/difference_other/pallas_call | solution.py:401
Async XLA Ops:
  1.3 8.9 %copy-start.1 = (f32[16,128]{1,0:T(8,128)S(1)}, f32[16,128]{1,0:T(8,128)}, u32[]{:S(2)}) copy-start(f32[16,128]{1,0:T(8,128)} %constant.5.clone.factors_ref) | copy-start | bytes 24580
  1.3 8.9 %copy-start.2 = (f32[1,31]{1,0:T(1,128)S(1)}, f32[1,31]{1,0:T(1,128)}, u32[]{:S(2)}) copy-start(f32[1,31]{1,0:T(1,128)} %coef_ref.1) | copy-start | bytes 376
  6.0 18.3 %collective-permute-start = (bf16[576,256]{1,0:T(8,128)(2,1)S(1)}, bf16[576,256]{1,0:T(8,128)(2,1)S(1)}, u32[]{:S(2)}, u32[]{:S(2)}) collective-permute-start(bf16[576,256]{1,0:T(8,128)(2,1)S(1)} %get-tuple-element.51), channel_id=1, source_target_pairs={{0,1},{1,2},{2,3},{3,4},{4,5},{5,6},{6,7},{7,8},{8,9},{9,10},{10,1... | collective-permute-start | bytes 884744 | tf_op jit(solution)/shard_map/ppermute | solution.py:435
  8.6 18.8 %collective-permute-start.1 = (bf16[480,256]{1,0:T(8,128)(2,1)S(1)}, bf16[480,256]{1,0:T(8,128)(2,1)S(1)}, u32[]{:S(2)}, u32[]{:S(2)}) collective-permute-start(bf16[480,256]{1,0:T(8,128)(2,1)S(1)} %get-tuple-element.52), channel_id=1, source_target_pairs={{0,1},{1,2},{2,3},{3,4},{4,5},{5,6},{6,7},{7,8},{8,9},{9,10},{10,1... | collective-permute-start | bytes 737288 | tf_op jit(solution)/shard_map/ppermute | solution.py:435
  10.2 9.5 %copy-start = (bf16[128,1920]{1,0:T(8,128)(2,1)S(1)}, bf16[128,1920]{1,0:T(8,128)(2,1)}, u32[]{:S(2)}) copy-start(bf16[128,1920]{1,0:T(8,128)(2,1)} %constant.4.clone.band_ref) | copy-start | bytes 1474564
  14.8 9.5 %collective-permute-start.2 = (bf16[32,512]{1,0:T(8,128)(2,1)S(1)}, bf16[32,512]{1,0:T(8,128)(2,1)S(1)}, u32[]{:S(2)}, u32[]{:S(2)}) collective-permute-start(bf16[32,512]{1,0:T(8,128)(2,1)S(1)} %get-tuple-element.53), channel_id=1, source_target_pairs={{0,31},{1,0},{2,1},{3,2},{4,3},{5,4},{6,5},{7,6},{8,7},{9,8},{10,9... | collective-permute-start | bytes 98312 | tf_op jit(solution)/shard_map/ppermute | solution.py:435
  23.3 6.7 %collective-permute-start.3 = (bf16[256,1280]{1,0:T(8,128)(2,1)S(1)}, bf16[256,1280]{1,0:T(8,128)(2,1)S(1)}, u32[]{:S(2)}, u32[]{:S(2)}) collective-permute-start(bf16[256,1280]{1,0:T(8,128)(2,1)S(1)} %get-tuple-element.60), channel_id=1, source_target_pairs={{0,32},{32,0},{64,96},{96,64},{128,160},{160,128},{192,224},{224,1... | collective-permute-start | bytes 1966088 | tf_op jit(solution)/shard_map/ppermute | solution.py:443
  27.1 2.9 %collective-permute-start.4 = (bf16[256,768]{1,0:T(8,128)(2,1)S(1)}, bf16[256,768]{1,0:T(8,128)(2,1)S(1)}, u32[]{:S(2)}, u32[]{:S(2)}) collective-permute-start(bf16[256,768]{1,0:T(8,128)(2,1)S(1)} %get-tuple-element.62), channel_id=1, source_target_pairs={{0,32},{32,0},{64,96},{96,64},{128,160},{160,128},{192,224},{224,1... | collective-permute-start | bytes 1179656 | tf_op jit(solution)/shard_map/ppermute | solution.py:443
  30.2 8.6 %collective-permute-start.5 = (bf16[64,2048]{1,0:T(8,128)(2,1)S(1)}, bf16[64,2048]{1,0:T(8,128)(2,1)S(1)}, u32[]{:S(2)}, u32[]{:S(2)}) collective-permute-start(bf16[64,2048]{1,0:T(8,128)(2,1)S(1)} %get-tuple-element.64), channel_id=1, source_target_pairs={{0,128},{32,160},{64,192},{96,224},{128,0},{160,32},{192,64},{224,... | collective-permute-start | bytes 786440 | tf_op jit(solution)/shard_map/ppermute | solution.py:435
  33.1 12.6 %collective-permute-start.6 = (bf16[64,2048]{1,0:T(8,128)(2,1)S(1)}, bf16[64,2048]{1,0:T(8,128)(2,1)S(1)}, u32[]{:S(2)}, u32[]{:S(2)}) collective-permute-start(bf16[64,2048]{1,0:T(8,128)(2,1)S(1)} %get-tuple-element.65), channel_id=1, source_target_pairs={{0,64},{32,96},{64,128},{96,160},{128,192},{160,224},{192,0},{224,... | collective-permute-start | bytes 786440 | tf_op jit(solution)/shard_map/ppermute | solution.py:435
  33.4 12.3 %collective-permute-start.7 = (bf16[64,2048]{1,0:T(8,128)(2,1)S(1)}, bf16[64,2048]{1,0:T(8,128)(2,1)S(1)}, u32[]{:S(2)}, u32[]{:S(2)}) collective-permute-start(bf16[64,2048]{1,0:T(8,128)(2,1)S(1)} %get-tuple-element.66), channel_id=1, source_target_pairs={{0,192},{32,224},{64,0},{96,32},{128,64},{160,96},{192,128},{224,1... | collective-permute-start | bytes 786440 | tf_op jit(solution)/shard_map/ppermute | solution.py:435
  45.8 6.8 %collective-permute-start.13 = (bf16[64,1024]{1,0:T(8,128)(2,1)S(1)}, bf16[64,1024]{1,0:T(8,128)(2,1)S(1)}, u32[]{:S(2)}, u32[]{:S(2)}) collective-permute-start(bf16[64,1024]{1,0:T(8,128)(2,1)S(1)} %coadd.1.refs_3_), channel_id=1, source_target_pairs={{0,128},{32,160},{64,192},{96,224},{128,0},{160,32},{192,64},{224,... | collective-permute-start | bytes 393224 | tf_op jit(solution)/shard_map/ppermute | solution.py:435
  46.9 8.3 %collective-permute-start.9 = (bf16[64,1024]{1,0:T(8,128)(2,1)S(1)}, bf16[64,1024]{1,0:T(8,128)(2,1)S(1)}, u32[]{:S(2)}, u32[]{:S(2)}) collective-permute-start(bf16[64,1024]{1,0:T(8,128)(2,1)S(1)} %coadd.1.refs_3_), channel_id=1, source_target_pairs={{0,64},{32,96},{64,128},{96,160},{128,192},{160,224},{192,0},{224,... | collective-permute-start | bytes 393224 | tf_op jit(solution)/shard_map/ppermute | solution.py:435
  48.9 7.2 %collective-permute-start.11 = (bf16[64,1024]{1,0:T(8,128)(2,1)S(1)}, bf16[64,1024]{1,0:T(8,128)(2,1)S(1)}, u32[]{:S(2)}, u32[]{:S(2)}) collective-permute-start(bf16[64,1024]{1,0:T(8,128)(2,1)S(1)} %coadd.1.refs_3_), channel_id=1, source_target_pairs={{0,192},{32,224},{64,0},{96,32},{128,64},{160,96},{192,128},{224,1... | collective-permute-start | bytes 393224 | tf_op jit(solution)/shard_map/ppermute | solution.py:435
  49.5 7.9 %collective-permute-start.8 = (bf16[64,1024]{1,0:T(8,128)(2,1)S(1)}, bf16[64,1024]{1,0:T(8,128)(2,1)S(1)}, u32[]{:S(2)}, u32[]{:S(2)}) collective-permute-start(bf16[64,1024]{1,0:T(8,128)(2,1)S(1)} %coadd.1.refs_3_), channel_id=1, source_target_pairs={{0,32},{32,0},{64,96},{96,64},{128,160},{160,128},{192,224},{224,1... | collective-permute-start | bytes 393224 | tf_op jit(solution)/shard_map/ppermute | solution.py:443
  52.6 4.8 %collective-permute-start.14 = (bf16[64,1024]{1,0:T(8,128)(2,1)S(1)}, bf16[64,1024]{1,0:T(8,128)(2,1)S(1)}, u32[]{:S(2)}, u32[]{:S(2)}) collective-permute-start(bf16[64,1024]{1,0:T(8,128)(2,1)S(1)} %collective-permute-done.13.refs_5_), channel_id=1, source_target_pairs={{0,32},{32,0},{64,96},{96,64},{128,160},{160,128},{192,224},{224,1... | collective-permute-start | bytes 393224 | tf_op jit(solution)/shard_map/ppermute | solution.py:443
  55.2 2.3 %collective-permute-start.10 = (bf16[64,1024]{1,0:T(8,128)(2,1)S(1)}, bf16[64,1024]{1,0:T(8,128)(2,1)S(1)}, u32[]{:S(2)}, u32[]{:S(2)}) collective-permute-start(bf16[64,1024]{1,0:T(8,128)(2,1)S(1)} %collective-permute-done.9.refs_3_), channel_id=1, source_target_pairs={{0,32},{32,0},{64,96},{96,64},{128,160},{160,128},{192,224},{224,1... | collective-permute-start | bytes 393224 | tf_op jit(solution)/shard_map/ppermute | solution.py:443
  56.1 1.3 %collective-permute-start.12 = (bf16[64,1024]{1,0:T(8,128)(2,1)S(1)}, bf16[64,1024]{1,0:T(8,128)(2,1)S(1)}, u32[]{:S(2)}, u32[]{:S(2)}) collective-permute-start(bf16[64,1024]{1,0:T(8,128)(2,1)S(1)} %collective-permute-done.11.refs_4_), channel_id=1, source_target_pairs={{0,32},{32,0},{64,96},{96,64},{128,160},{160,128},{192,224},{224,1... | collective-permute-start | bytes 393224 | tf_op jit(solution)/shard_map/ppermute | solution.py:443

commit v5 on v4

--- a/solution.py
+++ b/solution.py
@@ -353,10 +353,10 @@
     )
 
 
-def pair_kernel(keep_ref, got_ref, keep2_ref, got2_ref, own_ref, two_ref, one_ref, three_ref):
+def pair_kernel(keep_ref, got_ref, keep2_ref, got2_ref, own_ref, two_ref, three_ref, one_ref):
     chip = lax.axis_index("visit") // 2
     width = keep_ref.shape[1]
-    for ahead, out_ref in ((0, own_ref), (2, two_ref), (1, one_ref), (3, three_ref)):
+    for ahead, out_ref in ((0, own_ref), (2, two_ref), (3, three_ref), (1, one_ref)):
         rows = pl.ds(pl.multiple_of(((chip + ahead) % 4) * PIECE, PIECE), PIECE)
         first = keep_ref[rows, :].astype(F32) + got_ref[rows, :].astype(F32)
         second = keep2_ref[rows, :].astype(F32) + got2_ref[rows, :].astype(F32)
@@ -555,7 +555,7 @@
         3 << 20,
         "pair_sum",
     )(*inner_sum, keep, partner(give))
-    others = [shifted(x, "visit", 2 * ahead) for ahead, x in zip((2, 1, 3), others)]
+    others = [shifted(x, "visit", 2 * ahead) for ahead, x in zip((2, 3, 1), others)]
     (piece,) = call(
         coadd_kernel, [((PIECE, COLS), BF16)], [], [VMEM_SPEC] * 4, 8 * PIECE * COLS, 2 << 20, "coadd"
     )(own_piece, *others)

time: 59.1 us -> 59.2 us (level)
  waiting for transfers between devices: 10.8 us -> 12 us
  starting transfers between devices: 24.7 us -> 23.6 us
    ppermute x6, starting transfers between devices: 6.37 us -> 4.29 us  [partner(): lax.ppermute(x, 'visit', [(i, i ^ 1) for i in range(lax.axis_size('visit'...]
    ppermute x9, waiting for transfers between devices: 10.7 us -> 11.9 us  [shifted(): return lax.ppermute(x, axis, [(i, (i + by) % size) for i in range(size)])]
    ppermute x9, starting transfers between devices: 18.4 us -> 19.3 us  [shifted(): return lax.ppermute(x, axis, [(i, (i + by) % size) for i in range(size)])]
  transfers between devices with their start and end apart: 15 -> 15, of which waited for: 3 -> 5; matrix products, arithmetic and copies ran while one was open for 0% -> 0% of each run, Pallas kernels for 26% -> 26%
where the time goes in v5:
time: 59.2 us
  starting transfers between devices  23.6 us (40%)
  Pallas kernels  21.9 us (37%)
  waiting for transfers between devices  12 us (20%)
  between operations  1.58 us (3%)
    ppermute x9, starting transfers between devices, shifted(): return lax.ppermute(x, axis, [(i, (i + by) % size) for i in range(size)])  19.3 us
    ppermute x9, waiting for transfers between devices, shifted(): return lax.ppermute(x, axis, [(i, (i + by) % size) for i in range(size)])  11.9 us
    pallas_call x1, Pallas kernels, per_device(): call(edge_kernel, [((2 * REACH + 32, EDGE), BF16), ((2 * (ROWS - REACH),...  4.73 us
    pallas_call x1, Pallas kernels, per_device(): call(middle_kernel, [((ROWS, COLS - EDGE + LANES), BF16), ((ROWS, COLS -...  4.57 us
    ppermute x6, starting transfers between devices, partner(): lax.ppermute(x, 'visit', [(i, i ^ 1) for i in range(lax.axis_size('visit'...  4.29 us
    pallas_call x1, Pallas kernels, per_device(): call(inner_kernel, [((ROWS, 4 * LANES), F32), ((ROWS // 2, inner_width),...  3.51 us
    pallas_call x3, Pallas kernels, finish(): call(functools.partial(final_kernel, places), [((ROWS, COLS), F32), ((ROW...  3.45 us
    pallas_call x1, Pallas kernels, per_device(): call(given_kernel, half_outs + [((ROWS, LANES), F32)] * 2, half_scratch +...  2.72 us
  transfers between devices with their start and end apart: 15, of which 5 were waited for; matrix products, arithmetic and copies ran while one was open for 0% of the time, Pallas kernels for 26%

profile of v5, /device:TPU:1, one launch (start us, length us, event | category | flops | bytes accessed | tf_op | source)
XLA Modules:
  0.0 59.2 jit_solution(10879098212341643351)
XLA Ops:
  1.3 0.0 copy-start.1
  1.3 0.0 copy-start.2
  1.3 4.7 %edge_columns.1 = (bf16[576,256]{1,0:T(8,128)(2,1)S(1)}, bf16[480,256]{1,0:T(8,128)(2,1)S(1)}, f32[1024,256]{1,0:T(8,128)S(1)}, bf16[512,128]{1,0:T(8,128)(2,1)S...) custom-call(s32[1,1]{1,0:T(1,128)S(6)} %copy.20.offset_ref, ...), custom_call_target="tpu_custom_call" | custom-call | flops 1207959552 | bytes 8388608 | tf_op jit(solution)/shard_map/edge_columns/pallas_call | solution.py:460
  6.0 2.6 %collective-permute-start = (bf16[576,256]{1,0:T(8,128)(2,1)S(1)}, bf16[576,256]{1,0:T(8,128)(2,1)S(1)}, u32[]{:S(2)}, u32[]{:S(2)}) collective-permute-start(bf16[576,256]{1,0:T(8,128)(2,1)S(1)} %get-tuple-element.51), channel_id=1, source_target_pairs={{0,1},{1,2},{2,3},{3,4},{4,5},{5,6},{6,7},{7,8},{8,9},{9,10},{10,1... | collective-permute-start | bytes 884744 | tf_op jit(solution)/shard_map/ppermute | solution.py:435
  8.6 1.6 %collective-permute-start.1 = (bf16[480,256]{1,0:T(8,128)(2,1)S(1)}, bf16[480,256]{1,0:T(8,128)(2,1)S(1)}, u32[]{:S(2)}, u32[]{:S(2)}) collective-permute-start(bf16[480,256]{1,0:T(8,128)(2,1)S(1)} %get-tuple-element.52), channel_id=1, source_target_pairs={{0,1},{1,2},{2,3},{3,4},{4,5},{5,6},{6,7},{7,8},{8,9},{9,10},{10,1... | collective-permute-start | bytes 737288 | tf_op jit(solution)/shard_map/ppermute | solution.py:435
  10.2 0.0 copy-done.1
  10.2 0.0 copy-done.2
  10.2 0.0 copy-start
  10.2 4.6 %middle_columns.1 = (bf16[512,896]{1,0:T(8,128)(2,1)S(1)}, bf16[512,768]{1,0:T(8,128)(2,1)S(1)}, bf16[256,1536]{1,0:T(8,128)(2,1)S(1)}, bf16[32,512]{1,0:T(8,128)(2,1)S(1)}, f32[32,512]{1,0:T(8,128)S(1)}) custom-call(s32[1,1]{1,0:T(1,128)S(6)} %copy.20.offset_ref, f32[1,31]{1,0:T(1,128)S(1)} %copy-done.2, bf16[512,1024]{1,0:T(8,128)(2,1)S(1)} %get-tuple-element.39.low_ref, ...), custom_call_target="tpu_custom_call" | custom-call | flops 1048576 | bytes 1024 | tf_op jit(solution)/shard_map/middle_columns/pallas_call | solution.py:496
  14.8 5.0 %collective-permute-start.2 = (bf16[32,512]{1,0:T(8,128)(2,1)S(1)}, bf16[32,512]{1,0:T(8,128)(2,1)S(1)}, u32[]{:S(2)}, u32[]{:S(2)}) collective-permute-start(bf16[32,512]{1,0:T(8,128)(2,1)S(1)} %get-tuple-element.53), channel_id=1, source_target_pairs={{0,31},{1,0},{2,1},{3,2},{4,3},{5,4},{6,5},{7,6},{8,7},{9,8},{10,9... | collective-permute-start | bytes 98312 | tf_op jit(solution)/shard_map/ppermute | solution.py:435
  19.8 0.0 copy-done
  19.8 3.5 %inner_match.1 = (f32[512,512]{1,0:T(8,128)S(1)}, bf16[256,1280]{1,0:T(8,128)(2,1)S(1)}, bf16[256,1280]{1,0:T(8,128)(2,1)S(1)}) custom-call(bf16[512,896]{1,0:T(8,128)(2,1)S(1)} %get-tuple-element.47.patch_ref, bf16[512,768]{1,0:T(8,128)(2,1)S(1)} %get-tuple-element.48.weight_ref, bf16[256,1536]{1,0:T(8,128)(2,1)S(1)} %get-tuple-element.49.taps_ref, ...), custom_call_target="tpu_custom_call" | custom-call | flops 1048576 | bytes 1024 | tf_op jit(solution)/shard_map/inner_match/pallas_call | solution.py:514
  23.3 1.1 %collective-permute-start.3 = (bf16[256,1280]{1,0:T(8,128)(2,1)S(1)}, bf16[256,1280]{1,0:T(8,128)(2,1)S(1)}, u32[]{:S(2)}, u32[]{:S(2)}) collective-permute-start(bf16[256,1280]{1,0:T(8,128)(2,1)S(1)} %get-tuple-element.60), channel_id=1, source_target_pairs={{0,32},{32,0},{64,96},{96,64},{128,160},{160,128},{192,224},{224,1... | collective-permute-start | bytes 1966088 | tf_op jit(solution)/shard_map/ppermute | solution.py:443
  24.3 0.0 collective-permute-done.2.ahead_ref
  24.3 0.0 collective-permute-done.got_ref
  24.3 2.7 %given_match.1 = (f32[256,512]{1,0:T(8,128)S(1)}, bf16[256,768]{1,0:T(8,128)(2,1)S(1)}, f32[512,128]{1,0:T(8,128)S(1)}, f32[512,128]{1,0:T(8,128)S(1)}) custom-call(s32[1,1]{1,0:T(1,128)S(6)} %copy.20.offset_ref, bf16[576,256]{1,0:T(8,128)(2,1)S(1)} %collective-permute-done.got_ref, bf16[32,512]{1,0:T(8,128)(2,1)S(1)} %collective-permute-done.2.ahead_ref, ...), custom_call_target="tpu_custom_call" | custom-call | flops 1048576 | bytes 1024 | tf_op jit(solution)/shard_map/given_match/pallas_call | solution.py:531
  27.1 0.3 collective-permute-start.4
  27.4 0.0 collective-permute-done.1.rest_ref
  27.4 2.6 %kept_match.1 = (f32[256,512]{1,0:T(8,128)S(1)}, bf16[256,768]{1,0:T(8,128)(2,1)S(1)}) custom-call(s32[1,1]{1,0:T(1,128)S(6)} %copy.20.offset_ref, bf16[576,256]{1,0:T(8,128)(2,1)S(1)} %collective-permute-done.got_ref, bf16[480,256]{1,0:T(8,128)(2,1)S(1)} %collective-permute-done.1.rest_ref, f32[1024,256]{1,0:T(8,128)S(1)} %get-tuple-element.46.edge_ref, ...), custom_call_target="tpu_custom_call" | custom-call | flops 20937965568 | bytes 67108864 | tf_op jit(solution)/shard_map/kept_match/pallas_call | solution.py:540
  30.0 0.0 collective-permute-done.3.got_ref
  30.0 0.0 collective-permute-done.4.got2_ref
  30.0 0.3 pair_sum.1
  30.2 2.8 %collective-permute-start.5 = (bf16[64,2048]{1,0:T(8,128)(2,1)S(1)}, bf16[64,2048]{1,0:T(8,128)(2,1)S(1)}, u32[]{:S(2)}, u32[]{:S(2)}) collective-permute-start(bf16[64,2048]{1,0:T(8,128)(2,1)S(1)} %get-tuple-element.64), channel_id=1, source_target_pairs={{0,128},{32,160},{64,192},{96,224},{128,0},{160,32},{192,64},{224,... | collective-permute-start | bytes 786440 | tf_op jit(solution)/shard_map/ppermute | solution.py:435
  33.1 0.9 %collective-permute-start.6 = (bf16[64,2048]{1,0:T(8,128)(2,1)S(1)}, bf16[64,2048]{1,0:T(8,128)(2,1)S(1)}, u32[]{:S(2)}, u32[]{:S(2)}) collective-permute-start(bf16[64,2048]{1,0:T(8,128)(2,1)S(1)} %get-tuple-element.65), channel_id=1, source_target_pairs={{0,192},{32,224},{64,0},{96,32},{128,64},{160,96},{192,128},{224,1... | collective-permute-start | bytes 786440 | tf_op jit(solution)/shard_map/ppermute | solution.py:435
  33.9 0.6 %collective-permute-start.7 = (bf16[64,2048]{1,0:T(8,128)(2,1)S(1)}, bf16[64,2048]{1,0:T(8,128)(2,1)S(1)}, u32[]{:S(2)}, u32[]{:S(2)}) collective-permute-start(bf16[64,2048]{1,0:T(8,128)(2,1)S(1)} %get-tuple-element.66), channel_id=1, source_target_pairs={{0,64},{32,96},{64,128},{96,160},{128,192},{160,224},{192,0},{224,... | collective-permute-start | bytes 786440 | tf_op jit(solution)/shard_map/ppermute | solution.py:435
  34.5 4.3 %collective-permute-done.5.one_ref = bf16[64,2048]{1,0:T(8,128)(2,1)S(1)} collective-permute-done((bf16[64,2048]{1,0:T(8,128)(2,1)S(1)}, bf16[64,2048]{1,0:T(8,128)(2,1)S(1)}, u32[]{:S(2)}, u32[]{:S(2)}) %collective-permute-start.5) | collective-permute-done | bytes 262176 | tf_op jit(solution)/shard_map/ppermute | solution.py:435
  38.8 5.9 %collective-permute-done.6.two_ref = bf16[64,2048]{1,0:T(8,128)(2,1)S(1)} collective-permute-done((bf16[64,2048]{1,0:T(8,128)(2,1)S(1)}, bf16[64,2048]{1,0:T(8,128)(2,1)S(1)}, u32[]{:S(2)}, u32[]{:S(2)}) %collective-permute-start.6) | collective-permute-done | bytes 262176 | tf_op jit(solution)/shard_map/ppermute | solution.py:435
  44.7 0.6 collective-permute-done.7.three_ref
  45.3 0.1 coadd.1.refs_3_
  45.4 3.2 %collective-permute-start.13 = (bf16[64,1024]{1,0:T(8,128)(2,1)S(1)}, bf16[64,1024]{1,0:T(8,128)(2,1)S(1)}, u32[]{:S(2)}, u32[]{:S(2)}) collective-permute-start(bf16[64,1024]{1,0:T(8,128)(2,1)S(1)} %coadd.1.refs_3_), channel_id=1, source_target_pairs={{0,128},{32,160},{64,192},{96,224},{128,0},{160,32},{192,64},{224,... | collective-permute-start | bytes 393224 | tf_op jit(solution)/shard_map/ppermute | solution.py:435
  48.6 0.3 collective-permute-start.9
  49.0 2.4 %collective-permute-start.11 = (bf16[64,1024]{1,0:T(8,128)(2,1)S(1)}, bf16[64,1024]{1,0:T(8,128)(2,1)S(1)}, u32[]{:S(2)}, u32[]{:S(2)}) collective-permute-start(bf16[64,1024]{1,0:T(8,128)(2,1)S(1)} %coadd.1.refs_3_), channel_id=1, source_target_pairs={{0,192},{32,224},{64,0},{96,32},{128,64},{160,96},{192,128},{224,1... | collective-permute-start | bytes 393224 | tf_op jit(solution)/shard_map/ppermute | solution.py:435
  51.3 1.3 %collective-permute-start.8 = (bf16[64,1024]{1,0:T(8,128)(2,1)S(1)}, bf16[64,1024]{1,0:T(8,128)(2,1)S(1)}, u32[]{:S(2)}, u32[]{:S(2)}) collective-permute-start(bf16[64,1024]{1,0:T(8,128)(2,1)S(1)} %coadd.1.refs_3_), channel_id=1, source_target_pairs={{0,32},{32,0},{64,96},{96,64},{128,160},{160,128},{192,224},{224,1... | collective-permute-start | bytes 393224 | tf_op jit(solution)/shard_map/ppermute | solution.py:443
  52.6 0.8 %difference_near.1 = (f32[512,1024]{1,0:T(8,128)}, f32[512,1024]{1,0:T(8,128)}) custom-call(f32[512,512]{1,0:T(8,128)S(1)} %get-tuple-element.50.refs_0_, f32[256,512]{1,0:T(8,128)S(1)} %get-tuple-element.57.refs_1_, f32[256,512]{1,0:T(8,128)S(1)} %get-tuple-element.58.refs_2_, bf16[64,1024]{1,0:T(8,128)(2,1)S(1)} %coadd.1.refs_3_), custom_call_target="tpu_custom_call" | custom-call | flops 65536 | bytes 1048576 | tf_op jit(solution)/shard_map/difference_near/pallas_call | solution.py:401
  53.5 0.0 collective-permute-done.13.refs_5_
  53.5 0.4 collective-permute-start.14
  53.9 1.1 %collective-permute-done.9.refs_3_ = bf16[64,1024]{1,0:T(8,128)(2,1)S(1)} collective-permute-done((bf16[64,1024]{1,0:T(8,128)(2,1)S(1)}, bf16[64,1024]{1,0:T(8,128)(2,1)S(1)}, u32[]{:S(2)}, u32[]{:S(2)}) %collective-permute-start.9) | collective-permute-done | bytes 131104 | tf_op jit(solution)/shard_map/ppermute | solution.py:435
  55.0 1.2 %collective-permute-start.10 = (bf16[64,1024]{1,0:T(8,128)(2,1)S(1)}, bf16[64,1024]{1,0:T(8,128)(2,1)S(1)}, u32[]{:S(2)}, u32[]{:S(2)}) collective-permute-start(bf16[64,1024]{1,0:T(8,128)(2,1)S(1)} %collective-permute-done.9.refs_3_), channel_id=1, source_target_pairs={{0,32},{32,0},{64,96},{96,64},{128,160},{160,128},{192,224},{224,1... | collective-permute-start | bytes 393224 | tf_op jit(solution)/shard_map/ppermute | solution.py:443
  56.2 0.0 collective-permute-done.11.refs_4_
  56.2 0.0 collective-permute-start.12
  56.2 1.2 %difference_own.1 = (f32[512,1024]{1,0:T(8,128)}, f32[512,1024]{1,0:T(8,128)}) custom-call(f32[512,512]{1,0:T(8,128)S(1)} %get-tuple-element.50.refs_0_, f32[256,512]{1,0:T(8,128)S(1)} %get-tuple-element.57.refs_1_, f32[256,512]{1,0:T(8,128)S(1)} %get-tuple-element.58.refs_2_, ...), custom_call_target="tpu_custom_call", output_to_operand_aliasing={{0}: (6, {}), {1}: (7, {})} | custom-call | flops 196608 | bytes 67108864 | tf_op jit(solution)/shard_map/difference_own/pallas_call | solution.py:401
  57.5 0.0 collective-permute-done.8.refs_3_
  57.5 0.0 collective-permute-done.14.refs_6_
  57.5 0.0 collective-permute-done.10.refs_4_
  57.5 0.1 collective-permute-done.12.refs_5_
  57.6 1.4 %difference_other.1 = (f32[512,1024]{1,0:T(8,128)}, f32[512,1024]{1,0:T(8,128)}) custom-call(f32[512,512]{1,0:T(8,128)S(1)} %get-tuple-element.50.refs_0_, f32[256,512]{1,0:T(8,128)S(1)} %get-tuple-element.57.refs_1_, f32[256,512]{1,0:T(8,128)S(1)} %get-tuple-element.58.refs_2_, ...), custom_call_target="tpu_custom_call", output_to_operand_aliasing={{0}: (7, {}), {1}: (8, {})} | custom-call | flops 262144 | bytes 3145728 | tf_op jit(solution)/shard_map/difference_other/pallas_call | solution.py:401
Async XLA Ops:
  1.3 8.9 %copy-start.1 = (f32[16,128]{1,0:T(8,128)S(1)}, f32[16,128]{1,0:T(8,128)}, u32[]{:S(2)}) copy-start(f32[16,128]{1,0:T(8,128)} %constant.5.clone.factors_ref) | copy-start | bytes 24580
  1.3 8.9 %copy-start.2 = (f32[1,31]{1,0:T(1,128)S(1)}, f32[1,31]{1,0:T(1,128)}, u32[]{:S(2)}) copy-start(f32[1,31]{1,0:T(1,128)} %coef_ref.1) | copy-start | bytes 376
  6.0 18.3 %collective-permute-start = (bf16[576,256]{1,0:T(8,128)(2,1)S(1)}, bf16[576,256]{1,0:T(8,128)(2,1)S(1)}, u32[]{:S(2)}, u32[]{:S(2)}) collective-permute-start(bf16[576,256]{1,0:T(8,128)(2,1)S(1)} %get-tuple-element.51), channel_id=1, source_target_pairs={{0,1},{1,2},{2,3},{3,4},{4,5},{5,6},{6,7},{7,8},{8,9},{9,10},{10,1... | collective-permute-start | bytes 884744 | tf_op jit(solution)/shard_map/ppermute | solution.py:435
  8.6 18.8 %collective-permute-start.1 = (bf16[480,256]{1,0:T(8,128)(2,1)S(1)}, bf16[480,256]{1,0:T(8,128)(2,1)S(1)}, u32[]{:S(2)}, u32[]{:S(2)}) collective-permute-start(bf16[480,256]{1,0:T(8,128)(2,1)S(1)} %get-tuple-element.52), channel_id=1, source_target_pairs={{0,1},{1,2},{2,3},{3,4},{4,5},{5,6},{6,7},{7,8},{8,9},{9,10},{10,1... | collective-permute-start | bytes 737288 | tf_op jit(solution)/shard_map/ppermute | solution.py:435
  10.2 9.5 %copy-start = (bf16[128,1920]{1,0:T(8,128)(2,1)S(1)}, bf16[128,1920]{1,0:T(8,128)(2,1)}, u32[]{:S(2)}) copy-start(bf16[128,1920]{1,0:T(8,128)(2,1)} %constant.4.clone.band_ref) | copy-start | bytes 1474564
  14.8 9.5 %collective-permute-start.2 = (bf16[32,512]{1,0:T(8,128)(2,1)S(1)}, bf16[32,512]{1,0:T(8,128)(2,1)S(1)}, u32[]{:S(2)}, u32[]{:S(2)}) collective-permute-start(bf16[32,512]{1,0:T(8,128)(2,1)S(1)} %get-tuple-element.53), channel_id=1, source_target_pairs={{0,31},{1,0},{2,1},{3,2},{4,3},{5,4},{6,5},{7,6},{8,7},{9,8},{10,9... | collective-permute-start | bytes 98312 | tf_op jit(solution)/shard_map/ppermute | solution.py:435
  23.3 6.7 %collective-permute-start.3 = (bf16[256,1280]{1,0:T(8,128)(2,1)S(1)}, bf16[256,1280]{1,0:T(8,128)(2,1)S(1)}, u32[]{:S(2)}, u32[]{:S(2)}) collective-permute-start(bf16[256,1280]{1,0:T(8,128)(2,1)S(1)} %get-tuple-element.60), channel_id=1, source_target_pairs={{0,32},{32,0},{64,96},{96,64},{128,160},{160,128},{192,224},{224,1... | collective-permute-start | bytes 1966088 | tf_op jit(solution)/shard_map/ppermute | solution.py:443
  27.1 2.9 %collective-permute-start.4 = (bf16[256,768]{1,0:T(8,128)(2,1)S(1)}, bf16[256,768]{1,0:T(8,128)(2,1)S(1)}, u32[]{:S(2)}, u32[]{:S(2)}) collective-permute-start(bf16[256,768]{1,0:T(8,128)(2,1)S(1)} %get-tuple-element.62), channel_id=1, source_target_pairs={{0,32},{32,0},{64,96},{96,64},{128,160},{160,128},{192,224},{224,1... | collective-permute-start | bytes 1179656 | tf_op jit(solution)/shard_map/ppermute | solution.py:443
  30.2 8.6 %collective-permute-start.5 = (bf16[64,2048]{1,0:T(8,128)(2,1)S(1)}, bf16[64,2048]{1,0:T(8,128)(2,1)S(1)}, u32[]{:S(2)}, u32[]{:S(2)}) collective-permute-start(bf16[64,2048]{1,0:T(8,128)(2,1)S(1)} %get-tuple-element.64), channel_id=1, source_target_pairs={{0,128},{32,160},{64,192},{96,224},{128,0},{160,32},{192,64},{224,... | collective-permute-start | bytes 786440 | tf_op jit(solution)/shard_map/ppermute | solution.py:435
  33.1 11.7 %collective-permute-start.6 = (bf16[64,2048]{1,0:T(8,128)(2,1)S(1)}, bf16[64,2048]{1,0:T(8,128)(2,1)S(1)}, u32[]{:S(2)}, u32[]{:S(2)}) collective-permute-start(bf16[64,2048]{1,0:T(8,128)(2,1)S(1)} %get-tuple-element.65), channel_id=1, source_target_pairs={{0,192},{32,224},{64,0},{96,32},{128,64},{160,96},{192,128},{224,1... | collective-permute-start | bytes 786440 | tf_op jit(solution)/shard_map/ppermute | solution.py:435
  33.9 11.4 %collective-permute-start.7 = (bf16[64,2048]{1,0:T(8,128)(2,1)S(1)}, bf16[64,2048]{1,0:T(8,128)(2,1)S(1)}, u32[]{:S(2)}, u32[]{:S(2)}) collective-permute-start(bf16[64,2048]{1,0:T(8,128)(2,1)S(1)} %get-tuple-element.66), channel_id=1, source_target_pairs={{0,64},{32,96},{64,128},{96,160},{128,192},{160,224},{192,0},{224,... | collective-permute-start | bytes 786440 | tf_op jit(solution)/shard_map/ppermute | solution.py:435
  45.4 8.1 %collective-permute-start.13 = (bf16[64,1024]{1,0:T(8,128)(2,1)S(1)}, bf16[64,1024]{1,0:T(8,128)(2,1)S(1)}, u32[]{:S(2)}, u32[]{:S(2)}) collective-permute-start(bf16[64,1024]{1,0:T(8,128)(2,1)S(1)} %coadd.1.refs_3_), channel_id=1, source_target_pairs={{0,128},{32,160},{64,192},{96,224},{128,0},{160,32},{192,64},{224,... | collective-permute-start | bytes 393224 | tf_op jit(solution)/shard_map/ppermute | solution.py:435
  48.6 6.4 %collective-permute-start.9 = (bf16[64,1024]{1,0:T(8,128)(2,1)S(1)}, bf16[64,1024]{1,0:T(8,128)(2,1)S(1)}, u32[]{:S(2)}, u32[]{:S(2)}) collective-permute-start(bf16[64,1024]{1,0:T(8,128)(2,1)S(1)} %coadd.1.refs_3_), channel_id=1, source_target_pairs={{0,64},{32,96},{64,128},{96,160},{128,192},{160,224},{192,0},{224,... | collective-permute-start | bytes 393224 | tf_op jit(solution)/shard_map/ppermute | solution.py:435
  49.0 7.3 %collective-permute-start.11 = (bf16[64,1024]{1,0:T(8,128)(2,1)S(1)}, bf16[64,1024]{1,0:T(8,128)(2,1)S(1)}, u32[]{:S(2)}, u32[]{:S(2)}) collective-permute-start(bf16[64,1024]{1,0:T(8,128)(2,1)S(1)} %coadd.1.refs_3_), channel_id=1, source_target_pairs={{0,192},{32,224},{64,0},{96,32},{128,64},{160,96},{192,128},{224,1... | collective-permute-start | bytes 393224 | tf_op jit(solution)/shard_map/ppermute | solution.py:435
  51.3 6.2 %collective-permute-start.8 = (bf16[64,1024]{1,0:T(8,128)(2,1)S(1)}, bf16[64,1024]{1,0:T(8,128)(2,1)S(1)}, u32[]{:S(2)}, u32[]{:S(2)}) collective-permute-start(bf16[64,1024]{1,0:T(8,128)(2,1)S(1)} %coadd.1.refs_3_), channel_id=1, source_target_pairs={{0,32},{32,0},{64,96},{96,64},{128,160},{160,128},{192,224},{224,1... | collective-permute-start | bytes 393224 | tf_op jit(solution)/shard_map/ppermute | solution.py:443
  53.5 4.0 %collective-permute-start.14 = (bf16[64,1024]{1,0:T(8,128)(2,1)S(1)}, bf16[64,1024]{1,0:T(8,128)(2,1)S(1)}, u32[]{:S(2)}, u32[]{:S(2)}) collective-permute-start(bf16[64,1024]{1,0:T(8,128)(2,1)S(1)} %collective-permute-done.13.refs_5_), channel_id=1, source_target_pairs={{0,32},{32,0},{64,96},{96,64},{128,160},{160,128},{192,224},{224,1... | collective-permute-start | bytes 393224 | tf_op jit(solution)/shard_map/ppermute | solution.py:443
  55.0 2.4 %collective-permute-start.10 = (bf16[64,1024]{1,0:T(8,128)(2,1)S(1)}, bf16[64,1024]{1,0:T(8,128)(2,1)S(1)}, u32[]{:S(2)}, u32[]{:S(2)}) collective-permute-start(bf16[64,1024]{1,0:T(8,128)(2,1)S(1)} %collective-permute-done.9.refs_3_), channel_id=1, source_target_pairs={{0,32},{32,0},{64,96},{96,64},{128,160},{160,128},{192,224},{224,1... | collective-permute-start | bytes 393224 | tf_op jit(solution)/shard_map/ppermute | solution.py:443
  56.2 1.3 %collective-permute-start.12 = (bf16[64,1024]{1,0:T(8,128)(2,1)S(1)}, bf16[64,1024]{1,0:T(8,128)(2,1)S(1)}, u32[]{:S(2)}, u32[]{:S(2)}) collective-permute-start(bf16[64,1024]{1,0:T(8,128)(2,1)S(1)} %collective-permute-done.11.refs_4_), channel_id=1, source_target_pairs={{0,32},{32,0},{64,96},{96,64},{128,160},{160,128},{192,224},{224,1... | collective-permute-start | bytes 393224 | tf_op jit(solution)/shard_map/ppermute | solution.py:443

commit v6 on v4

--- a/solution.py
+++ b/solution.py
@@ -132,10 +132,7 @@
     for load in loads:
         load.start()
     shift = offset_ref[0, 0]
-    for load in loads[:2]:
-        load.wait()
-    build_rows(row_first_ref, row_taps_ref, flip_ref, rows_ref, rows2_ref)
-    for load in loads[2:4]:
+    for load in loads[:4]:
         load.wait()
     table_ref[...] = jnp.zeros_like(table_ref)
     for tap in range(TAPS):
@@ -146,9 +143,10 @@
     parts = jnp.concatenate([table[:, :EDGE], table[:, COLS - LANES :]], axis=1)
     build_cols(parts, 0, EDGE + LANES, cols_ref, cols2_ref)
     loads[4].wait()
+    loads[5].wait()
     low_ref[...] = held_ref[...].astype(BF16)
     across = dot(low_ref[...], cols_ref[...]).astype(BF16)
-    loads[5].wait()
+    build_rows(row_first_ref, row_taps_ref, flip_ref, rows_ref, rows2_ref)
     low2_ref[...] = held2_ref[...].astype(BF16)
     across2 = dot(low2_ref[...], cols2_ref[...]).astype(BF16)
     warped = dot(rows_ref[...], across)

time: 59.1 us -> 58.8 us (level)
  no operation moved by 1% of the time
where the time goes in v6:
time: 58.8 us; the launch traced here: 58.7 us
  starting transfers between devices  24.7 us (42%)
  Pallas kernels  21.6 us (37%)
  waiting for transfers between devices  10.8 us (18%)
  between operations  1.58 us (3%)
    ppermute x9, starting transfers between devices, shifted(): return lax.ppermute(x, axis, [(i, (i + by) % size) for i in range(size)])  18.4 us
    ppermute x9, waiting for transfers between devices, shifted(): return lax.ppermute(x, axis, [(i, (i + by) % size) for i in range(size)])  10.7 us
    ppermute x6, starting transfers between devices, partner(): lax.ppermute(x, 'visit', [(i, i ^ 1) for i in range(lax.axis_size('visit'...  6.35 us
    pallas_call x1, Pallas kernels, per_device(): call(middle_kernel, [((ROWS, COLS - EDGE + LANES), BF16), ((ROWS, COLS -...  4.57 us
    pallas_call x1, Pallas kernels, per_device(): call(edge_kernel, [((2 * REACH + 32, EDGE), BF16), ((2 * (ROWS - REACH),...  4.37 us
    pallas_call x1, Pallas kernels, per_device(): call(inner_kernel, [((ROWS, 4 * LANES), F32), ((ROWS // 2, inner_width),...  3.51 us
    pallas_call x3, Pallas kernels, finish(): call(functools.partial(final_kernel, places), [((ROWS, COLS), F32), ((ROW...  3.45 us
    pallas_call x1, Pallas kernels, per_device(): call(given_kernel, half_outs + [((ROWS, LANES), F32)] * 2, half_scratch +...  2.71 us
  transfers between devices with their start and end apart: 15, of which 3 were waited for; matrix products, arithmetic and copies ran while one was open for 0% of the time, Pallas kernels for 26%

profile of v6, /device:TPU:1, one launch (start us, length us, event | category | flops | bytes accessed | tf_op | source)
XLA Modules:
  0.0 58.7 jit_solution(14025182364098537041)
XLA Ops:
  1.3 0.0 copy-start.1
  1.3 0.0 copy-start.2
  1.3 4.4 %edge_columns.1 = (bf16[576,256]{1,0:T(8,128)(2,1)S(1)}, bf16[480,256]{1,0:T(8,128)(2,1)S(1)}, f32[1024,256]{1,0:T(8,128)S(1)}, bf16[512,128]{1,0:T(8,128)(2,1)S...) custom-call(s32[1,1]{1,0:T(1,128)S(6)} %copy.20.offset_ref, ...), custom_call_target="tpu_custom_call" | custom-call | flops 1207959552 | bytes 8388608 | tf_op jit(solution)/shard_map/edge_columns/pallas_call | solution.py:458
  5.7 2.5 %collective-permute-start = (bf16[576,256]{1,0:T(8,128)(2,1)S(1)}, bf16[576,256]{1,0:T(8,128)(2,1)S(1)}, u32[]{:S(2)}, u32[]{:S(2)}) collective-permute-start(bf16[576,256]{1,0:T(8,128)(2,1)S(1)} %get-tuple-element.51), channel_id=1, source_target_pairs={{0,1},{1,2},{2,3},{3,4},{4,5},{5,6},{6,7},{7,8},{8,9},{9,10},{10,1... | collective-permute-start | bytes 884744 | tf_op jit(solution)/shard_map/ppermute | solution.py:433
  8.2 1.6 %collective-permute-start.1 = (bf16[480,256]{1,0:T(8,128)(2,1)S(1)}, bf16[480,256]{1,0:T(8,128)(2,1)S(1)}, u32[]{:S(2)}, u32[]{:S(2)}) collective-permute-start(bf16[480,256]{1,0:T(8,128)(2,1)S(1)} %get-tuple-element.52), channel_id=1, source_target_pairs={{0,1},{1,2},{2,3},{3,4},{4,5},{5,6},{6,7},{7,8},{8,9},{9,10},{10,1... | collective-permute-start | bytes 737288 | tf_op jit(solution)/shard_map/ppermute | solution.py:433
  9.9 0.0 copy-done.1
  9.9 0.0 copy-done.2
  9.9 0.0 copy-start
  9.9 4.6 %middle_columns.1 = (bf16[512,896]{1,0:T(8,128)(2,1)S(1)}, bf16[512,768]{1,0:T(8,128)(2,1)S(1)}, bf16[256,1536]{1,0:T(8,128)(2,1)S(1)}, bf16[32,512]{1,0:T(8,128)(2,1)S(1)}, f32[32,512]{1,0:T(8,128)S(1)}) custom-call(s32[1,1]{1,0:T(1,128)S(6)} %copy.20.offset_ref, f32[1,31]{1,0:T(1,128)S(1)} %copy-done.2, bf16[512,1024]{1,0:T(8,128)(2,1)S(1)} %get-tuple-element.39.low_ref, ...), custom_call_target="tpu_custom_call" | custom-call | flops 1048576 | bytes 1024 | tf_op jit(solution)/shard_map/middle_columns/pallas_call | solution.py:494
  14.4 5.0 %collective-permute-start.2 = (bf16[32,512]{1,0:T(8,128)(2,1)S(1)}, bf16[32,512]{1,0:T(8,128)(2,1)S(1)}, u32[]{:S(2)}, u32[]{:S(2)}) collective-permute-start(bf16[32,512]{1,0:T(8,128)(2,1)S(1)} %get-tuple-element.53), channel_id=1, source_target_pairs={{0,31},{1,0},{2,1},{3,2},{4,3},{5,4},{6,5},{7,6},{8,7},{9,8},{10,9... | collective-permute-start | bytes 98312 | tf_op jit(solution)/shard_map/ppermute | solution.py:433
  19.4 0.0 copy-done
  19.4 3.5 %inner_match.1 = (f32[512,512]{1,0:T(8,128)S(1)}, bf16[256,1280]{1,0:T(8,128)(2,1)S(1)}, bf16[256,1280]{1,0:T(8,128)(2,1)S(1)}) custom-call(bf16[512,896]{1,0:T(8,128)(2,1)S(1)} %get-tuple-element.47.patch_ref, bf16[512,768]{1,0:T(8,128)(2,1)S(1)} %get-tuple-element.48.weight_ref, bf16[256,1536]{1,0:T(8,128)(2,1)S(1)} %get-tuple-element.49.taps_ref, ...), custom_call_target="tpu_custom_call" | custom-call | flops 1048576 | bytes 1024 | tf_op jit(solution)/shard_map/inner_match/pallas_call | solution.py:512
  22.9 1.0 %collective-permute-start.3 = (bf16[256,1280]{1,0:T(8,128)(2,1)S(1)}, bf16[256,1280]{1,0:T(8,128)(2,1)S(1)}, u32[]{:S(2)}, u32[]{:S(2)}) collective-permute-start(bf16[256,1280]{1,0:T(8,128)(2,1)S(1)} %get-tuple-element.60), channel_id=1, source_target_pairs={{0,32},{32,0},{64,96},{96,64},{128,160},{160,128},{192,224},{224,1... | collective-permute-start | bytes 1966088 | tf_op jit(solution)/shard_map/ppermute | solution.py:441
  24.0 0.0 collective-permute-done.2.ahead_ref
  24.0 0.0 collective-permute-done.got_ref
  24.0 2.7 %given_match.1 = (f32[256,512]{1,0:T(8,128)S(1)}, bf16[256,768]{1,0:T(8,128)(2,1)S(1)}, f32[512,128]{1,0:T(8,128)S(1)}, f32[512,128]{1,0:T(8,128)S(1)}) custom-call(s32[1,1]{1,0:T(1,128)S(6)} %copy.20.offset_ref, bf16[576,256]{1,0:T(8,128)(2,1)S(1)} %collective-permute-done.got_ref, bf16[32,512]{1,0:T(8,128)(2,1)S(1)} %collective-permute-done.2.ahead_ref, ...), custom_call_target="tpu_custom_call" | custom-call | flops 1048576 | bytes 1024 | tf_op jit(solution)/shard_map/given_match/pallas_call | solution.py:529
  26.7 0.3 collective-permute-start.4
  27.0 0.0 collective-permute-done.1.rest_ref
  27.0 2.6 %kept_match.1 = (f32[256,512]{1,0:T(8,128)S(1)}, bf16[256,768]{1,0:T(8,128)(2,1)S(1)}) custom-call(s32[1,1]{1,0:T(1,128)S(6)} %copy.20.offset_ref, bf16[576,256]{1,0:T(8,128)(2,1)S(1)} %collective-permute-done.got_ref, bf16[480,256]{1,0:T(8,128)(2,1)S(1)} %collective-permute-done.1.rest_ref, f32[1024,256]{1,0:T(8,128)S(1)} %get-tuple-element.46.edge_ref, ...), custom_call_target="tpu_custom_call" | custom-call | flops 20937965568 | bytes 67108864 | tf_op jit(solution)/shard_map/kept_match/pallas_call | solution.py:538
  29.6 0.0 collective-permute-done.3.got_ref
  29.6 0.0 collective-permute-done.4.got2_ref
  29.6 0.3 pair_sum.1
  29.9 2.8 %collective-permute-start.5 = (bf16[64,2048]{1,0:T(8,128)(2,1)S(1)}, bf16[64,2048]{1,0:T(8,128)(2,1)S(1)}, u32[]{:S(2)}, u32[]{:S(2)}) collective-permute-start(bf16[64,2048]{1,0:T(8,128)(2,1)S(1)} %get-tuple-element.64), channel_id=1, source_target_pairs={{0,128},{32,160},{64,192},{96,224},{128,0},{160,32},{192,64},{224,... | collective-permute-start | bytes 786440 | tf_op jit(solution)/shard_map/ppermute | solution.py:433
  32.7 0.3 collective-permute-start.6
  33.0 2.4 %collective-permute-start.7 = (bf16[64,2048]{1,0:T(8,128)(2,1)S(1)}, bf16[64,2048]{1,0:T(8,128)(2,1)S(1)}, u32[]{:S(2)}, u32[]{:S(2)}) collective-permute-start(bf16[64,2048]{1,0:T(8,128)(2,1)S(1)} %get-tuple-element.66), channel_id=1, source_target_pairs={{0,192},{32,224},{64,0},{96,32},{128,64},{160,96},{192,128},{224,1... | collective-permute-start | bytes 786440 | tf_op jit(solution)/shard_map/ppermute | solution.py:433
  35.4 3.1 %collective-permute-done.5.one_ref = bf16[64,2048]{1,0:T(8,128)(2,1)S(1)} collective-permute-done((bf16[64,2048]{1,0:T(8,128)(2,1)S(1)}, bf16[64,2048]{1,0:T(8,128)(2,1)S(1)}, u32[]{:S(2)}, u32[]{:S(2)}) %collective-permute-start.5) | collective-permute-done | bytes 262176 | tf_op jit(solution)/shard_map/ppermute | solution.py:433
  38.5 6.8 %collective-permute-done.6.two_ref = bf16[64,2048]{1,0:T(8,128)(2,1)S(1)} collective-permute-done((bf16[64,2048]{1,0:T(8,128)(2,1)S(1)}, bf16[64,2048]{1,0:T(8,128)(2,1)S(1)}, u32[]{:S(2)}, u32[]{:S(2)}) %collective-permute-start.6) | collective-permute-done | bytes 262176 | tf_op jit(solution)/shard_map/ppermute | solution.py:433
  45.3 0.0 collective-permute-done.7.three_ref
  45.3 0.1 coadd.1.refs_3_
  45.5 1.1 %collective-permute-start.13 = (bf16[64,1024]{1,0:T(8,128)(2,1)S(1)}, bf16[64,1024]{1,0:T(8,128)(2,1)S(1)}, u32[]{:S(2)}, u32[]{:S(2)}) collective-permute-start(bf16[64,1024]{1,0:T(8,128)(2,1)S(1)} %coadd.1.refs_3_), channel_id=1, source_target_pairs={{0,128},{32,160},{64,192},{96,224},{128,0},{160,32},{192,64},{224,... | collective-permute-start | bytes 393224 | tf_op jit(solution)/shard_map/ppermute | solution.py:433
  46.5 2.1 %collective-permute-start.9 = (bf16[64,1024]{1,0:T(8,128)(2,1)S(1)}, bf16[64,1024]{1,0:T(8,128)(2,1)S(1)}, u32[]{:S(2)}, u32[]{:S(2)}) collective-permute-start(bf16[64,1024]{1,0:T(8,128)(2,1)S(1)} %coadd.1.refs_3_), channel_id=1, source_target_pairs={{0,64},{32,96},{64,128},{96,160},{128,192},{160,224},{192,0},{224,... | collective-permute-start | bytes 393224 | tf_op jit(solution)/shard_map/ppermute | solution.py:433
  48.6 0.6 %collective-permute-start.11 = (bf16[64,1024]{1,0:T(8,128)(2,1)S(1)}, bf16[64,1024]{1,0:T(8,128)(2,1)S(1)}, u32[]{:S(2)}, u32[]{:S(2)}) collective-permute-start(bf16[64,1024]{1,0:T(8,128)(2,1)S(1)} %coadd.1.refs_3_), channel_id=1, source_target_pairs={{0,192},{32,224},{64,0},{96,32},{128,64},{160,96},{192,128},{224,1... | collective-permute-start | bytes 393224 | tf_op jit(solution)/shard_map/ppermute | solution.py:433
  49.2 2.2 %collective-permute-start.8 = (bf16[64,1024]{1,0:T(8,128)(2,1)S(1)}, bf16[64,1024]{1,0:T(8,128)(2,1)S(1)}, u32[]{:S(2)}, u32[]{:S(2)}) collective-permute-start(bf16[64,1024]{1,0:T(8,128)(2,1)S(1)} %coadd.1.refs_3_), channel_id=1, source_target_pairs={{0,32},{32,0},{64,96},{96,64},{128,160},{160,128},{192,224},{224,1... | collective-permute-start | bytes 393224 | tf_op jit(solution)/shard_map/ppermute | solution.py:441
  51.4 0.8 %difference_near.1 = (f32[512,1024]{1,0:T(8,128)}, f32[512,1024]{1,0:T(8,128)}) custom-call(f32[512,512]{1,0:T(8,128)S(1)} %get-tuple-element.50.refs_0_, f32[256,512]{1,0:T(8,128)S(1)} %get-tuple-element.57.refs_1_, f32[256,512]{1,0:T(8,128)S(1)} %get-tuple-element.58.refs_2_, bf16[64,1024]{1,0:T(8,128)(2,1)S(1)} %coadd.1.refs_3_), custom_call_target="tpu_custom_call" | custom-call | flops 65536 | bytes 1048576 | tf_op jit(solution)/shard_map/difference_near/pallas_call | solution.py:399
  52.3 0.0 collective-permute-done.13.refs_5_
  52.3 1.7 %collective-permute-start.14 = (bf16[64,1024]{1,0:T(8,128)(2,1)S(1)}, bf16[64,1024]{1,0:T(8,128)(2,1)S(1)}, u32[]{:S(2)}, u32[]{:S(2)}) collective-permute-start(bf16[64,1024]{1,0:T(8,128)(2,1)S(1)} %collective-permute-done.13.refs_5_), channel_id=1, source_target_pairs={{0,32},{32,0},{64,96},{96,64},{128,160},{160,128},{192,224},{224,1... | collective-permute-start | bytes 393224 | tf_op jit(solution)/shard_map/ppermute | solution.py:441
  54.0 0.8 %collective-permute-done.9.refs_3_ = bf16[64,1024]{1,0:T(8,128)(2,1)S(1)} collective-permute-done((bf16[64,1024]{1,0:T(8,128)(2,1)S(1)}, bf16[64,1024]{1,0:T(8,128)(2,1)S(1)}, u32[]{:S(2)}, u32[]{:S(2)}) %collective-permute-start.9) | collective-permute-done | bytes 131104 | tf_op jit(solution)/shard_map/ppermute | solution.py:433
  54.8 1.0 %collective-permute-start.10 = (bf16[64,1024]{1,0:T(8,128)(2,1)S(1)}, bf16[64,1024]{1,0:T(8,128)(2,1)S(1)}, u32[]{:S(2)}, u32[]{:S(2)}) collective-permute-start(bf16[64,1024]{1,0:T(8,128)(2,1)S(1)} %collective-permute-done.9.refs_3_), channel_id=1, source_target_pairs={{0,32},{32,0},{64,96},{96,64},{128,160},{160,128},{192,224},{224,1... | collective-permute-start | bytes 393224 | tf_op jit(solution)/shard_map/ppermute | solution.py:441
  55.8 0.0 collective-permute-done.11.refs_4_
  55.8 0.1 collective-permute-start.12
  55.8 1.2 %difference_own.1 = (f32[512,1024]{1,0:T(8,128)}, f32[512,1024]{1,0:T(8,128)}) custom-call(f32[512,512]{1,0:T(8,128)S(1)} %get-tuple-element.50.refs_0_, f32[256,512]{1,0:T(8,128)S(1)} %get-tuple-element.57.refs_1_, f32[256,512]{1,0:T(8,128)S(1)} %get-tuple-element.58.refs_2_, ...), custom_call_target="tpu_custom_call", output_to_operand_aliasing={{0}: (6, {}), {1}: (7, {})} | custom-call | flops 196608 | bytes 67108864 | tf_op jit(solution)/shard_map/difference_own/pallas_call | solution.py:399
  57.1 0.0 collective-permute-done.8.refs_3_
  57.1 0.0 collective-permute-done.14.refs_6_
  57.1 0.0 collective-permute-done.10.refs_4_
  57.1 0.0 collective-permute-done.12.refs_5_
  57.1 1.4 %difference_other.1 = (f32[512,1024]{1,0:T(8,128)}, f32[512,1024]{1,0:T(8,128)}) custom-call(f32[512,512]{1,0:T(8,128)S(1)} %get-tuple-element.50.refs_0_, f32[256,512]{1,0:T(8,128)S(1)} %get-tuple-element.57.refs_1_, f32[256,512]{1,0:T(8,128)S(1)} %get-tuple-element.58.refs_2_, ...), custom_call_target="tpu_custom_call", output_to_operand_aliasing={{0}: (7, {}), {1}: (8, {})} | custom-call | flops 262144 | bytes 3145728 | tf_op jit(solution)/shard_map/difference_other/pallas_call | solution.py:399
Async XLA Ops:
  1.3 8.6 %copy-start.1 = (f32[16,128]{1,0:T(8,128)S(1)}, f32[16,128]{1,0:T(8,128)}, u32[]{:S(2)}) copy-start(f32[16,128]{1,0:T(8,128)} %constant.5.clone.factors_ref) | copy-start | bytes 24580
  1.3 8.6 %copy-start.2 = (f32[1,31]{1,0:T(1,128)S(1)}, f32[1,31]{1,0:T(1,128)}, u32[]{:S(2)}) copy-start(f32[1,31]{1,0:T(1,128)} %coef_ref.1) | copy-start | bytes 376
  5.7 18.3 %collective-permute-start = (bf16[576,256]{1,0:T(8,128)(2,1)S(1)}, bf16[576,256]{1,0:T(8,128)(2,1)S(1)}, u32[]{:S(2)}, u32[]{:S(2)}) collective-permute-start(bf16[576,256]{1,0:T(8,128)(2,1)S(1)} %get-tuple-element.51), channel_id=1, source_target_pairs={{0,1},{1,2},{2,3},{3,4},{4,5},{5,6},{6,7},{7,8},{8,9},{9,10},{10,1... | collective-permute-start | bytes 884744 | tf_op jit(solution)/shard_map/ppermute | solution.py:433
  8.2 18.8 %collective-permute-start.1 = (bf16[480,256]{1,0:T(8,128)(2,1)S(1)}, bf16[480,256]{1,0:T(8,128)(2,1)S(1)}, u32[]{:S(2)}, u32[]{:S(2)}) collective-permute-start(bf16[480,256]{1,0:T(8,128)(2,1)S(1)} %get-tuple-element.52), channel_id=1, source_target_pairs={{0,1},{1,2},{2,3},{3,4},{4,5},{5,6},{6,7},{7,8},{8,9},{9,10},{10,1... | collective-permute-start | bytes 737288 | tf_op jit(solution)/shard_map/ppermute | solution.py:433
  9.9 9.5 %copy-start = (bf16[128,1920]{1,0:T(8,128)(2,1)S(1)}, bf16[128,1920]{1,0:T(8,128)(2,1)}, u32[]{:S(2)}) copy-start(bf16[128,1920]{1,0:T(8,128)(2,1)} %constant.4.clone.band_ref) | copy-start | bytes 1474564
  14.4 9.5 %collective-permute-start.2 = (bf16[32,512]{1,0:T(8,128)(2,1)S(1)}, bf16[32,512]{1,0:T(8,128)(2,1)S(1)}, u32[]{:S(2)}, u32[]{:S(2)}) collective-permute-start(bf16[32,512]{1,0:T(8,128)(2,1)S(1)} %get-tuple-element.53), channel_id=1, source_target_pairs={{0,31},{1,0},{2,1},{3,2},{4,3},{5,4},{6,5},{7,6},{8,7},{9,8},{10,9... | collective-permute-start | bytes 98312 | tf_op jit(solution)/shard_map/ppermute | solution.py:433
  22.9 6.7 %collective-permute-start.3 = (bf16[256,1280]{1,0:T(8,128)(2,1)S(1)}, bf16[256,1280]{1,0:T(8,128)(2,1)S(1)}, u32[]{:S(2)}, u32[]{:S(2)}) collective-permute-start(bf16[256,1280]{1,0:T(8,128)(2,1)S(1)} %get-tuple-element.60), channel_id=1, source_target_pairs={{0,32},{32,0},{64,96},{96,64},{128,160},{160,128},{192,224},{224,1... | collective-permute-start | bytes 1966088 | tf_op jit(solution)/shard_map/ppermute | solution.py:441
  26.7 2.9 %collective-permute-start.4 = (bf16[256,768]{1,0:T(8,128)(2,1)S(1)}, bf16[256,768]{1,0:T(8,128)(2,1)S(1)}, u32[]{:S(2)}, u32[]{:S(2)}) collective-permute-start(bf16[256,768]{1,0:T(8,128)(2,1)S(1)} %get-tuple-element.62), channel_id=1, source_target_pairs={{0,32},{32,0},{64,96},{96,64},{128,160},{160,128},{192,224},{224,1... | collective-permute-start | bytes 1179656 | tf_op jit(solution)/shard_map/ppermute | solution.py:441
  29.9 8.6 %collective-permute-start.5 = (bf16[64,2048]{1,0:T(8,128)(2,1)S(1)}, bf16[64,2048]{1,0:T(8,128)(2,1)S(1)}, u32[]{:S(2)}, u32[]{:S(2)}) collective-permute-start(bf16[64,2048]{1,0:T(8,128)(2,1)S(1)} %get-tuple-element.64), channel_id=1, source_target_pairs={{0,128},{32,160},{64,192},{96,224},{128,0},{160,32},{192,64},{224,... | collective-permute-start | bytes 786440 | tf_op jit(solution)/shard_map/ppermute | solution.py:433
  32.7 12.6 %collective-permute-start.6 = (bf16[64,2048]{1,0:T(8,128)(2,1)S(1)}, bf16[64,2048]{1,0:T(8,128)(2,1)S(1)}, u32[]{:S(2)}, u32[]{:S(2)}) collective-permute-start(bf16[64,2048]{1,0:T(8,128)(2,1)S(1)} %get-tuple-element.65), channel_id=1, source_target_pairs={{0,64},{32,96},{64,128},{96,160},{128,192},{160,224},{192,0},{224,... | collective-permute-start | bytes 786440 | tf_op jit(solution)/shard_map/ppermute | solution.py:433
  33.0 12.3 %collective-permute-start.7 = (bf16[64,2048]{1,0:T(8,128)(2,1)S(1)}, bf16[64,2048]{1,0:T(8,128)(2,1)S(1)}, u32[]{:S(2)}, u32[]{:S(2)}) collective-permute-start(bf16[64,2048]{1,0:T(8,128)(2,1)S(1)} %get-tuple-element.66), channel_id=1, source_target_pairs={{0,192},{32,224},{64,0},{96,32},{128,64},{160,96},{192,128},{224,1... | collective-permute-start | bytes 786440 | tf_op jit(solution)/shard_map/ppermute | solution.py:433
  45.5 6.8 %collective-permute-start.13 = (bf16[64,1024]{1,0:T(8,128)(2,1)S(1)}, bf16[64,1024]{1,0:T(8,128)(2,1)S(1)}, u32[]{:S(2)}, u32[]{:S(2)}) collective-permute-start(bf16[64,1024]{1,0:T(8,128)(2,1)S(1)} %coadd.1.refs_3_), channel_id=1, source_target_pairs={{0,128},{32,160},{64,192},{96,224},{128,0},{160,32},{192,64},{224,... | collective-permute-start | bytes 393224 | tf_op jit(solution)/shard_map/ppermute | solution.py:433
  46.5 8.2 %collective-permute-start.9 = (bf16[64,1024]{1,0:T(8,128)(2,1)S(1)}, bf16[64,1024]{1,0:T(8,128)(2,1)S(1)}, u32[]{:S(2)}, u32[]{:S(2)}) collective-permute-start(bf16[64,1024]{1,0:T(8,128)(2,1)S(1)} %coadd.1.refs_3_), channel_id=1, source_target_pairs={{0,64},{32,96},{64,128},{96,160},{128,192},{160,224},{192,0},{224,... | collective-permute-start | bytes 393224 | tf_op jit(solution)/shard_map/ppermute | solution.py:433
  48.6 7.2 %collective-permute-start.11 = (bf16[64,1024]{1,0:T(8,128)(2,1)S(1)}, bf16[64,1024]{1,0:T(8,128)(2,1)S(1)}, u32[]{:S(2)}, u32[]{:S(2)}) collective-permute-start(bf16[64,1024]{1,0:T(8,128)(2,1)S(1)} %coadd.1.refs_3_), channel_id=1, source_target_pairs={{0,192},{32,224},{64,0},{96,32},{128,64},{160,96},{192,128},{224,1... | collective-permute-start | bytes 393224 | tf_op jit(solution)/shard_map/ppermute | solution.py:433
  49.2 7.9 %collective-permute-start.8 = (bf16[64,1024]{1,0:T(8,128)(2,1)S(1)}, bf16[64,1024]{1,0:T(8,128)(2,1)S(1)}, u32[]{:S(2)}, u32[]{:S(2)}) collective-permute-start(bf16[64,1024]{1,0:T(8,128)(2,1)S(1)} %coadd.1.refs_3_), channel_id=1, source_target_pairs={{0,32},{32,0},{64,96},{96,64},{128,160},{160,128},{192,224},{224,1... | collective-permute-start | bytes 393224 | tf_op jit(solution)/shard_map/ppermute | solution.py:441
  52.3 4.8 %collective-permute-start.14 = (bf16[64,1024]{1,0:T(8,128)(2,1)S(1)}, bf16[64,1024]{1,0:T(8,128)(2,1)S(1)}, u32[]{:S(2)}, u32[]{:S(2)}) collective-permute-start(bf16[64,1024]{1,0:T(8,128)(2,1)S(1)} %collective-permute-done.13.refs_5_), channel_id=1, source_target_pairs={{0,32},{32,0},{64,96},{96,64},{128,160},{160,128},{192,224},{224,1... | collective-permute-start | bytes 393224 | tf_op jit(solution)/shard_map/ppermute | solution.py:441
  54.8 2.3 %collective-permute-start.10 = (bf16[64,1024]{1,0:T(8,128)(2,1)S(1)}, bf16[64,1024]{1,0:T(8,128)(2,1)S(1)}, u32[]{:S(2)}, u32[]{:S(2)}) collective-permute-start(bf16[64,1024]{1,0:T(8,128)(2,1)S(1)} %collective-permute-done.9.refs_3_), channel_id=1, source_target_pairs={{0,32},{32,0},{64,96},{96,64},{128,160},{160,128},{192,224},{224,1... | collective-permute-start | bytes 393224 | tf_op jit(solution)/shard_map/ppermute | solution.py:441
  55.8 1.3 %collective-permute-start.12 = (bf16[64,1024]{1,0:T(8,128)(2,1)S(1)}, bf16[64,1024]{1,0:T(8,128)(2,1)S(1)}, u32[]{:S(2)}, u32[]{:S(2)}) collective-permute-start(bf16[64,1024]{1,0:T(8,128)(2,1)S(1)} %collective-permute-done.11.refs_4_), channel_id=1, source_target_pairs={{0,32},{32,0},{64,96},{96,64},{128,160},{160,128},{192,224},{224,1... | collective-permute-start | bytes 393224 | tf_op jit(solution)/shard_map/ppermute | solution.py:441
